TPU v7x, 32 devices: a whole 2x2x4 slice. The times are simulated.
32 devices in a mesh: shard: 2 (over core), rep: 16 (over z, y, x).
Axes of the slice: x: 2, y: 2, z: 4, core: 2. Of those that a mesh axis runs over, the one named last changes fastest.
Arguments:
- tokens: bfloat16 [128, 512, 768], P(('shard', 'rep')), may hold values from -6 to 6
- teacher: bfloat16 [128, 512, 768], P(('shard', 'rep')), may hold values from -6 to 6
- block_ids: int32 [128, 512], P(('shard', 'rep')), may hold values from 0 to 3, never falling along the last dimension, each value on 1 to 256 neighbouring positions
- qkv_weight: bfloat16 [768, 2304], P('shard'), may hold values from -0.21875 to 0.21875
- out_weight: bfloat16 [768, 768], P('shard'), may hold values from -0.875 to 0.875
- up_weight: bfloat16 [768, 3072], P('shard'), may hold values from -0.21875 to 0.21875
- down_weight: bfloat16 [3072, 768], P('shard'), may hold values from -0.109375 to 0.109375
- biases: bfloat16 [768, 4], P('shard'), may hold values from -1.5 to 1.5
- hidden_bias: bfloat16 [3072], P('shard'), may hold values from -1.5 to 1.5
- norm_gain: bfloat16 [768, 2], P('shard'), may hold values from 0.25 to 1.75
- norm_shift: bfloat16 [768, 2], P('shard'), may hold values from -1.5 to 1.5
Outputs:
- layer_out: bfloat16 [128, 512, 768], P(('shard', 'rep'))
- token_grad: float32 [128, 512, 768], P(('shard', 'rep'))
- qkv_grad: float32 [768, 2304], P('shard')
- out_grad: float32 [768, 768], P('shard')
- up_grad: float32 [768, 3072], P('shard')
- down_grad: float32 [3072, 768], P('shard')
- bias_grad: float32 [768, 4], P('shard')
- hidden_grad: float32 [3072], P('shard')
- gain_grad: float32 [768, 2], P('shard')
- shift_grad: float32 [768, 2], P('shard')
Inputs may be any that keep to these rules, and one draw needn't show every extreme that they name: `block_ids`: along each sequence the block ids never fall; each block has 1 to 256 tokens and some block has exactly 256.
All inputs are finite; a program needn't handle non-finite values.
Results may differ from a plain program's by a relative error of at most 0.01.
Values may be sent and summed in bfloat16 or wider, within the bound.
A program may use at most 384 MiB of HBM per device.

v0:
```python
import jax
import jax.numpy as jnp
from jax import lax
from jax.sharding import PartitionSpec as P

HEAD_DIM = 64


EPS = 1e-05


def as_sent(value):
    return jax.tree.map(lambda a: a.astype(jnp.bfloat16) if a.dtype == jnp.float32 else a, value)


def binarize(latent):
    matrix = latent.astype(jnp.float32)
    scales = jnp.mean(jnp.abs(matrix), axis=0)
    signed = jnp.where(matrix >= 0, 1.0, -1.0).astype(jnp.float32)
    return (scales * signed).astype(jnp.bfloat16)


def prepare(gathered):
    qkv_latent, out_latent, up_latent, down_latent, bias_all, hidden_all, gain_all, shift_all = (
        gathered
    )
    return (
        binarize(qkv_latent),
        binarize(out_latent),
        binarize(up_latent),
        binarize(down_latent),
        bias_all.astype(jnp.float32),
        hidden_all.astype(jnp.float32),
        gain_all.astype(jnp.float32),
        shift_all.astype(jnp.float32),
    )


def layer_norm(resid, gain, shift):
    center = resid - jnp.mean(resid, axis=-1, keepdims=True)
    inverse = lax.rsqrt(jnp.mean(center * center, axis=-1, keepdims=True) + EPS)
    normed = center * inverse
    return (normed * gain + shift, normed, inverse)


def norm_back(upstream, normed, inverse, gain):
    scaled = upstream * gain
    centered = (
        scaled
        - jnp.mean(scaled, axis=-1, keepdims=True)
        - normed * jnp.mean(scaled * normed, axis=-1, keepdims=True)
    )
    return (centered * inverse, jnp.sum(upstream * normed, axis=0), jnp.sum(upstream, axis=0))


def gelu_slope(pre_act):
    return (
        0.5 * (1.0 + lax.erf(pre_act * 0.7071067811865476))
        + pre_act * jnp.exp(-0.5 * pre_act * pre_act) * 0.3989422804014327
    )


def masked_scores(query_part, key_low, block_part, blocks):
    scores = jnp.einsum(
        "qhd,khd->hqk", query_part, key_low, preferred_element_type=jnp.float32
    ) * HEAD_DIM ** (-0.5)
    allowed = block_part[:, None] >= blocks[None, :]
    return jnp.where(allowed[None], scores, -1e30)


def forward(tokens_now, blocks, weights):
    qkv_bin, out_bin, up_bin, down_bin, bias_all, hidden_all, gains, shifts = weights
    length, width = tokens_now.shape
    heads = width // HEAD_DIM
    rows = min(512, length)
    joined = jnp.dot(tokens_now, qkv_bin, preferred_element_type=jnp.float32)
    query_low = (
        (joined[:, :width] + bias_all[:, 0]).astype(jnp.bfloat16).reshape(length, heads, HEAD_DIM)
    )
    key_low = joined[:, width : 2 * width].astype(jnp.bfloat16).reshape(length, heads, HEAD_DIM)
    value_low = (
        (joined[:, 2 * width :] + bias_all[:, 1])
        .astype(jnp.bfloat16)
        .reshape(length, heads, HEAD_DIM)
    )
    query_blocks = query_low.reshape(length // rows, rows, heads, HEAD_DIM)
    block_rows = blocks.reshape(length // rows, rows)

    def attend(item):
        query_part, block_part = item
        scores = masked_scores(query_part, key_low, block_part, blocks)
        peak = jnp.max(scores, axis=-1, keepdims=True)
        shifted = jnp.exp(scores - peak)
        total = jnp.sum(shifted, axis=-1, keepdims=True)
        probs = (shifted / total).astype(jnp.bfloat16)
        context = jnp.einsum("hqk,khd->qhd", probs, value_low, preferred_element_type=jnp.float32)
        return (context.astype(jnp.bfloat16), peak + jnp.log(total))

    context_low, log_total = lax.map(attend, (query_blocks, block_rows))
    context_low = context_low.reshape(length, width)
    attended = jnp.dot(context_low, out_bin, preferred_element_type=jnp.float32) + bias_all[:, 2]
    first, first_normed, first_inverse = layer_norm(
        tokens_now.astype(jnp.float32) + attended, gains[:, 0], shifts[:, 0]
    )
    first_low = first.astype(jnp.bfloat16)
    pre_act = jnp.dot(first_low, up_bin, preferred_element_type=jnp.float32) + hidden_all
    hidden_low = jax.nn.gelu(pre_act, approximate=False).astype(jnp.bfloat16)
    mixed = jnp.dot(hidden_low, down_bin, preferred_element_type=jnp.float32) + bias_all[:, 3]
    final, final_normed, final_inverse = layer_norm(first + mixed, gains[:, 1], shifts[:, 1])
    saved = (
        query_blocks,
        key_low,
        value_low,
        block_rows,
        log_total,
        context_low,
        first_normed,
        first_inverse,
        first_low,
        pre_act,
        hidden_low,
        final_normed,
        final_inverse,
    )
    return (final, saved)


def backward(tokens_now, blocks, final, target, saved, weights):
    (
        query_blocks,
        key_low,
        value_low,
        block_rows,
        log_total,
        context_low,
        first_normed,
        first_inverse,
        first_low,
        pre_act,
        hidden_low,
        final_normed,
        final_inverse,
    ) = saved
    qkv_bin, out_bin, up_bin, down_bin, bias_all, hidden_all, gains, shifts = weights
    length, width = tokens_now.shape
    heads = width // HEAD_DIM
    upstream = final - target.astype(jnp.float32)
    second_back, gain_two, shift_two = norm_back(upstream, final_normed, final_inverse, gains[:, 1])
    mixed_low = second_back.astype(jnp.bfloat16)
    down_grad = jnp.einsum("lf,ld->fd", hidden_low, mixed_low, preferred_element_type=jnp.float32)
    hidden_back = jnp.einsum("ld,fd->lf", mixed_low, down_bin, preferred_element_type=jnp.float32)
    pre_back = hidden_back * gelu_slope(pre_act)
    hidden_grad = jnp.sum(pre_back, axis=0)
    pre_low = pre_back.astype(jnp.bfloat16)
    up_grad = jnp.einsum("ld,lf->df", first_low, pre_low, preferred_element_type=jnp.float32)
    first_back = second_back + jnp.einsum(
        "lf,df->ld", pre_low, up_bin, preferred_element_type=jnp.float32
    )
    resid_back, gain_one, shift_one = norm_back(
        first_back, first_normed, first_inverse, gains[:, 0]
    )
    attended_low = resid_back.astype(jnp.bfloat16)
    out_grad = jnp.einsum(
        "le,ld->ed", context_low, attended_low, preferred_element_type=jnp.float32
    )
    context_back = jnp.einsum(
        "ld,ed->le", attended_low, out_bin, preferred_element_type=jnp.float32
    ).astype(jnp.bfloat16)
    context_blocks = context_back.reshape(query_blocks.shape)
    factor = HEAD_DIM ** (-0.5)

    def attend_back(carry, item):
        key_sum, value_sum = carry
        query_part, block_part, log_part, context_part = item
        scores = masked_scores(query_part, key_low, block_part, blocks)
        probs = jnp.exp(scores - log_part)
        prob_back = jnp.einsum(
            "qhd,khd->hqk", context_part, value_low, preferred_element_type=jnp.float32
        )
        row_dot = jnp.sum(prob_back * probs, axis=-1, keepdims=True)
        score_low = (probs * (prob_back - row_dot)).astype(jnp.bfloat16)
        query_back = (
            jnp.einsum("hqk,khd->qhd", score_low, key_low, preferred_element_type=jnp.float32)
            * factor
        )
        key_sum = (
            key_sum
            + jnp.einsum("hqk,qhd->khd", score_low, query_part, preferred_element_type=jnp.float32)
            * factor
        )
        value_sum = value_sum + jnp.einsum(
            "hqk,qhd->khd",
            probs.astype(jnp.bfloat16),
            context_part,
            preferred_element_type=jnp.float32,
        )
        return ((key_sum, value_sum), query_back)

    zeros = jnp.zeros((length, heads, HEAD_DIM), jnp.float32)
    (key_back, value_back), query_back = lax.scan(
        attend_back, (zeros, zeros), (query_blocks, block_rows, log_total, context_blocks)
    )
    query_back = query_back.reshape(length, width)
    key_back = key_back.reshape(length, width)
    value_back = value_back.reshape(length, width)
    joined_low = jnp.concatenate([query_back, key_back, value_back], axis=1).astype(jnp.bfloat16)
    qkv_grad = jnp.einsum("ld,le->de", tokens_now, joined_low, preferred_element_type=jnp.float32)
    token_grad = resid_back + jnp.einsum(
        "le,de->ld", joined_low, qkv_bin, preferred_element_type=jnp.float32
    )
    bias_grad = jnp.stack(
        [
            jnp.sum(query_back, axis=0),
            jnp.sum(value_back, axis=0),
            jnp.sum(resid_back, axis=0),
            jnp.sum(second_back, axis=0),
        ],
        axis=1,
    )
    gain_grad = jnp.stack([gain_one, gain_two], axis=1)
    shift_grad = jnp.stack([shift_one, shift_two], axis=1)
    return (
        token_grad,
        (qkv_grad, out_grad, up_grad, down_grad, bias_grad, hidden_grad, gain_grad, shift_grad),
    )


def body(
    tokens,
    teacher,
    block_ids,
    qkv_weight,
    out_weight,
    up_weight,
    down_weight,
    biases,
    hidden_bias,
    norm_gain,
    norm_shift,
):
    outputs = []
    token_grads = []
    totals = None
    for micro in range(tokens.shape[0]):
        forward_weights = prepare(
            (
                lax.all_gather(qkv_weight, "shard", axis=0, tiled=True),
                lax.all_gather(out_weight, "shard", axis=0, tiled=True),
                lax.all_gather(up_weight, "shard", axis=0, tiled=True),
                lax.all_gather(down_weight, "shard", axis=0, tiled=True),
                lax.all_gather(biases, "shard", axis=0, tiled=True),
                lax.all_gather(hidden_bias, "shard", axis=0, tiled=True),
                lax.all_gather(norm_gain, "shard", axis=0, tiled=True),
                lax.all_gather(norm_shift, "shard", axis=0, tiled=True),
            )
        )
        final, saved = forward(tokens[micro], block_ids[micro], forward_weights)
        outputs.append(final.astype(jnp.bfloat16))
        backward_weights = prepare(
            (
                lax.all_gather(qkv_weight, "shard", axis=0, tiled=True),
                lax.all_gather(out_weight, "shard", axis=0, tiled=True),
                lax.all_gather(up_weight, "shard", axis=0, tiled=True),
                lax.all_gather(down_weight, "shard", axis=0, tiled=True),
                lax.all_gather(biases, "shard", axis=0, tiled=True),
                lax.all_gather(hidden_bias, "shard", axis=0, tiled=True),
                lax.all_gather(norm_gain, "shard", axis=0, tiled=True),
                lax.all_gather(norm_shift, "shard", axis=0, tiled=True),
            )
        )
        token_grad, grads = backward(
            tokens[micro], block_ids[micro], final, teacher[micro], saved, backward_weights
        )
        token_grads.append(token_grad)
        if totals is None:
            totals = grads
        else:
            totals = tuple((earlier + later for earlier, later in zip(totals, grads)))
    owned = jax.tree.map(
        lambda part: part.astype(jnp.float32),
        lax.psum_scatter(as_sent(totals), "shard", scatter_dimension=0, tiled=True),
    )
    summed = jax.tree.map(lambda part: part.astype(jnp.float32), lax.psum(as_sent(owned), "rep"))
    return (
        jnp.stack(outputs),
        jnp.stack(token_grads),
        summed[0],
        summed[1],
        summed[2],
        summed[3],
        summed[4],
        summed[5],
        summed[6],
        summed[7],
    )


def solution(mesh):
    placed = (
        P(("shard", "rep"), None, None),
        P(("shard", "rep"), None, None),
        P(("shard", "rep"), None),
        P("shard", None),
        P("shard", None),
        P("shard", None),
        P("shard", None),
        P("shard", None),
        P("shard"),
        P("shard", None),
        P("shard", None),
    )
    return jax.shard_map(
        body,
        mesh=mesh,
        in_specs=placed,
        out_specs=(
            P(("shard", "rep"), None, None),
            P(("shard", "rep"), None, None),
            P("shard", None),
            P("shard", None),
            P("shard", None),
            P("shard", None),
            P("shard", None),
            P("shard"),
            P("shard", None),
            P("shard", None),
        ),
        check_vma=False,
    )
```

profile of v0, /device:TPU:0, one launch (start us, length us, event | category | flops | bytes accessed | tf_op | source)
XLA Modules:
  0.0 833.3 jit_solution(7230255110996487131)
XLA Ops:
  24.4 12.6 %all-gather.6.cloned.1.call-done = bf16[768,2304]{1,0:T(8,128)(2,1)} async-done(((bf16[384,2304]{1,0:T(8,128)(2,1)}), bf16[768,2304]{1,0:T(8,128)(2,1)}) %all-gather.6.cloned.1.call-update) | async-done | bytes 3538960 | tf_op jit(solution)/shard_map/all_gather | solution.py:247
  39.8 4.4 convolution_bitcast_fusion.3
  51.1 3.1 fusion.93
  56.4 3.8 fusion
  61.0 5.1 fusion.131
  66.1 3.6 fusion.243
  76.3 3.8 fusion.128
  89.3 4.1 fusion.129
  103.6 3.6 fusion.130
  113.9 3.3 fusion.8
  117.2 3.5 fusion.9
  121.3 5.1 fusion.223
  126.4 4.9 fusion.226
  131.4 4.9 fusion.229
  136.4 63.6 %fusion.13 = (bf16[512,3072]{1,0:T(8,128)(2,1)S(1)}, bf16[512,3072]{1,0:T(8,128)(2,1)S(1)}, bf16[512,3072]{1,0:T(8,128)(2,1)S(1)}, bf16[512,3072]{1,0:T(8,128)(2,1)S(1)}, f32[512,3072]{1,0:T(8,128)}) fusion(f32[3072]{0:T(1024)S(1)} %bitcast.293, f32[512,3072]{1,0:T(8,128)} %fusion.229, f32[512,3072]{1,0:T(8,128)} %fusion.226, f32[512,3072]{1,0:T(8,128)} %fusion.223, ...), kind=kOutput, calls=%fused_computation.57 | convolution fusion | flops 2842951680 | bytes 43278336 | tf_op jit(solution)/shard_map/dot_general | solution.py:106
  200.2 2.9 fusion.248
  203.5 2.9 fusion.247
  206.8 2.9 fusion.249
  209.8 2.9 fusion.250
  212.7 3.1 fusion.142
  216.5 4.0 fusion.140
  220.5 3.1 fusion.241
  223.6 8.6 %fusion.254 = (f32[3072]{0:T(1024)}, bf16[512,3072]{1,0:T(8,128)(2,1)S(1)}) fusion(f32[512,3072]{1,0:T(8,128)} %fusion.229, f32[3072]{0:T(1024)S(1)} %bitcast.294, bf16[3072,768]{1,0:T(8,128)(2,1)S(1)} %copy-done.63, f32[768]{0:T(1024)S(1)} %copy-done.209, f32[512,768]{1,0:T(8,128)S(1)} %get-tuple-element.425), kind=kOutput, calls=%fused_computation.492 | convolution fusion | flops 2446980096 | bytes 15756288 | tf_op jit(solution)/shard_map/ld,fd->lf/dot_general | solution.py:151
  234.9 8.1 fusion.253
  243.0 5.4 multiply_reduce_fusion.11
  250.6 8.0 fusion.251
  258.6 8.8 %fusion.252 = (f32[3072]{0:T(1024)}, bf16[512,3072]{1,0:T(8,128)(2,1)S(1)}) fusion(f32[512,3072]{1,0:T(8,128)} %fusion.226, f32[3072]{0:T(1024)S(1)} %bitcast.297, bf16[3072,768]{1,0:T(8,128)(2,1)S(1)} %copy-done.63, f32[768]{0:T(1024)S(1)} %copy-done.209, f32[512,768]{1,0:T(8,128)S(1)} %get-tuple-element.427), kind=kOutput, calls=%fused_computation.490 | convolution fusion | flops 2446980096 | bytes 15756288 | tf_op jit(solution)/shard_map/ld,fd->lf/dot_general | solution.py:151
  267.4 2.7 fusion.122
  270.2 5.7 fusion.240
  281.1 14.1 %multiply_reduce_fusion.3 = (f32[12,512]{1,0:T(8,128)}, f32[12,512,512]{1,2,0:T(8,128)}) fusion(f32[12,512]{1,0:T(8,128)S(1)} %copy-done.133, f32[12,512,512]{1,2,0:T(8,128)} %copy-done.1, pred[512,512]{0,1:T(8,128)(4,1)S(1)} %copy-done.26, bf16[512,12,64]{0,2,1:T(8,128)(2,1)} %bitcast.263, bf16[512,12,64]{0,2,1:T(8,128)(2,1)} %bitcast.262), kind=kOutput, calls=%fused_computation.10 | convolution fusion | flops 418375680 | bytes 27049984 | tf_op jit(solution)/shard_map/while/body/eval_jaxpr/qhd,khd->hqk/dot_general | solution.py:177
  295.2 8.1 bitcast_convert_fusion.6
  308.2 9.3 %multiply_reduce_fusion.2 = (f32[12,512]{1,0:T(8,128)S(1)}, f32[12,512,512]{1,2,0:T(8,128)}) fusion(f32[12,512]{1,0:T(8,128)S(1)} %copy-done.134, f32[12,512,512]{1,2,0:T(8,128)} %copy-done.3, pred[512,512]{0,1:T(8,128)(4,1)S(1)} %copy-done.30, bf16[512,12,64]{0,2,1:T(8,128)(2,1)S(1)} %bitcast.265, bf16[512,12,64]{0,2,1:T(8,128)(2,1)S(1)} %bitcast.260), kind=kOutput, calls=%fused_computation.7 | convolution fusion | flops 418375680 | bytes 27049984 | tf_op jit(solution)/shard_map/while/body/eval_jaxpr/qhd,khd->hqk/dot_general | solution.py:177
  317.5 7.9 bitcast_convert_fusion.4
  328.9 9.8 %multiply_reduce_fusion.1 = (f32[12,512]{1,0:T(8,128)}, f32[12,512,512]{1,2,0:T(8,128)}) fusion(f32[12,512]{1,0:T(8,128)S(1)} %copy-done.132, f32[12,512,512]{1,2,0:T(8,128)} %copy-done.2, pred[512,512]{0,1:T(8,128)(4,1)S(1)} %copy-done.28, bf16[512,12,64]{0,2,1:T(8,128)(2,1)S(1)} %bitcast.267, bf16[512,12,64]{0,2,1:T(8,128)(2,1)S(1)} %bitcast.258), kind=kOutput, calls=%fused_computation.4 | convolution fusion | flops 418375680 | bytes 27049984 | tf_op jit(solution)/shard_map/while/body/eval_jaxpr/qhd,khd->hqk/dot_general | solution.py:177
  338.7 8.3 bitcast_convert_fusion.2
  351.1 10.9 %multiply_reduce_fusion = (f32[12,512]{1,0:T(8,128)}, f32[12,512,512]{1,2,0:T(8,128)}) fusion(f32[12,512]{1,0:T(8,128)S(1)} %copy-done.131, f32[12,512,512]{1,2,0:T(8,128)} %copy-done, pred[512,512]{0,1:T(8,128)(4,1)S(1)} %copy-done.22, bf16[512,12,64]{0,2,1:T(8,128)(2,1)S(1)} %bitcast.269, bf16[512,12,64]{0,2,1:T(8,128)(2,1)S(1)} %bitcast.256), kind=kOutput, calls=%fused_computation.1 | convolution fusion | flops 418375680 | bytes 27049984 | tf_op jit(solution)/shard_map/while/body/eval_jaxpr/qhd,khd->hqk/dot_general | solution.py:177
  362.0 9.5 %bitcast_convert_fusion = (bf16[512,12,64]{0,2,1:T(8,128)(2,1)}, f32[12,512,64]{1,2,0:T(8,128)}) fusion(bf16[512,12,64]{0,2,1:T(8,128)(2,1)} %bitcast.270, f32[12,512]{1,0:T(8,128)S(1)} %copy-done.131, f32[12,512,512]{1,2,0:T(8,128)} %copy-done, pred[512,512]{0,1:T(8,128)(4,1)S(1)} %copy-done.22), kind=kOutput, calls=%fused_computation.204 | convolution fusion | flops 415629312 | bytes 16015360 | tf_op jit(solution)/shard_map/while/body/eval_jaxpr/hqk,qhd->khd/dot_general | solution.py:191
  371.5 10.8 %multiply_convert_fusion.2 = bf16[12,512,512]{1,2,0:T(8,128)(2,1)} fusion(f32[12,512,512]{1,2,0:T(8,128)} %get-tuple-element.502, f32[12,512]{1,0:T(8,128)S(1)} %get-tuple-element.501, f32[12,512]{1,0:T(8,128)S(1)} %copy-done.134, f32[12,512,512]{1,2,0:T(8,128)S(1)} %bitcast.236, pred[512,512]{0,1:T(8,128)(4,1)} %broadcast_compare_fusion.2), kind=kLoop, calls=%fused_computation.6 | loop fusion | flops 18874368 | bytes 31768576 | tf_op jit(solution)/shard_map/while/body/eval_jaxpr/convert_element_type | solution.py:181
  382.3 5.5 bitcast_convert_fusion.5
  387.8 2.9 multiply_convert_fusion.10
  390.8 8.1 multiply_convert_fusion.3
  401.6 2.9 multiply_convert_fusion.11
  404.5 8.0 multiply_convert_fusion.1
  414.8 2.9 multiply_convert_fusion.9
  417.8 7.2 multiply_convert_fusion
  432.3 4.9 fusion.146
  437.3 4.9 fusion.144
  442.1 8.0 fusion.87
  450.2 3.8 copy.104
  460.7 9.1 %fusion.180 = f32[3072,768]{1,0:T(8,128)} fusion(bf16[512,3072]{1,0:T(8,128)(2,1)} %copy-done.87, f32[512,768]{1,0:T(8,128)S(1)} %copy-done.38), kind=kOutput, calls=%fused_computation.374 | convolution fusion | flops 2416312320 | bytes 14155776 | tf_op jit(solution)/shard_map/lf,ld->fd/dot_general | solution.py:150
  469.9 8.3 fusion.186
  478.3 5.2 fusion.174
  483.4 13.1 %add_convert_fusion = bf16[3072,768]{1,0:T(8,128)(2,1)} fusion(f32[3072,768]{1,0:T(8,128)} %fusion.174, f32[3072,768]{1,0:T(8,128)} %fusion.186, f32[3072,768]{1,0:T(8,128)} %fusion.180, bf16[512,3072]{1,0:T(8,128)(2,1)S(1)} %copy-done.83, f32[512,768]{1,0:T(8,128)S(1)} %copy-done.34), kind=kOutput, calls=%fused_computation.46 | convolution fusion | flops 2425749504 | bytes 37748736 | tf_op jit(solution)/shard_map/lf,ld->fd/dot_general | solution.py:150
  497.9 7.4 fusion.112
  505.4 5.6 fusion.104
  511.1 5.6 fusion.108
  516.7 13.4 %add_convert_fusion.1 = bf16[768,3072]{1,0:T(8,128)(2,1)} fusion(f32[768,3072]{1,0:T(8,128)} %fusion.104, f32[768,3072]{1,0:T(8,128)} %fusion.112, f32[768,3072]{1,0:T(8,128)} %fusion.108, bf16[512,3072]{1,0:T(8,128)(2,1)S(1)} %copy-done.93, f32[512,768]{1,0:T(8,128)S(1)} %copy-done.7, f32[512]{0:T(512)S(1)} %copy-done.158, f32[512]{0:T(512)S(1)} %copy-done.149, ...), kind=kOutput, calls=%fused_computation.47 | convolution fusion | flops 2427322368 | bytes 37758976 | tf_op jit(solution)/shard_map/ld,lf->df/dot_general | solution.py:155
  538.7 4.6 copy.105
  549.3 4.4 add_bitcast_fusion.3
  560.4 3.1 pad_maximum_fusion
  567.5 9.8 %reduce-scatter.24.cloned.1.call-done = bf16[384,4]{1,0:T(8,128)(2,1)} async-done(((bf16[768,4]{1,0:T(8,128)(2,1)}), bf16[384,4]{1,0:T(8,128)(2,1)}) %reduce-scatter.24.cloned.1.call-update) | async-done | bytes 3088
  578.3 80.5 %all-reduce.1 = (bf16[384,4]{0,1:T(4,128)(2,1)S(1)}, bf16[1536]{0:T(1024)(128)(2,1)S(1)}, bf16[384,2]{0,1:T(2,128)(2,1)S(1)}, bf16[384,2]{0,1:T(2,128)(2,1)S(1)}) all-reduce(bf16[384,4]{0,1:T(4,128)(2,1)S(1)} %copy.107, bf16[1536]{0:T(1024)(128)(2,1)S(1)} %dynamic-slice.1, ...), channel_id=1, replica_groups=mesh['shard'=2,'rep'=16] {'rep'}, use_global_device_ids=true, to_apply=%region_73.74 | all-reduce | flops 4608 | bytes 18432 | tf_op jit(solution)/shard_map/psum | solution.py:283
  661.2 154.1 %all-reduce.5.cloned.1.call-done = (bf16[384,2304]{0,1:T(8,128)(2,1)}, bf16[384,768]{1,0:T(8,128)(2,1)}, bf16[384,3072]{1,0:T(8,128)(2,1)}, bf16[1536,768]{1,0:T(8,128)(2,1)}) async-done(((bf16[384,2304]{0,1:T(8,128)(2,1)}, bf16[384,768]{1,0:T(8,128)(2,1)}, bf16[384,3072]{1,0:T(8,128)(2,1)}, bf16[1536,768]{1,0:T(8,128)(2,1)}), (bf16[384,2304]{0,1:T(8,128)(2,1)}, bf16[384,768]{1,0:T(8,128)(2,1)}, ...) | async-done | bytes 7077904 | tf_op jit(solution)/shard_map/psum | solution.py:283
  815.3 4.6 convert_element_type.497
  (688 shorter events, 140.0 us)
Async XLA Ops:
  7.2 13.2 %copy-start.202 = (bf16[1536]{0:T(1024)(128)(2,1)S(1)}, bf16[1536]{0:T(1024)(128)(2,1)}, u32[]{:S(2)}) copy-start(bf16[1536]{0:T(1024)(128)(2,1)} %param.19) | copy-start | bytes 9220
  7.2 15.6 %all-gather.8.cloned.1.call-start = ((), (), s32[]{:S(2)}) async-start(), calls=%async_computation.8 | async-start | bytes 1769472 | tf_op jit(solution)/shard_map/all_gather | solution.py:248
  8.0 29.1 %all-gather.6.cloned.1.call-start = ((), (), s32[]{:S(2)}) async-start(), calls=%async_computation.7 | async-start | bytes 5308416 | tf_op jit(solution)/shard_map/all_gather | solution.py:247
  8.7 105.2 %all-gather.10.cloned.1.call-start = ((), (), s32[]{:S(2)}) async-start(), calls=%async_computation.9 | async-start | bytes 7077888 | tf_op jit(solution)/shard_map/all_gather | solution.py:249
  9.4 107.8 %all-gather.12.cloned.1.call-start = ((), (), s32[]{:S(2)}) async-start(), calls=%async_computation.10 | async-start | bytes 7077888 | tf_op jit(solution)/shard_map/all_gather | solution.py:250
  10.0 528.7 %reduce-scatter.22.cloned.1.call-start = ((), (), s32[]{:S(2)}) async-start(), calls=%async_computation.14 | async-start | bytes 5308416
  12.6 67.5 %copy-start.191 = (f32[768]{0:T(1024)}, f32[768]{0:T(1024)S(1)}, u32[]{:S(2)}) copy-start(f32[768]{0:T(1024)S(1)} %get-tuple-element.385) | copy-start | bytes 9220
  16.0 115.4 %copy-start.141 = (f32[768]{0:T(1024)}, f32[768]{0:T(1024)S(1)}, u32[]{:S(2)}) copy-start(f32[768]{0:T(1024)S(1)} %get-tuple-element.388) | copy-start | bytes 9220
  18.3 113.0 %copy-start.144 = (f32[768]{0:T(1024)}, f32[768]{0:T(1024)S(1)}, u32[]{:S(2)}) copy-start(f32[768]{0:T(1024)S(1)} %get-tuple-element.390) | copy-start | bytes 9220
  18.6 55.8 %copy-start.21 = (pred[512,512]{0,1:T(8,128)(4,1)}, pred[512,512]{0,1:T(8,128)(4,1)S(1)}, u32[]{:S(2)}) copy-start(pred[512,512]{0,1:T(8,128)(4,1)S(1)} %broadcast_compare_fusion) | copy-start | bytes 786436
  24.4 41.6 %copy-start.203 = (f32[768]{0:T(1024)}, f32[768]{0:T(1024)S(1)}, u32[]{:S(2)}) copy-start(f32[768]{0:T(1024)S(1)} %broadcast_multiply_fusion.3) | copy-start | bytes 9220
  39.8 9.1 %copy-start.177 = (f32[2304]{0:T(1024)}, f32[2304]{0:T(1024)S(1)}, u32[]{:S(2)}) copy-start(f32[2304]{0:T(1024)S(1)} %broadcast_multiply_fusion.1) | copy-start | bytes 27652
  44.4 9.8 %copy-start.17 = (bf16[512,768]{0,1:T(8,128)(2,1)}, bf16[512,768]{0,1:T(8,128)(2,1)S(1)}, u32[]{:S(2)}) copy-start(bf16[512,768]{0,1:T(8,128)(2,1)S(1)} %slice.287) | copy-start | bytes 2359300
  46.6 23.0 %copy-start.13 = (bf16[512,768]{0,1:T(8,128)(2,1)}, bf16[512,768]{0,1:T(8,128)(2,1)S(1)}, u32[]{:S(2)}) copy-start(bf16[512,768]{0,1:T(8,128)(2,1)S(1)} %slice.284) | copy-start | bytes 2359300
  48.9 33.8 %copy-start.15 = (bf16[512,768]{0,1:T(8,128)(2,1)}, bf16[512,768]{0,1:T(8,128)(2,1)S(1)}, u32[]{:S(2)}) copy-start(bf16[512,768]{0,1:T(8,128)(2,1)S(1)} %slice.285) | copy-start | bytes 2359300
  51.1 45.9 %copy-start.19 = (bf16[512,768]{0,1:T(8,128)(2,1)}, bf16[512,768]{0,1:T(8,128)(2,1)S(1)}, u32[]{:S(2)}) copy-start(bf16[512,768]{0,1:T(8,128)(2,1)S(1)} %slice.286) | copy-start | bytes 2359300
  69.6 43.0 %copy-start.150 = (f32[512]{0:T(512)}, f32[512]{0:T(512)S(1)}, u32[]{:S(2)}) copy-start(f32[512]{0:T(512)S(1)} %broadcast_multiply_fusion.27) | copy-start | bytes 6148
  82.6 38.7 %copy-start.5 = (f32[512,768]{1,0:T(8,128)}, f32[512,768]{1,0:T(8,128)S(1)}, u32[]{:S(2)}) copy-start(f32[512,768]{1,0:T(8,128)S(1)} %get-tuple-element.475) | copy-start | bytes 4718596
  82.6 38.7 %copy-start.147 = (f32[512]{0:T(512)}, f32[512]{0:T(512)S(1)}, u32[]{:S(2)}) copy-start(f32[512]{0:T(512)S(1)} %broadcast_multiply_fusion.21) | copy-start | bytes 6148
  95.9 30.6 %copy-start.153 = (f32[512]{0:T(512)}, f32[512]{0:T(512)S(1)}, u32[]{:S(2)}) copy-start(f32[512]{0:T(512)S(1)} %broadcast_multiply_fusion.23) | copy-start | bytes 6148
  109.6 21.7 %copy-start.46 = (f32[512,768]{1,0:T(8,128)}, f32[512,768]{1,0:T(8,128)S(1)}, u32[]{:S(2)}) copy-start(f32[512,768]{1,0:T(8,128)S(1)} %get-tuple-element.467) | copy-start | bytes 4718596
  109.7 21.7 %copy-start.159 = (f32[512]{0:T(512)}, f32[512]{0:T(512)S(1)}, u32[]{:S(2)}) copy-start(f32[512]{0:T(512)S(1)} %broadcast_multiply_fusion.25) | copy-start | bytes 6148
  110.0 11.3 %copy-start.156 = (f32[512]{0:T(512)}, f32[512]{0:T(512)S(1)}, u32[]{:S(2)}) copy-start(f32[512]{0:T(512)S(1)} %add_rsqrt_fusion.1) | copy-start | bytes 6148
  110.0 16.4 %copy-start.183 = (f32[512]{0:T(512)}, f32[512]{0:T(512)S(1)}, u32[]{:S(2)}) copy-start(f32[512]{0:T(512)S(1)} %add_rsqrt_fusion.3) | copy-start | bytes 6148
  110.0 21.3 %copy-start.180 = (f32[512]{0:T(512)}, f32[512]{0:T(512)S(1)}, u32[]{:S(2)}) copy-start(f32[512]{0:T(512)S(1)} %add_rsqrt_fusion.5) | copy-start | bytes 6148
  136.4 63.7 %copy-start.6 = (f32[512,768]{1,0:T(8,128)S(1)}, f32[512,768]{1,0:T(8,128)}, u32[]{:S(2)}) copy-start(f32[512,768]{1,0:T(8,128)} %copy-done.5) | copy-start | bytes 4718596
  136.4 63.7 %copy-start.63 = (bf16[3072,768]{1,0:T(8,128)(2,1)S(1)}, bf16[3072,768]{1,0:T(8,128)(2,1)}, u32[]{:S(2)}) copy-start(bf16[3072,768]{1,0:T(8,128)(2,1)} %all-gather.12.cloned.1.call-done) | copy-start | bytes 14155780
  136.4 63.8 %copy-start.142 = (f32[768]{0:T(1024)S(1)}, f32[768]{0:T(1024)}, u32[]{:S(2)}) copy-start(f32[768]{0:T(1024)} %copy-done.141) | copy-start | bytes 9220
  136.4 63.8 %copy-start.145 = (f32[768]{0:T(1024)S(1)}, f32[768]{0:T(1024)}, u32[]{:S(2)}) copy-start(f32[768]{0:T(1024)} %copy-done.144) | copy-start | bytes 9220
  136.4 63.8 %copy-start.148 = (f32[512]{0:T(512)S(1)}, f32[512]{0:T(512)}, u32[]{:S(2)}) copy-start(f32[512]{0:T(512)} %copy-done.147) | copy-start | bytes 6148
  136.4 63.8 %copy-start.157 = (f32[512]{0:T(512)S(1)}, f32[512]{0:T(512)}, u32[]{:S(2)}) copy-start(f32[512]{0:T(512)} %copy-done.156) | copy-start | bytes 6148
  136.4 63.8 %copy-start.190 = (f32[768]{0:T(1024)S(1)}, f32[768]{0:T(1024)}, u32[]{:S(2)}) copy-start(f32[768]{0:T(1024)} %get-tuple-element.384) | copy-start | bytes 9220
  136.4 63.7 %copy-start.209 = (f32[768]{0:T(1024)S(1)}, f32[768]{0:T(1024)}, u32[]{:S(2)}) copy-start(f32[768]{0:T(1024)} %broadcast_multiply_fusion.2) | copy-start | bytes 9220
  200.1 9.6 %copy-start.87 = (bf16[512,3072]{1,0:T(8,128)(2,1)}, bf16[512,3072]{1,0:T(8,128)(2,1)S(1)}, u32[]{:S(2)}) copy-start(bf16[512,3072]{1,0:T(8,128)(2,1)S(1)} %get-tuple-element.433) | copy-start | bytes 9437188
  220.5 46.9 %copy-start.60 = (f32[512,768]{1,0:T(8,128)}, f32[512,768]{1,0:T(8,128)S(1)}, u32[]{:S(2)}) copy-start(f32[512,768]{1,0:T(8,128)S(1)} %get-tuple-element.427) | copy-start | bytes 4718596
  223.6 19.4 %copy-start.35 = (f32[512,768]{1,0:T(8,128)}, f32[512,768]{1,0:T(8,128)S(1)}, u32[]{:S(2)}) copy-start(f32[512,768]{1,0:T(8,128)S(1)} %get-tuple-element.415) | copy-start | bytes 4718596
  250.6 19.6 %copy-start.33 = (f32[512,768]{1,0:T(8,128)}, f32[512,768]{1,0:T(8,128)S(1)}, u32[]{:S(2)}) copy-start(f32[512,768]{1,0:T(8,128)S(1)} %get-tuple-element.403) | copy-start | bytes 4718596
  258.6 11.6 %copy-start.92 = (bf16[512,3072]{1,0:T(8,128)(2,1)}, bf16[512,3072]{1,0:T(8,128)(2,1)S(1)}, u32[]{:S(2)}) copy-start(bf16[512,3072]{1,0:T(8,128)(2,1)S(1)} %get-tuple-element.512) | copy-start | bytes 9437188
  281.1 14.1 %copy-start.80 = (bf16[512,768]{0,1:T(8,128)(2,1)S(1)}, bf16[512,768]{0,1:T(8,128)(2,1)}, u32[]{:S(2)}) copy-start(bf16[512,768]{0,1:T(8,128)(2,1)} %copy.71) | copy-start | bytes 2359300
  351.1 20.4 %slice-start.9 = ((s8[12582912]{0:T(1024)(128)(4,1)}), s8[4194304]{0:T(1024)(128)(4,1)S(1)}, s32[]{:S(2)}) async-start(s8[12582912]{0:T(1024)(128)(4,1)} %bitcast.235), calls=%async_computation.28 | async-start | bytes 8388608
  351.1 20.4 %slice-start.10 = ((s8[12582912]{0:T(1024)(128)(4,1)}), s8[4194304]{0:T(1024)(128)(4,1)S(1)}, s32[]{:S(2)}) async-start(s8[12582912]{0:T(1024)(128)(4,1)} %bitcast.235), calls=%async_computation.29 | async-start | bytes 8388608
  362.0 9.5 %slice-start.11 = ((s8[12582912]{0:T(1024)(128)(4,1)}), s8[4194304]{0:T(1024)(128)(4,1)S(1)}, s32[]{:S(2)}) async-start(s8[12582912]{0:T(1024)(128)(4,1)} %bitcast.235), calls=%async_computation.30 | async-start | bytes 8388608
  371.5 10.8 %copy-start.20 = (bf16[512,768]{0,1:T(8,128)(2,1)S(1)}, bf16[512,768]{0,1:T(8,128)(2,1)}, u32[]{:S(2)}) copy-start(bf16[512,768]{0,1:T(8,128)(2,1)} %copy-done.19) | copy-start | bytes 2359300
  371.5 19.2 %slice-start.3 = ((s8[12582912]{0:T(1024)(128)(4,1)}), s8[4194304]{0:T(1024)(128)(4,1)S(1)}, s32[]{:S(2)}) async-start(s8[12582912]{0:T(1024)(128)(4,1)} %bitcast.231), calls=%async_computation.22 | async-start | bytes 8388608
  371.5 19.2 %slice-start.4 = ((s8[12582912]{0:T(1024)(128)(4,1)}), s8[4194304]{0:T(1024)(128)(4,1)S(1)}, s32[]{:S(2)}) async-start(s8[12582912]{0:T(1024)(128)(4,1)} %bitcast.231), calls=%async_computation.23 | async-start | bytes 8388608
  390.8 13.7 %slice-start.6 = ((s8[12582912]{0:T(1024)(128)(4,1)}), s8[4194304]{0:T(1024)(128)(4,1)S(1)}, s32[]{:S(2)}) async-start(s8[12582912]{0:T(1024)(128)(4,1)} %bitcast.233), calls=%async_computation.25 | async-start | bytes 8388608
  390.8 13.7 %slice-start.7 = ((s8[12582912]{0:T(1024)(128)(4,1)}), s8[4194304]{0:T(1024)(128)(4,1)S(1)}, s32[]{:S(2)}) async-start(s8[12582912]{0:T(1024)(128)(4,1)} %bitcast.233), calls=%async_computation.26 | async-start | bytes 8388608
  404.5 13.2 %slice-start = ((s8[12582912]{0:T(1024)(128)(4,1)}), s8[4194304]{0:T(1024)(128)(4,1)S(1)}, s32[]{:S(2)}) async-start(s8[12582912]{0:T(1024)(128)(4,1)} %bitcast.229), calls=%async_computation.19 | async-start | bytes 8388608
  404.5 13.2 %slice-start.1 = ((s8[12582912]{0:T(1024)(128)(4,1)}), s8[4194304]{0:T(1024)(128)(4,1)S(1)}, s32[]{:S(2)}) async-start(s8[12582912]{0:T(1024)(128)(4,1)} %bitcast.229), calls=%async_computation.20 | async-start | bytes 8388608
  414.8 22.4 %copy-start.97 = (bf16[512,12,64]{0,2,1:T(8,128)(2,1)}, bf16[512,12,64]{0,2,1:T(8,128)(2,1)S(1)}, u32[]{:S(2)}) copy-start(bf16[512,12,64]{0,2,1:T(8,128)(2,1)S(1)} %get-tuple-element.497) | copy-start | bytes 2359300
  427.3 14.8 %copy-start.31 = (bf16[512,12,64]{0,2,1:T(8,128)(2,1)}, bf16[512,12,64]{0,2,1:T(8,128)(2,1)S(1)}, u32[]{:S(2)}) copy-start(bf16[512,12,64]{0,2,1:T(8,128)(2,1)S(1)} %get-tuple-element.491) | copy-start | bytes 2359300
  429.4 12.8 %copy-start.128 = (bf16[12,512,64]{1,2,0:T(8,128)(2,1)}, bf16[12,512,64]{1,2,0:T(8,128)(2,1)S(1)}, u32[]{:S(2)}) copy-start(bf16[12,512,64]{1,2,0:T(8,128)(2,1)S(1)} %multiply_convert_fusion.8) | copy-start | bytes 2359300
  454.1 89.3 %reduce-scatter.16.cloned.1.call-start = ((), (), s32[]{:S(2)}) async-start(), calls=%async_computation.11 | async-start | bytes 1769472 | tf_op jit(solution)/shard_map/reduce_scatter | solution.py:281
  460.7 9.2 %copy-start.36 = (f32[512,768]{1,0:T(8,128)S(1)}, f32[512,768]{1,0:T(8,128)}, u32[]{:S(2)}) copy-start(f32[512,768]{1,0:T(8,128)} %copy-done.35) | copy-start | bytes 4718596
  469.8 73.5 %reduce-scatter.20.cloned.1.call-start = ((), (), s32[]{:S(2)}) async-start(), calls=%async_computation.13 | async-start | bytes 7077888 | tf_op jit(solution)/shard_map/reduce_scatter | solution.py:281
  496.6 8.8 %copy-start.53 = (f32[512,768]{1,0:T(8,128)S(1)}, f32[512,768]{1,0:T(8,128)}, u32[]{:S(2)}) copy-start(f32[512,768]{1,0:T(8,128)} %copy-done.49) | copy-start | bytes 4718596
  496.6 8.8 %copy-start.155 = (f32[512]{0:T(512)S(1)}, f32[512]{0:T(512)}, u32[]{:S(2)}) copy-start(f32[512]{0:T(512)} %copy-done.153) | copy-start | bytes 6148
  496.6 8.8 %copy-start.185 = (f32[512]{0:T(512)S(1)}, f32[512]{0:T(512)}, u32[]{:S(2)}) copy-start(f32[512]{0:T(512)} %copy-done.183) | copy-start | bytes 6148
  496.6 47.9 %reduce-scatter.18.cloned.1.call-start = ((), (), s32[]{:S(2)}) async-start(), calls=%async_computation.12 | async-start | bytes 7077888 | tf_op jit(solution)/shard_map/reduce_scatter | solution.py:281
  530.4 35.2 %reduce-scatter.28.cloned.1.call-start = ((), (), s32[]{:S(2)}) async-start(), calls=%async_computation.17 | async-start | bytes 294912
  535.9 30.6 %reduce-scatter.26.cloned.1.call-start = ((), (), s32[]{:S(2)}) async-start(), calls=%async_computation.16 | async-start | bytes 294912
  537.6 39.7 %reduce-scatter.24.cloned.1.call-start = ((), (), s32[]{:S(2)}) async-start(), calls=%async_computation.15 | async-start | bytes 294912
  538.6 10.7 %copy-start.65 = (bf16[768,2304]{1,0:T(8,128)(2,1)S(1)}, bf16[768,2304]{1,0:T(8,128)(2,1)}, u32[]{:S(2)}) copy-start(bf16[768,2304]{1,0:T(8,128)(2,1)} %all-gather.6.cloned.1.call-done) | copy-start | bytes 10616836
  538.6 276.7 %all-reduce.5.cloned.1.call-start = ((), (), s32[]{:S(2)}) async-start(), calls=%async_computation.18 | async-start | bytes 14155776 | tf_op jit(solution)/shard_map/psum | solution.py:283
  (190 other events, 722.3 us)
Sparse Core Ops, SparseCore 0:
  9.6 11.9 all-gather.7
  23.1 13.8 all-gather.5
  38.6 15.6 all-gather.9
  55.6 15.6 all-gather.11
  454.2 12.5 reduce-scatter.21
  470.0 9.9 reduce-scatter.15
  496.7 13.8 reduce-scatter.19
  530.5 13.9 reduce-scatter.17
  546.7 8.6 reduce-scatter.27
  557.5 8.7 reduce-scatter.25
  568.5 8.7 reduce-scatter.23
  584.1 231.0 all-reduce.4
where the time goes:
time: 843 us; the launch traced here: 833 us
  matrix products  398 us (47%)
  waiting for transfers between devices  180 us (21%)
  other arithmetic  106 us (13%)
  blocking collectives  90.5 us (11%)
  local copies, waits for them, and re-layouts  39.8 us (5%)
  between operations  18.3 us (2%)
    psum x1, waiting for transfers between devices, body(): lax.psum(as_sent(owned), 'rep')  154 us
    psum x1, blocking collectives, body(): lax.psum(as_sent(owned), 'rep')  80.5 us
    dot_general x4, matrix products, forward(): jnp.dot(first_low, up_bin, preferred_element_type=jnp.float32) + hidden_all  78.6 us
    dot_general x4, matrix products, attend_back(): jnp.einsum('qhd,khd->hqk', context_part, value_low, preferred_element_typ...  44.1 us
    dot_general x4, matrix products, backward(): jnp.einsum('lf,ld->fd', hidden_low, mixed_low, preferred_element_type=jnp...  35.6 us
    convert_element_type x4, other arithmetic, attend_back(): score_low = (probs * (prob_back - row_dot)).astype(jnp.bfloat16)  34.1 us
    dot_general x4, matrix products, attend_back(): jnp.einsum('hqk,qhd->khd', probs.astype(jnp.bfloat16), context_part, pref...  33.7 us
    dot_general x4, matrix products, backward(): jnp.einsum('ld,fd->lf', mixed_low, down_bin, preferred_element_type=jnp.f...  33.4 us
  transfers between devices with their start and end apart: 12, of which 4 were waited for; matrix products, arithmetic and copies ran while one was open for 22% of the time, Pallas kernels for 0%

commit v1 on v0

v1 whole, which is shorter than its diff:
```python
import functools

import jax
import jax.numpy as jnp
from jax import lax
from jax.experimental import pallas as pl
from jax.experimental.pallas import tpu as pltpu
from jax.sharding import PartitionSpec as P

HEAD_DIM = 64
EPS = 1e-05
NEG = -1e30
BF = jnp.bfloat16
F32 = jnp.float32
MB = 1 << 20


def params(mb=56, **kw):
    return pltpu.CompilerParams(vmem_limit_bytes=mb * MB, **kw)


def dot(a, b):
    return jnp.dot(a, b, preferred_element_type=F32)


def dot_nt(a, b):
    return lax.dot_general(a, b, (((1,), (1,)), ((), ())), preferred_element_type=F32)


def dot_tn(a, b):
    return lax.dot_general(a, b, (((0,), (0,)), ((), ())), preferred_element_type=F32)


def full(shape):
    return pl.BlockSpec(shape, lambda *_: (0,) * len(shape))


def cost(flops, nbytes, trans=0):
    return pl.CostEstimate(flops=int(flops), bytes_accessed=int(nbytes), transcendentals=int(trans))


def binary_halves(first, second):
    rows = 2 * first.shape[0]
    total = jnp.sum(jnp.abs(first.astype(F32)), axis=0, keepdims=True) + jnp.sum(
        jnp.abs(second.astype(F32)), axis=0, keepdims=True
    )
    scale = (total / rows).astype(BF)
    return (
        jnp.where(first >= 0, scale, -scale).astype(BF),
        jnp.where(second >= 0, scale, -scale).astype(BF),
    )


def prep_qkv_kernel(core_ref, own_ref, other_ref, small_own_ref, small_other_ref, out_ref, small_ref):
    core = core_ref[0]
    half = own_ref.shape[0]
    own_at = pl.multiple_of(core * half, half)
    other_at = pl.multiple_of((1 - core) * half, half)
    own, other = binary_halves(own_ref[...], other_ref[...])
    out_ref[pl.ds(own_at, half), :] = own
    out_ref[pl.ds(other_at, half), :] = other

    @pl.when(pl.program_id(0) == 0)
    def _():
        small_ref[:, pl.ds(own_at, half)] = small_own_ref[...].astype(F32)
        small_ref[:, pl.ds(other_at, half)] = small_other_ref[...].astype(F32)


def prep_qkv(core, own, other, small_own, small_other):
    half, cols = own.shape
    rows = 2 * half
    step = rows
    return pl.pallas_call(
        prep_qkv_kernel,
        grid_spec=pltpu.PrefetchScalarGridSpec(
            num_scalar_prefetch=1,
            grid=(cols // step,),
            in_specs=[
                pl.BlockSpec((half, step), lambda j, c: (0, j)),
                pl.BlockSpec((half, step), lambda j, c: (0, j)),
                full(small_own.shape),
                full(small_own.shape),
            ],
            out_specs=[
                pl.BlockSpec((rows, step), lambda j, c: (0, j)),
                full((small_own.shape[0], rows)),
            ],
        ),
        out_shape=[
            jax.ShapeDtypeStruct((rows, cols), BF),
            jax.ShapeDtypeStruct((small_own.shape[0], rows), F32),
        ],
        compiler_params=params(),
        cost_estimate=cost(4 * rows * cols, 4 * rows * cols),
        name="prep_qkv",
    )(core, own, other, small_own, small_other)


def prep_rest_kernel(core_ref, out_a, out_b, up_a, up_b, dn_a, dn_b, out_ref, up_ref, dn_ref):
    core = core_ref[0]
    half = out_a.shape[0]
    width = 2 * half
    own_at = pl.multiple_of(core * half, half)
    other_at = pl.multiple_of((1 - core) * half, half)
    own, other = binary_halves(out_a[...], out_b[...])
    out_ref[pl.ds(own_at, half), :] = own
    out_ref[pl.ds(other_at, half), :] = other
    hidden = up_a.shape[1]
    chunks = hidden // width
    for j in range(hidden // half):
        own, other = binary_halves(up_a[:, j * half : (j + 1) * half], up_b[:, j * half : (j + 1) * half])
        at = (j % chunks) * width + (j // chunks) * half
        up_ref[pl.ds(own_at, half), at : at + half] = own
        up_ref[pl.ds(other_at, half), at : at + half] = other
    own, other = binary_halves(dn_a[...], dn_b[...])
    for c in range(chunks):
        dn_ref[pl.ds(pl.multiple_of(c * width + own_at, half), half), :] = own[c * half : (c + 1) * half]
        dn_ref[pl.ds(pl.multiple_of(c * width + other_at, half), half), :] = other[c * half : (c + 1) * half]


def prep_rest(core, out_a, out_b, up_a, up_b, dn_a, dn_b):
    half, width = out_a.shape
    hidden = up_a.shape[1]
    vm = pl.BlockSpec(memory_space=pltpu.VMEM)
    return pl.pallas_call(
        prep_rest_kernel,
        in_specs=[pl.BlockSpec(memory_space=pltpu.SMEM)] + [vm] * 6,
        out_specs=[vm] * 3,
        out_shape=[
            jax.ShapeDtypeStruct((width, width), BF),
            jax.ShapeDtypeStruct((width, hidden), BF),
            jax.ShapeDtypeStruct((hidden, width), BF),
        ],
        compiler_params=params(),
        cost_estimate=cost(8 * width * hidden, 8 * width * hidden),
        name="prep_rest",
    )(core, out_a, out_b, up_a, up_b, dn_a, dn_b)


def attend_kernel(
    tokens_ref, rows_ref, cols_ref, qkv_ref, out_ref, small_ref, joined_ref, ctx_ref, lse_ref, norm_ref, inv_ref,
    bias_ref,
):
    length, width = tokens_ref.shape[1:]
    x = tokens_ref[0]
    for part, bias_row in ((0, 0), (1, None), (2, 1)):
        joined = dot(x, qkv_ref[:, part * width : (part + 1) * width])
        if bias_row is not None:
            joined = joined + small_ref[bias_row : bias_row + 1, :]
        joined_ref[0, :, part * width : (part + 1) * width] = joined.astype(BF)
    bias_ref[...] = jnp.where(cols_ref[0] >= rows_ref[0], 0.0, NEG).astype(F32)
    lane = lax.broadcasted_iota(jnp.int32, (length, 128), 1)
    low = lane < HEAD_DIM
    lse_all = jnp.zeros((length, 128), F32)
    tile = min(TILE_F, length)
    for pair in range(width // 128):
        q2 = joined_ref[0, :, pair * 128 : pair * 128 + 128] * BF(0.125)
        k2 = joined_ref[0, :, width + pair * 128 : width + pair * 128 + 128]
        v2 = joined_ref[0, :, 2 * width + pair * 128 : 2 * width + pair * 128 + 128]
        for t in range(length // tile):
            rows = slice(t * tile, (t + 1) * tile)
            parts = []
            for h in range(2):
                mine = low[rows] if h == 0 else ~low[rows]
                qm = jnp.where(mine, q2[rows], BF(0))
                scores = dot_nt(qm, k2) + bias_ref[rows, :]
                peak = jnp.max(scores, axis=-1, keepdims=True)
                raised = jnp.exp(scores - peak)
                total = jnp.sum(raised, axis=-1, keepdims=True)
                parts.append(dot(raised.astype(BF), v2) / total)
                lse_ref_col = peak + jnp.log(total)
                bias_lane = lane[rows] == 2 * pair + h
                lse_cols = jnp.where(bias_lane, lse_ref_col, 0.0)
                if h == 0:
                    pair_lse = lse_cols
                else:
                    pair_lse = pair_lse + lse_cols
            ctx_ref[0, rows, pair * 128 : pair * 128 + 128] = jnp.where(low[rows], parts[0], parts[1]).astype(BF)
            if t == 0:
                tiles_lse = [pair_lse]
            else:
                tiles_lse.append(pair_lse)
        lse_all = lse_all + jnp.concatenate(tiles_lse, axis=0)
    lse_ref[0] = lse_all.T[0:16, :]
    resid = x.astype(F32) + dot(ctx_ref[0], out_ref[...]) + small_ref[2:3, :]
    center = resid - jnp.mean(resid, axis=-1, keepdims=True)
    inverse = lax.rsqrt(jnp.mean(center * center, axis=-1, keepdims=True) + EPS)
    norm_ref[0] = center * inverse
    inv_ref[0] = inverse


TILE_F = 256


def attend(tokens, block_ids, qkv_bin, out_bin, small):
    seqs, length, width = tokens.shape
    rows = block_ids.reshape(seqs, 1, length)
    cols = block_ids.reshape(seqs, length, 1)
    per_seq = lambda *shape: pl.BlockSpec((1,) + shape, lambda s: (s,) + (0,) * len(shape))
    return pl.pallas_call(
        attend_kernel,
        grid=(seqs,),
        in_specs=[
            per_seq(length, width),
            per_seq(1, length),
            per_seq(length, 1),
            full(qkv_bin.shape),
            full(out_bin.shape),
            full(small.shape),
        ],
        out_specs=[
            per_seq(length, 3 * width),
            per_seq(length, width),
            per_seq(16, length),
            per_seq(length, width),
            per_seq(length, 1),
        ],
        out_shape=[
            jax.ShapeDtypeStruct((seqs, length, 3 * width), BF),
            jax.ShapeDtypeStruct((seqs, length, width), BF),
            jax.ShapeDtypeStruct((seqs, 16, length), F32),
            jax.ShapeDtypeStruct((seqs, length, width), F32),
            jax.ShapeDtypeStruct((seqs, length, 1), F32),
        ],
        scratch_shapes=[pltpu.VMEM((length, length), F32)],
        compiler_params=params(),
        cost_estimate=cost(seqs * length * width * (8 * width + 16 * length), 30 * seqs * length * width),
        name="attend",
    )(tokens, rows, cols, qkv_bin, out_bin, small)


def gelu_pair(u):
    cdf = 0.5 + 0.5 * lax.erf(u * 0.7071067811865476)
    density = jnp.exp(-0.5 * u * u) * 0.3989422804014327
    return u * cdf, cdf + u * density


def norm_back(upstream, normed, inverse, gain):
    scaled = upstream * gain
    weighted = upstream * normed
    centered = (
        scaled
        - jnp.mean(scaled, axis=-1, keepdims=True)
        - normed * jnp.mean(weighted * gain, axis=-1, keepdims=True)
    )
    return centered * inverse, jnp.sum(weighted, axis=0, keepdims=True), jnp.sum(upstream, axis=0, keepdims=True)


def feed_kernel(
    norm_ref, teacher_ref, small_ref, up_ref, dn_ref,
    final_ref, first_low_ref, hidden_ref, slope_ref, second_ref, mixed_ref, sums_ref,
):
    width = norm_ref.shape[2]
    first = norm_ref[0] * small_ref[4:5, :] + small_ref[6:7, :]
    first_low = first.astype(BF)
    first_low_ref[0] = first_low
    acc = first + small_ref[3:4, :]
    for c in range(up_ref.shape[1] // width):
        cols = slice(c * width, (c + 1) * width)
        pre = dot(first_low, up_ref[:, cols]) + small_ref[8 + c : 9 + c, :]
        value, slope = gelu_pair(pre)
        value = value.astype(BF)
        hidden_ref[0, :, cols] = value
        slope_ref[0, :, cols] = slope.astype(BF)
        acc = acc + dot(value, dn_ref[cols, :])
    center = acc - jnp.mean(acc, axis=-1, keepdims=True)
    inverse = lax.rsqrt(jnp.mean(center * center, axis=-1, keepdims=True) + EPS)
    normed = center * inverse
    gain = small_ref[5:6, :]
    final = normed * gain + small_ref[7:8, :]
    final_ref[0] = final.astype(BF)
    upstream = final - teacher_ref[0].astype(F32)
    second, gain_sum, shift_sum = norm_back(upstream, normed, inverse, gain)
    second_ref[0] = second
    mixed_ref[0] = second.astype(BF)

    @pl.when(pl.program_id(0) == 0)
    def _():
        sums_ref[...] = jnp.zeros_like(sums_ref)

    sums_ref[0:1, :] += gain_sum
    sums_ref[1:2, :] += shift_sum
    sums_ref[2:3, :] += jnp.sum(second, axis=0, keepdims=True)


def feed(norm, teacher, small, up_bin, dn_bin):
    seqs, length, width = norm.shape
    hidden = up_bin.shape[1]
    per_seq = lambda *shape: pl.BlockSpec((1,) + shape, lambda s: (s,) + (0,) * len(shape))
    like = lambda n, dt: jax.ShapeDtypeStruct((seqs, length, n), dt)
    return pl.pallas_call(
        feed_kernel,
        grid=(seqs,),
        in_specs=[
            per_seq(length, width),
            per_seq(length, width),
            full(small.shape),
            full(up_bin.shape),
            full(dn_bin.shape),
        ],
        out_specs=[
            per_seq(length, width),
            per_seq(length, width),
            per_seq(length, hidden),
            per_seq(length, hidden),
            per_seq(length, width),
            per_seq(length, width),
            full((8, width)),
        ],
        out_shape=[
            like(width, BF), like(width, BF), like(hidden, BF), like(hidden, BF), like(width, F32), like(width, BF),
            jax.ShapeDtypeStruct((8, width), F32),
        ],
        compiler_params=params(),
        cost_estimate=cost(4 * seqs * length * width * hidden, 36 * seqs * length * width),
        name="feed",
    )(norm, teacher, small, up_bin, dn_bin)


def feed_back_kernel(
    mixed_ref, first_ref, hidden_ref, slope_ref, up_ref, dn_ref,
    pre_ref, dgrad_ref, ugrad_ref, hsum_ref, dacc, uacc,
):
    tile = pl.program_id(1)
    mixed = mixed_ref[0]
    pre_back = dot_nt(mixed, dn_ref[...]) * slope_ref[0].astype(F32)
    pre_low = pre_back.astype(BF)
    pre_ref[0] = pre_low
    dpart = dot_tn(hidden_ref[0], mixed)
    upart = dot_tn(first_ref[0], pre_low)
    hpart = jnp.sum(pre_back, axis=0, keepdims=True)

    @pl.when(tile == 0)
    def _():
        dacc[...] = dpart
        uacc[...] = upart
        hsum_ref[0, 0:1, :] = hpart

    @pl.when(tile > 0)
    def _():
        dacc[...] += dpart
        uacc[...] += upart
        hsum_ref[0, 0:1, :] += hpart

    @pl.when(tile == pl.num_programs(1) - 1)
    def _():
        dgrad_ref[...] = dacc[...].astype(BF)
        ugrad_ref[...] = uacc[...].astype(BF)


def feed_back(mixed, first_low, hidden, slope, up_bin, dn_bin):
    seqs, length, width = mixed.shape
    units = hidden.shape[2]
    chunks = units // width
    return pl.pallas_call(
        feed_back_kernel,
        grid=(chunks, seqs),
        in_specs=[
            pl.BlockSpec((1, length, width), lambda c, s: (s, 0, 0)),
            pl.BlockSpec((1, length, width), lambda c, s: (s, 0, 0)),
            pl.BlockSpec((1, length, width), lambda c, s: (s, 0, c)),
            pl.BlockSpec((1, length, width), lambda c, s: (s, 0, c)),
            pl.BlockSpec((width, width), lambda c, s: (0, c)),
            pl.BlockSpec((width, width), lambda c, s: (c, 0)),
        ],
        out_specs=[
            pl.BlockSpec((1, length, width), lambda c, s: (s, 0, c)),
            pl.BlockSpec((width, width), lambda c, s: (c, 0)),
            pl.BlockSpec((width, width), lambda c, s: (c, 0)),
            pl.BlockSpec((1, 8, width), lambda c, s: (c, 0, 0)),
        ],
        out_shape=[
            jax.ShapeDtypeStruct((seqs, length, units), BF),
            jax.ShapeDtypeStruct((units, width), BF),
            jax.ShapeDtypeStruct((units, width), BF),
            jax.ShapeDtypeStruct((chunks, 8, width), F32),
        ],
        scratch_shapes=[pltpu.VMEM((width, width), F32), pltpu.VMEM((width, width), F32)],
        compiler_params=params(),
        cost_estimate=cost(6 * seqs * length * width * units, 20 * seqs * length * units),
        name="feed_back",
    )(mixed, first_low, hidden, slope, up_bin, dn_bin)


def norm_kernel(
    second_ref, pre_ref, norm_ref, inv_ref, ctx_ref, up_ref, out_ref, small_ref,
    resid_ref, cback_ref, rowdot_ref, ograd_ref, sums_ref, oacc,
):
    s = pl.program_id(0)
    width = second_ref.shape[2]
    back = second_ref[0] + dot_nt(pre_ref[0], up_ref[...])
    resid, gain_sum, shift_sum = norm_back(back, norm_ref[0], inv_ref[0], small_ref[4:5, :])
    resid_ref[0] = resid
    low = resid.astype(BF)
    cback = dot_nt(low, out_ref[...]).astype(BF)
    cback_ref[0] = cback
    ctx = ctx_ref[0]
    opart = dot_tn(ctx, low)
    prod = cback.astype(F32) * ctx.astype(F32)
    high = prod.astype(BF)
    rest = (prod - high.astype(F32)).astype(BF)
    heads = lax.broadcasted_iota(jnp.int32, (16, width), 0)
    lanes = lax.broadcasted_iota(jnp.int32, (16, width), 1)
    pick = jnp.where((lanes >= heads * HEAD_DIM) & (lanes < heads * HEAD_DIM + HEAD_DIM), 1.0, 0.0).astype(BF)
    rowdot_ref[0] = dot_nt(pick, high) + dot_nt(pick, rest)

    @pl.when(s == 0)
    def _():
        oacc[...] = opart
        sums_ref[...] = jnp.zeros_like(sums_ref)

    @pl.when(s > 0)
    def _():
        oacc[...] += opart

    sums_ref[0:1, :] += gain_sum
    sums_ref[1:2, :] += shift_sum
    sums_ref[2:3, :] += jnp.sum(resid, axis=0, keepdims=True)

    @pl.when(s == pl.num_programs(0) - 1)
    def _():
        ograd_ref[...] = oacc[...].astype(BF)


def norm_one_back(second, pre_low, norm, inv, ctx, up_bin, out_bin, small):
    seqs, length, width = second.shape
    per_seq = lambda *shape: pl.BlockSpec((1,) + shape, lambda s: (s,) + (0,) * len(shape))
    return pl.pallas_call(
        norm_kernel,
        grid=(seqs,),
        in_specs=[
            per_seq(length, width),
            per_seq(length, pre_low.shape[2]),
            per_seq(length, width),
            per_seq(length, 1),
            per_seq(length, width),
            full(up_bin.shape),
            full(out_bin.shape),
            full(small.shape),
        ],
        out_specs=[
            per_seq(length, width),
            per_seq(length, width),
            per_seq(16, length),
            full((width, width)),
            full((8, width)),
        ],
        out_shape=[
            jax.ShapeDtypeStruct((seqs, length, width), F32),
            jax.ShapeDtypeStruct((seqs, length, width), BF),
            jax.ShapeDtypeStruct((seqs, 16, length), F32),
            jax.ShapeDtypeStruct((width, width), BF),
            jax.ShapeDtypeStruct((8, width), F32),
        ],
        scratch_shapes=[pltpu.VMEM((width, width), F32)],
        compiler_params=params(),
        cost_estimate=cost(2 * seqs * length * width * 6 * width, 40 * seqs * length * width),
        name="norm_one_back",
    )(second, pre_low, norm, inv, ctx, up_bin, out_bin, small)


GROUP = 256
TILE_B = 256


def attend_back_kernel(
    tokens_ref, rows_ref, cols_ref, q_ref, k_ref, v_ref, cback_ref, lse_ref, rowdot_ref,
    jlow_ref, grad_ref, sums_ref, acc, bias_ref,
):
    g, s = pl.program_id(0), pl.program_id(1)
    length = tokens_ref.shape[1]
    tile = min(TILE_B, length)
    bias_ref[...] = jnp.where(rows_ref[0] >= cols_ref[0], 0.0, NEG).astype(F32)
    lane = lax.broadcasted_iota(jnp.int32, (length, 128), 1)
    low = lane < HEAD_DIM

    for pair in range(GROUP // 128):
        at = slice(pair * 128, pair * 128 + 128)
        q2 = q_ref[0, :, at] * BF(0.125)
        k2 = k_ref[0, :, at]
        v2 = v_ref[0, :, at]
        do2 = cback_ref[0, :, at]
        dq = None
        for t in range(length // tile):
            rows = slice(t * tile, (t + 1) * tile)
            dks, dvs = [], []
            for h in range(2):
                mine = low[rows] if h == 0 else ~low[rows]
                km = jnp.where(mine, k2[rows], BF(0))
                vm = jnp.where(mine, v2[rows], BF(0))
                head = g * (GROUP // HEAD_DIM) + pair * 2 + h
                lse = lse_ref[0, pl.ds(head, 1), :]
                rowdot = rowdot_ref[0, pl.ds(head, 1), :]
                probs = jnp.exp(dot_nt(km, q2) + bias_ref[rows, :] - lse)
                dprobs = dot_nt(vm, do2)
                dscore = (probs * (dprobs - rowdot)).astype(BF)
                dvs.append(dot(probs.astype(BF), do2))
                dks.append(dot(dscore, q2))
                part = dot_tn(dscore, km * BF(0.125))
                dq = part if dq is None else dq + part
            dk = jnp.where(low[rows], dks[0], dks[1])
            dv = jnp.where(low[rows], dvs[0], dvs[1])
            jlow_ref[0, rows, GROUP + pair * 128 : GROUP + pair * 128 + 128] = dk.astype(BF)
            jlow_ref[0, rows, 2 * GROUP + pair * 128 : 2 * GROUP + pair * 128 + 128] = dv.astype(BF)
            vsum = jnp.sum(dv, axis=0, keepdims=True)
            vtotal = vsum if t == 0 else vtotal + vsum
        jlow_ref[0, :, at] = dq.astype(BF)
        qsum = jnp.sum(dq, axis=0, keepdims=True)

        @pl.when(s == 0)
        def _():
            sums_ref[0, 0:1, at] = qsum
            sums_ref[0, 1:2, at] = vtotal

        @pl.when(s > 0)
        def _():
            sums_ref[0, 0:1, at] += qsum
            sums_ref[0, 1:2, at] += vtotal

    part = dot_tn(tokens_ref[0], jlow_ref[0])

    @pl.when(s == 0)
    def _():
        acc[...] = part

    @pl.when(s > 0)
    def _():
        acc[...] += part

    @pl.when(s == pl.num_programs(1) - 1)
    def _():
        grad_ref[...] = acc[...].astype(BF)


def attend_back(tokens, block_ids, joined, cback, lse, rowdot):
    seqs, length, width = tokens.shape
    rows = block_ids.reshape(seqs, 1, length)
    cols = block_ids.reshape(seqs, length, 1)
    groups = width // GROUP
    whole = lambda *shape: pl.BlockSpec((1,) + shape, lambda g, s: (s,) + (0,) * len(shape))
    part = lambda k: pl.BlockSpec((1, length, GROUP), lambda g, s: (s, 0, k * groups + g))
    return pl.pallas_call(
        attend_back_kernel,
        grid=(groups, seqs),
        in_specs=[
            whole(length, width),
            whole(1, length),
            whole(length, 1),
            part(0),
            part(1),
            part(2),
            part(0),
            whole(16, length),
            whole(16, length),
        ],
        out_specs=[
            pl.BlockSpec((1, length, 3 * GROUP), lambda g, s: (s, 0, g)),
            pl.BlockSpec((width, 3 * GROUP), lambda g, s: (g, 0)),
            pl.BlockSpec((1, 8, GROUP), lambda g, s: (g, 0, 0)),
        ],
        out_shape=[
            jax.ShapeDtypeStruct((seqs, length, 3 * width), BF),
            jax.ShapeDtypeStruct((groups * width, 3 * GROUP), BF),
            jax.ShapeDtypeStruct((groups, 8, GROUP), F32),
        ],
        scratch_shapes=[pltpu.VMEM((width, 3 * GROUP), F32), pltpu.VMEM((length, length), F32)],
        compiler_params=params(),
        cost_estimate=cost(seqs * length * width * (6 * width + 40 * length), 30 * seqs * length * width),
        name="attend_back",
    )(tokens, rows, cols, joined, joined, joined, cback, lse, rowdot)


def token_kernel(resid_ref, jlow_ref, qkv_ref, grad_ref):
    width = resid_ref.shape[2]
    groups = width // GROUP
    total = resid_ref[0]
    for g in range(groups):
        for k in range(3):
            at = (3 * g + k) * GROUP
            col = k * width + g * GROUP
            total = total + dot_nt(jlow_ref[0, :, at : at + GROUP], qkv_ref[:, col : col + GROUP])
    grad_ref[0] = total


def token_back(resid, jlow, qkv_bin):
    seqs, length, width = resid.shape
    per_seq = lambda *shape: pl.BlockSpec((1,) + shape, lambda s: (s,) + (0,) * len(shape))
    return pl.pallas_call(
        token_kernel,
        grid=(seqs,),
        in_specs=[per_seq(length, width), per_seq(length, 3 * width), full(qkv_bin.shape)],
        out_specs=per_seq(length, width),
        out_shape=jax.ShapeDtypeStruct((seqs, length, width), F32),
        compiler_params=params(),
        cost_estimate=cost(6 * seqs * length * width * width, 16 * seqs * length * width),
        name="token_back",
    )(resid, jlow, qkv_bin)


def layer(core, tokens, teacher, block_ids, own, other, small_own, small_other):
    qkv_bin, small = prep_qkv(core, own[0], other[0], small_own, small_other)
    out_bin, up_bin, dn_bin = prep_rest(core, own[1], other[1], own[2], other[2], own[3], other[3])
    joined, ctx, lse, norm, inv = attend(tokens, block_ids, qkv_bin, out_bin, small)
    final, first_low, hidden, slope, second, mixed, sums_two = feed(norm, teacher, small, up_bin, dn_bin)
    pre_low, dgrad, ugrad, hsum = feed_back(mixed, first_low, hidden, slope, up_bin, dn_bin)
    resid, cback, rowdot, ograd, sums_one = norm_one_back(second, pre_low, norm, inv, ctx, up_bin, out_bin, small)
    jlow, qgrad, sums_qv = attend_back(tokens, block_ids, joined, cback, lse, rowdot)
    token_grad = token_back(resid, jlow, qkv_bin)
    return final, token_grad, dgrad, ugrad, ograd, qgrad, sums_two, hsum, sums_one, sums_qv


def as_sent(value):
    return jax.tree.map(lambda a: a.astype(BF), value)


def swap(value):
    return lax.ppermute(value, "shard", [(0, 1), (1, 0)])


def small_rows(biases, gain, shift, hidden_bias):
    rows = biases.shape[0]
    return jnp.concatenate([biases.T, gain.T, shift.T, hidden_bias.reshape(-1, rows)], axis=0)


def body(tokens, teacher, block_ids, *weights):
    qkv, out, up, down, biases, hidden_bias, gain, shift = weights
    shards = lax.axis_size("shard")
    if shards == 2:
        core = lax.axis_index("shard").reshape(1)
        own = (qkv, out, up, down)
        small_own = small_rows(biases, gain, shift, hidden_bias)
        small_other = swap(small_own)
        other = tuple(swap(w) for w in own)
    else:
        core = jnp.zeros((1,), jnp.int32)
        gathered = [lax.all_gather(w, "shard", axis=0, tiled=True) for w in weights]
        cut = [jnp.split(w, 2, axis=0) for w in gathered]
        own, other = (tuple(c[i] for c in cut[:4]) for i in range(2))
        small_own, small_other = (
            small_rows(cut[4][i], cut[6][i], cut[7][i], cut[5][i]) for i in range(2)
        )
    final, token_grad, dgrad, ugrad, ograd, qgrad, sums_two, hsum, sums_one, sums_qv = layer(
        core, tokens, teacher, block_ids, own, other, small_own, small_other
    )
    width, units = ograd.shape[0], dgrad.shape[0]
    chunks, half = units // width, width // 2
    groups = width // GROUP
    grads = (
        qgrad.reshape(groups, width, 3, GROUP).transpose(1, 2, 0, 3).reshape(width, 3 * width),
        ograd,
        ugrad.reshape(chunks, width, 2, half).transpose(1, 2, 0, 3).reshape(width, units),
        dgrad.reshape(chunks, 2, half, width).transpose(1, 0, 2, 3).reshape(units, width),
        jnp.stack([sums_qv[:, 0].reshape(-1), sums_qv[:, 1].reshape(-1), sums_one[2], sums_two[2]], axis=1),
        hsum[:, 0].reshape(chunks, 2, half).transpose(1, 0, 2).reshape(-1),
        jnp.stack([sums_one[0], sums_two[0]], axis=1),
        jnp.stack([sums_one[1], sums_two[1]], axis=1),
    )
    owned = lax.psum_scatter(as_sent(grads), "shard", scatter_dimension=0, tiled=True)
    summed = jax.tree.map(lambda part: part.astype(F32), lax.psum(owned, "rep"))
    return (final, token_grad) + tuple(summed)


def solution(mesh):
    placed = (
        P(("shard", "rep"), None, None),
        P(("shard", "rep"), None, None),
        P(("shard", "rep"), None),
        P("shard", None),
        P("shard", None),
        P("shard", None),
        P("shard", None),
        P("shard", None),
        P("shard"),
        P("shard", None),
        P("shard", None),
    )
    return jax.shard_map(
        body,
        mesh=mesh,
        in_specs=placed,
        out_specs=placed[:2] + placed[3:],
        check_vma=False,
    )
```

time: 843 us -> 641 us (0.76)
  matrix products: 398 us -> 0 us
  Pallas kernels: 0 us -> 257 us
  other arithmetic: 106 us -> 10.8 us
  local copies, waits for them, and re-layouts: 39.8 us -> 76 us
  waiting for transfers between devices: 180 us -> 192 us
    dot_general x72 -> x0, matrix products: 398 us -> none  [the longest x4 78.6 us: forward(): jnp.dot(first_low, up_bin, preferred_element_type=jnp.float32) + hidden_all]
    pallas_call x0 -> x8, Pallas kernels: none -> 257 us  [the longest x1 57.2 us: attend_back(): pl.pallas_call(attend_back_kernel, grid=(groups, seqs), in_specs=[whole(l...]
    reduce_sum x30 -> x0, other arithmetic: 44.1 us -> none  [the longest x4 11.5 us: attend(): total = jnp.sum(shifted, axis=-1, keepdims=True)]
    convert_element_type x21 -> x7, other arithmetic: 50.4 us -> 9.96 us  [body(): summed = jax.tree.map(lambda part: part.astype(F32), lax.psum(owned, 'rep'))]
    reshape x0 -> x6, local copies, waits for them, and re-layouts: none -> 31.9 us  [the longest x2 19.1 us: body(): ugrad.reshape(chunks, width, 2, half).transpose(1, 2, 0, 3)]
    transpose x0 -> x3, local copies, waits for them, and re-layouts: none -> 22.2 us  [the longest x1 10.9 us: body(): ugrad.reshape(chunks, width, 2, half).transpose(1, 2, 0, 3)]
    reduce_scatter x3, waiting for transfers between devices: 1.15 us -> 19.5 us  [body(): lax.psum_scatter(as_sent(grads), 'shard', scatter_dimension=0, tiled=True)]
    all_gather x4 -> x0, waiting for transfers between devices: 12.6 us -> none  [the longest x1 12.6 us: body(): lax.all_gather(qkv_weight, 'shard', axis=0, tiled=True)]
  transfers between devices with their start and end apart: 12 -> 13, of which waited for: 4 -> 7; matrix products, arithmetic and copies ran while one was open for 22% -> 8% of each run, Pallas kernels for 0% -> 3%
where the time goes in v1:
time: 641 us; the launch traced here: 636 us
  Pallas kernels  257 us (40%)
  waiting for transfers between devices  192 us (30%)
  blocking collectives  82.9 us (13%)
  local copies, waits for them, and re-layouts  76 us (12%)
  between operations  15.1 us (2%)
  other arithmetic  10.8 us (2%)
    psum x1, waiting for transfers between devices, body(): summed = jax.tree.map(lambda part: part.astype(F32), lax.psum(owned, 'rep'))  154 us
    psum x1, blocking collectives, body(): summed = jax.tree.map(lambda part: part.astype(F32), lax.psum(owned, 'rep'))  80.4 us
    pallas_call x1, Pallas kernels, attend_back(): pl.pallas_call(attend_back_kernel, grid=(groups, seqs), in_specs=[whole(l...  57.2 us
    pallas_call x1, Pallas kernels, attend(): pl.pallas_call(attend_kernel, grid=(seqs,), in_specs=[per_seq(length, wid...  49.9 us
    pallas_call x1, Pallas kernels, feed_back(): pl.pallas_call(feed_back_kernel, grid=(chunks, seqs), in_specs=[pl.BlockS...  47.5 us
    pallas_call x1, Pallas kernels, feed(): pl.pallas_call(feed_kernel, grid=(seqs,), in_specs=[per_seq(length, width...  38.2 us
    pallas_call x1, Pallas kernels, norm_one_back(): pl.pallas_call(norm_kernel, grid=(seqs,), in_specs=[per_seq(length, width...  34.1 us
    unnamed x31, local copies, waits for them, and re-layouts  20.8 us
  transfers between devices with their start and end apart: 13, of which 7 were waited for; matrix products, arithmetic and copies ran while one was open for 8% of the time, Pallas kernels for 3%

profile of v1, /device:TPU:0, one launch (start us, length us, event | category | flops | bytes accessed | tf_op | source)
XLA Modules:
  0.0 635.6 jit_solution(8645838421704544740)
XLA Ops:
  7.2 0.0 reduce-scatter.22.cloned.1.call-start
  7.2 0.5 collective-permute-start.3
  7.7 0.1 collective-permute-start.4
  7.8 0.4 collective-permute-start
  8.3 0.1 collective-permute-start.2
  8.3 0.7 reshape.58
  9.0 0.7 pad_maximum_fusion.small_own_ref
  9.8 0.5 collective-permute-start.1
  10.3 1.3 reshape.55.rows_ref
  11.6 2.1 copy.31.cols_ref
  13.6 0.9 collective-permute-done.1.small_other_ref
  14.5 4.5 collective-permute-done.other_ref
  19.0 5.1 prep_qkv.1
  24.2 0.8 copy-done.3
  25.0 0.8 copy-done.2
  25.8 11.5 %prep_rest.1 = (bf16[768,768]{1,0:T(8,128)(2,1)}, bf16[768,3072]{1,0:T(8,128)(2,1)}, bf16[3072,768]{1,0:T(8,128)(2,1)}) custom-call(s32[1]{0:T(128)} %bitcast.5.core_ref, bf16[384,768]{1,0:T(8,128)(2,1)} %out_a.1, bf16[384,768]{1,0:T(8,128)(2,1)} %copy-done.3, bf16[384,3072]{1,0:T(8,128)(2,1)} %up_a.1, bf16[384,3072]{1,0:T(8,128)(2,1)} %copy-done.2, ...), custom_call_target="tpu_custom_call" | custom-call | flops 18874368 | bytes 18874368 | tf_op jit(solution)/shard_map/prep_rest/pallas_call | solution.py:125
  37.3 49.9 %attend.1 = (bf16[4,512,2304]{2,1,0:T(8,128)(2,1)}, bf16[4,512,768]{2,1,0:T(8,128)(2,1)}, f32[4,16,512]{2,1,0:T(8,128)}, f32[4,512,768]{2,1,0:T(8,128)}, f32[4,512,1]{2,1,0:T(8,128)}) custom-call(bf16[4,512,768]{2,1,0:T(8,128)(2,1)} %tokens_ref.3, s32[4,1,512]{2,1,0:T(1,128)} %reshape.55.rows_ref, s32[4,512,1]{2,1,0:T(8,128)} %copy.31.cols_ref, ...), custom_call_target="tpu_custom_call" | custom-call | flops 22548578304 | bytes 47185920 | tf_op jit(solution)/shard_map/attend/pallas_call | solution.py:200
  87.2 38.2 %feed.1 = (bf16[4,512,768]{2,1,0:T(8,128)(2,1)}, bf16[4,512,768]{2,1,0:T(8,128)(2,1)}, bf16[4,512,3072]{2,1,0:T(8,128)(2,1)}, bf16[4,512,3072]{2,1,0:T(8,128)(2,...) custom-call(f32[4,512,768]{2,1,0:T(8,128)} %get-tuple-element.42.norm_ref, ...), custom_call_target="tpu_custom_call" | custom-call | flops 19327352832 | bytes 56623104 | tf_op jit(solution)/shard_map/feed/pallas_call | solution.py:291
  125.4 47.5 %feed_back.1 = (bf16[4,512,3072]{2,1,0:T(8,128)(2,1)}, bf16[3072,768]{1,0:T(8,128)(2,1)}, bf16[3072,768]{1,0:T(8,128)(2,1)}, f32[4,8,768]{2,1,0:T(8,128)}) custom-call(bf16[4,512,768]{2,1,0:T(8,128)(2,1)} %get-tuple-element.47.mixed_ref, bf16[4,512,768]{2,1,0:T(8,128)(2,1)} %get-tuple-element.48.first_ref, ...), custom_call_target="tpu_custom_call" | custom-call | flops 28991029248 | bytes 125829120 | tf_op jit(solution)/shard_map/feed_back/pallas_call | solution.py:355
  172.9 34.1 %norm_one_back.1 = (f32[4,512,768]{2,1,0:T(8,128)}, bf16[4,512,768]{2,1,0:T(8,128)(2,1)}, f32[4,16,512]{2,1,0:T(8,128)}, bf16[768,768]{1,0:T(8,128)(2,1)}, f32[8,768]{1,0:T(8,128)}) custom-call(f32[4,512,768]{2,1,0:T(8,128)} %get-tuple-element.46.second_ref, bf16[4,512,3072]{2,1,0:T(8,128)(2,1)} %get-tuple-element.51.pre_ref, ...), custom_call_target="tpu_custom_call" | custom-call | flops 14495514624 | bytes 62914560 | tf_op jit(solution)/shard_map/norm_one_back/pallas_call | solution.py:428
  207.0 57.2 %attend_back.1 = (bf16[4,512,2304]{2,1,0:T(8,128)(2,1)}, bf16[2304,768]{1,0:T(8,128)(2,1)}, f32[3,8,256]{2,1,0:T(8,128)}) custom-call(bf16[4,512,768]{2,1,0:T(8,128)(2,1)} %tokens_ref.3, s32[4,1,512]{2,1,0:T(1,128)} %reshape.55.rows_ref, s32[4,512,1]{2,1,0:T(8,128)} %copy.31.cols_ref, bf16[4,512,2304]{2,1,0:T(8,128)(2,1)} %get-tuple-element.55.q_ref.k_ref.v_ref, ...), custom_call_target="tpu_custom_call" | custom-call | flops 39460012032 | bytes 47185920 | tf_op jit(solution)/shard_map/attend_back/pallas_call | solution.py:542
  264.2 8.7 %reshape.59 = bf16[3,768,3,256]{3,2,1,0:T(4,128)(2,1)} reshape(bf16[2304,768]{1,0:T(8,128)(2,1)} %get-tuple-element.60) | data formatting | bytes 7077888 | tf_op jit(solution)/shard_map/reshape | solution.py:649
  272.9 6.5 %copy.33 = bf16[768,3,3,256]{0,3,2,1:T(8,128)(2,1)S(1)} copy(bf16[768,3,3,256]{3,1,0,2:T(4,128)(2,1)} %bitcast.34) | data formatting | bytes 7077888 | tf_op jit(solution)/shard_map/transpose | solution.py:649
  279.4 3.8 copy.38
  283.3 0.0 reduce-scatter.16.cloned.1.call-start
  283.3 0.7 reduce-scatter.16.cloned.1.call-update
  284.0 0.0 reduce-scatter.18.cloned.1.call-start
  284.1 10.4 %reshape.61 = bf16[4,768,2,384]{3,2,1,0:T(2,128)(2,1)} reshape(bf16[3072,768]{1,0:T(8,128)(2,1)} %get-tuple-element.62) | data formatting | bytes 9437184 | tf_op jit(solution)/shard_map/reshape | solution.py:651
  294.4 10.9 %copy.34 = bf16[768,2,4,384]{3,2,1,0:T(4,128)(2,1)} copy(bf16[768,2,4,384]{3,1,0,2:T(2,128)(2,1)} %bitcast.33) | data formatting | bytes 9437184 | tf_op jit(solution)/shard_map/transpose | solution.py:651
  305.3 8.8 %reshape.62 = bf16[768,3072]{1,0:T(8,128)(2,1)} reshape(bf16[768,2,4,384]{3,2,1,0:T(4,128)(2,1)} %copy.34) | data formatting | bytes 9437184 | tf_op jit(solution)/shard_map/reshape | solution.py:651
  314.1 0.0 reduce-scatter.20.cloned.1.call-start
  314.2 4.8 copy.35
  319.0 0.0 reduce-scatter.26.cloned.1.call-start
  319.1 0.7 copy-done.5
  319.8 0.8 copy.42
  320.7 0.0 reduce-scatter.28.cloned.1.call-start
  320.8 0.9 copy.44
  321.7 0.0 reduce-scatter.24.cloned.1.call-start
  321.7 0.8 copy.40
  322.6 0.0 all-reduce.5.cloned.1.call-start
  322.7 4.0 copy.39
  326.7 2.8 reduce-scatter.18.cloned.1.call-done
  329.5 16.6 %reduce-scatter.20.cloned.1.call-done = bf16[1536,768]{1,0:T(8,128)(2,1)} async-done(((bf16[3072,768]{1,0:T(8,128)(2,1)}), bf16[1536,768]{1,0:T(8,128)(2,1)}) %reduce-scatter.20.cloned.1.call-update) | async-done | bytes 2359312 | tf_op jit(solution)/shard_map/reduce_scatter | solution.py:658
  346.2 0.6 copy-done.9
  346.8 0.6 dynamic-slice
  348.0 0.9 fusion
  349.0 2.5 all-reduce
  351.5 0.1 dynamic-slice.1
  351.6 13.8 %token_back.1 = f32[4,512,768]{2,1,0:T(8,128)} custom-call(f32[4,512,768]{2,1,0:T(8,128)} %get-tuple-element.54.resid_ref, bf16[4,512,2304]{2,1,0:T(8,128)(2,1)} %get-tuple-element.59.jlow_ref, bf16[768,2304]{1,0:T(8,128)(2,1)} %get-tuple-element.39.qkv_ref), custom_call_target="tpu_custom_call" | custom-call | flops 7247757312 | bytes 25165824 | tf_op jit(solution)/shard_map/token_back/pallas_call | solution.py:588
  365.4 1.0 copy.43
  366.4 1.4 reduce-scatter.28.cloned.1.call-done
  367.8 1.0 copy.45
  368.8 10.6 %reduce-scatter.24.cloned.1.call-done = bf16[384,4]{1,0:T(8,128)(2,1)} async-done(((bf16[768,4]{1,0:T(8,128)(2,1)}), bf16[384,4]{1,0:T(8,128)(2,1)}) %reduce-scatter.24.cloned.1.call-update) | async-done | bytes 3088
  379.4 1.0 copy.41
  380.4 80.4 %all-reduce.1 = (bf16[384,4]{0,1:T(4,128)(2,1)S(1)}, bf16[1536]{0:T(1024)(128)(2,1)S(1)}, bf16[384,2]{0,1:T(2,128)(2,1)S(1)}, bf16[384,2]{0,1:T(2,128)(2,1)S(1)}) all-reduce(bf16[384,4]{0,1:T(4,128)(2,1)S(1)} %copy.41, bf16[1536]{0:T(1024)(128)(2,1)S(1)} %dynamic-slice.1, ...), channel_id=1, replica_groups=mesh['shard'=2,'rep'=16] {'rep'}, use_global_device_ids=true, to_apply=%region_9.0 | all-reduce | flops 4608 | bytes 18432 | tf_op jit(solution)/shard_map/psum | solution.py:659
  460.7 0.6 convert_element_type.41
  461.3 0.6 convert_element_type.46
  461.9 0.6 convert_element_type.47
  462.5 0.6 convert_element_type.45
  463.1 153.8 %all-reduce.5.cloned.1.call-done = (bf16[384,2304]{0,1:T(8,128)(2,1)}, bf16[384,768]{1,0:T(8,128)(2,1)}, bf16[384,3072]{1,0:T(8,128)(2,1)}, bf16[1536,768]{1,0:T(8,128)(2,1)}) async-done(((bf16[384,2304]{0,1:T(8,128)(2,1)}, bf16[384,768]{1,0:T(8,128)(2,1)}, bf16[384,3072]{1,0:T(8,128)(2,1)}, bf16[1536,768]{1,0:T(8,128)(2,1)}), (bf16[384,2304]{0,1:T(8,128)(2,1)}, bf16[384,768]{1,0:T(8,128)(2,1)}, ...) | async-done | bytes 7077904 | tf_op jit(solution)/shard_map/psum | solution.py:659
  616.9 2.3 convert_element_type.38
  619.2 4.0 copy.37
  623.2 2.8 convert_element_type.39
  626.0 2.5 convert_element_type.40
  (40 shorter events, 0.3 us)
Async XLA Ops:
  7.2 315.5 %reduce-scatter.22.cloned.1.call-start = ((), (), s32[]{:S(2)}) async-start(), calls=%async_computation.10 | async-start | bytes 5308416
  7.2 16.9 %collective-permute-start.3 = (bf16[384,3072]{1,0:T(8,128)(2,1)}, bf16[384,3072]{1,0:T(8,128)(2,1)S(1)}, u32[]{:S(2)}, u32[]{:S(2)}) collective-permute-start(bf16[384,3072]{1,0:T(8,128)(2,1)} %up_a.1), channel_id=1, source_target_pairs={{0,16},{16,0},{1,17},{17,1},{2,18},{18,2},{3,19},{19,3},{4,20},{20... | collective-permute-start | bytes 7077896 | tf_op jit(solution)/shard_map/ppermute | solution.py:617
  7.7 16.4 %collective-permute-start.4 = (bf16[1536,768]{1,0:T(8,128)(2,1)}, bf16[1536,768]{1,0:T(8,128)(2,1)}, u32[]{:S(2)}, u32[]{:S(2)}) collective-permute-start(bf16[1536,768]{1,0:T(8,128)(2,1)} %dn_a.1), channel_id=1, source_target_pairs={{0,16},{16,0},{1,17},{17,1},{2,18},{18,2},{3,19},{19,3},{4,20},{20... | collective-permute-start | bytes 7077896 | tf_op jit(solution)/shard_map/ppermute | solution.py:617
  7.8 11.2 %collective-permute-start = (bf16[384,2304]{1,0:T(8,128)(2,1)}, bf16[384,2304]{1,0:T(8,128)(2,1)}, u32[]{:S(2)}, u32[]{:S(2)}) collective-permute-start(bf16[384,2304]{1,0:T(8,128)(2,1)} %own_ref.1), channel_id=1, source_target_pairs={{0,16},{16,0},{1,17},{17,1},{2,18},{18,2},{3,19},{19,3},{4,20},{20... | collective-permute-start | bytes 5308424 | tf_op jit(solution)/shard_map/ppermute | solution.py:617
  8.3 15.9 %collective-permute-start.2 = (bf16[384,768]{1,0:T(8,128)(2,1)}, bf16[384,768]{1,0:T(8,128)(2,1)S(1)}, u32[]{:S(2)}, u32[]{:S(2)}) collective-permute-start(bf16[384,768]{1,0:T(8,128)(2,1)} %out_a.1), channel_id=1, source_target_pairs={{0,16},{16,0},{1,17},{17,1},{2,18},{18,2},{3,19},{19,3},{4,20},{20... | collective-permute-start | bytes 1769480 | tf_op jit(solution)/shard_map/ppermute | solution.py:617
  9.8 9.2 %copy-start.4 = (bf16[12,384]{1,0:T(8,128)(2,1)}, bf16[12,384]{1,0:T(8,128)(2,1)S(1)}, u32[]{:S(2)}) copy-start(bf16[12,384]{1,0:T(8,128)(2,1)S(1)} %pad_maximum_fusion.small_own_ref) | copy-start | bytes 27652
  9.8 4.7 collective-permute-start.1
  14.5 4.5 copy-start.8
  24.2 0.8 copy-start.3
  24.2 1.6 copy-start.2
  283.3 43.4 %reduce-scatter.16.cloned.1.call-start = ((), (), s32[]{:S(2)}) async-start(), calls=%async_computation.7 | async-start | bytes 1769472 | tf_op jit(solution)/shard_map/reduce_scatter | solution.py:658
  284.0 45.5 %reduce-scatter.18.cloned.1.call-start = ((), (), s32[]{:S(2)}) async-start(), calls=%async_computation.8 | async-start | bytes 7077888 | tf_op jit(solution)/shard_map/reduce_scatter | solution.py:658
  314.1 32.0 %reduce-scatter.20.cloned.1.call-start = ((), (), s32[]{:S(2)}) async-start(), calls=%async_computation.9 | async-start | bytes 7077888 | tf_op jit(solution)/shard_map/reduce_scatter | solution.py:658
  319.0 0.7 copy-start.5
  319.0 0.8 copy-start.7
  319.0 1.6 copy-start.6
  319.0 46.4 %reduce-scatter.26.cloned.1.call-start = ((), (), s32[]{:S(2)}) async-start(), calls=%async_computation.12 | async-start | bytes 294912
  320.7 47.1 %reduce-scatter.28.cloned.1.call-start = ((), (), s32[]{:S(2)}) async-start(), calls=%async_computation.13 | async-start | bytes 294912
  321.7 57.7 %reduce-scatter.24.cloned.1.call-start = ((), (), s32[]{:S(2)}) async-start(), calls=%async_computation.11 | async-start | bytes 294912
  322.6 294.3 %all-reduce.5.cloned.1.call-start = ((), (), s32[]{:S(2)}) async-start(), calls=%async_computation.14 | async-start | bytes 14155776 | tf_op jit(solution)/shard_map/psum | solution.py:659
  346.1 0.7 copy-start.9
  616.9 6.3 copy-start.1
  623.2 2.8 copy-start
Sparse Core Ops, SparseCore 0:
  283.4 13.9 reduce-scatter.21
  299.8 9.8 reduce-scatter.15
  314.3 15.1 reduce-scatter.17
  332.3 13.7 reduce-scatter.19
  348.2 8.7 reduce-scatter.25
  359.0 8.7 reduce-scatter.27
  370.6 8.7 reduce-scatter.23
  385.8 231.0 all-reduce.4

commit v2 on v1

--- a/solution.py
+++ b/solution.py
@@ -37,6 +37,15 @@
 
 def cost(flops, nbytes, trans=0):
     return pl.CostEstimate(flops=int(flops), bytes_accessed=int(nbytes), transcendentals=int(trans))
+
+
+def deal(core, acc, mine_ref, theirs_ref, at=0):
+    half = acc.shape[0] // 2
+    wide = acc.shape[1] // 2
+    for ref, who in ((mine_ref, core), (theirs_ref, 1 - core)):
+        rows = pl.ds(pl.multiple_of(who * half, half), half)
+        ref[at, 0:half, :] = acc[rows, 0:wide].astype(BF)
+        ref[at, half : 2 * half, :] = acc[rows, wide : 2 * wide].astype(BF)
 
 
 def binary_halves(first, second):
@@ -318,8 +327,8 @@
 
 
 def feed_back_kernel(
-    mixed_ref, first_ref, hidden_ref, slope_ref, up_ref, dn_ref,
-    pre_ref, dgrad_ref, ugrad_ref, hsum_ref, dacc, uacc,
+    core_ref, mixed_ref, first_ref, hidden_ref, slope_ref, dn_ref,
+    pre_ref, mine_ref, theirs_ref, hsum_ref, dacc, uacc,
 ):
     tile = pl.program_id(1)
     mixed = mixed_ref[0]
@@ -344,47 +353,49 @@
 
     @pl.when(tile == pl.num_programs(1) - 1)
     def _():
-        dgrad_ref[...] = dacc[...].astype(BF)
-        ugrad_ref[...] = uacc[...].astype(BF)
-
-
-def feed_back(mixed, first_low, hidden, slope, up_bin, dn_bin):
+        deal(core_ref[0], dacc, mine_ref, theirs_ref, 0)
+        deal(core_ref[0], uacc, mine_ref, theirs_ref, 1)
+
+
+def feed_back(core, mixed, first_low, hidden, slope, dn_bin):
     seqs, length, width = mixed.shape
     units = hidden.shape[2]
     chunks = units // width
     return pl.pallas_call(
         feed_back_kernel,
-        grid=(chunks, seqs),
-        in_specs=[
-            pl.BlockSpec((1, length, width), lambda c, s: (s, 0, 0)),
-            pl.BlockSpec((1, length, width), lambda c, s: (s, 0, 0)),
-            pl.BlockSpec((1, length, width), lambda c, s: (s, 0, c)),
-            pl.BlockSpec((1, length, width), lambda c, s: (s, 0, c)),
-            pl.BlockSpec((width, width), lambda c, s: (0, c)),
-            pl.BlockSpec((width, width), lambda c, s: (c, 0)),
-        ],
-        out_specs=[
-            pl.BlockSpec((1, length, width), lambda c, s: (s, 0, c)),
-            pl.BlockSpec((width, width), lambda c, s: (c, 0)),
-            pl.BlockSpec((width, width), lambda c, s: (c, 0)),
-            pl.BlockSpec((1, 8, width), lambda c, s: (c, 0, 0)),
-        ],
+        grid_spec=pltpu.PrefetchScalarGridSpec(
+            num_scalar_prefetch=1,
+            grid=(chunks, seqs),
+            in_specs=[
+                pl.BlockSpec((1, length, width), lambda c, s, _: (s, 0, 0)),
+                pl.BlockSpec((1, length, width), lambda c, s, _: (s, 0, 0)),
+                pl.BlockSpec((1, length, width), lambda c, s, _: (s, 0, c)),
+                pl.BlockSpec((1, length, width), lambda c, s, _: (s, 0, c)),
+                pl.BlockSpec((width, width), lambda c, s, _: (c, 0)),
+            ],
+            out_specs=[
+                pl.BlockSpec((1, length, width), lambda c, s, _: (s, 0, c)),
+                pl.BlockSpec((2, width, width // 2), lambda c, s, _: (c, 0, 0)),
+                pl.BlockSpec((2, width, width // 2), lambda c, s, _: (c, 0, 0)),
+                pl.BlockSpec((1, 8, width), lambda c, s, _: (c, 0, 0)),
+            ],
+            scratch_shapes=[pltpu.VMEM((width, width), F32), pltpu.VMEM((width, width), F32)],
+        ),
         out_shape=[
             jax.ShapeDtypeStruct((seqs, length, units), BF),
-            jax.ShapeDtypeStruct((units, width), BF),
-            jax.ShapeDtypeStruct((units, width), BF),
+            jax.ShapeDtypeStruct((2 * chunks, width, width // 2), BF),
+            jax.ShapeDtypeStruct((2 * chunks, width, width // 2), BF),
             jax.ShapeDtypeStruct((chunks, 8, width), F32),
         ],
-        scratch_shapes=[pltpu.VMEM((width, width), F32), pltpu.VMEM((width, width), F32)],
         compiler_params=params(),
         cost_estimate=cost(6 * seqs * length * width * units, 20 * seqs * length * units),
         name="feed_back",
-    )(mixed, first_low, hidden, slope, up_bin, dn_bin)
+    )(core, mixed, first_low, hidden, slope, dn_bin)
 
 
 def norm_kernel(
-    second_ref, pre_ref, norm_ref, inv_ref, ctx_ref, up_ref, out_ref, small_ref,
-    resid_ref, cback_ref, rowdot_ref, ograd_ref, sums_ref, oacc,
+    core_ref, second_ref, pre_ref, norm_ref, inv_ref, ctx_ref, up_ref, out_ref, small_ref,
+    resid_ref, cback_ref, rowdot_ref, mine_ref, theirs_ref, sums_ref, oacc,
 ):
     s = pl.program_id(0)
     width = second_ref.shape[2]
@@ -419,14 +430,16 @@
 
     @pl.when(s == pl.num_programs(0) - 1)
     def _():
-        ograd_ref[...] = oacc[...].astype(BF)
-
-
-def norm_one_back(second, pre_low, norm, inv, ctx, up_bin, out_bin, small):
+        deal(core_ref[0], oacc, mine_ref, theirs_ref)
+
+
+def norm_one_back(core, second, pre_low, norm, inv, ctx, up_bin, out_bin, small):
     seqs, length, width = second.shape
-    per_seq = lambda *shape: pl.BlockSpec((1,) + shape, lambda s: (s,) + (0,) * len(shape))
+    per_seq = lambda *shape: pl.BlockSpec((1,) + shape, lambda s, _: (s,) + (0,) * len(shape))
     return pl.pallas_call(
         norm_kernel,
+        grid_spec=pltpu.PrefetchScalarGridSpec(
+        num_scalar_prefetch=1,
         grid=(seqs,),
         in_specs=[
             per_seq(length, width),
@@ -442,21 +455,24 @@
             per_seq(length, width),
             per_seq(length, width),
             per_seq(16, length),
-            full((width, width)),
+            full((1, width, width // 2)),
+            full((1, width, width // 2)),
             full((8, width)),
         ],
+        scratch_shapes=[pltpu.VMEM((width, width), F32)],
+        ),
         out_shape=[
             jax.ShapeDtypeStruct((seqs, length, width), F32),
             jax.ShapeDtypeStruct((seqs, length, width), BF),
             jax.ShapeDtypeStruct((seqs, 16, length), F32),
-            jax.ShapeDtypeStruct((width, width), BF),
+            jax.ShapeDtypeStruct((1, width, width // 2), BF),
+            jax.ShapeDtypeStruct((1, width, width // 2), BF),
             jax.ShapeDtypeStruct((8, width), F32),
         ],
-        scratch_shapes=[pltpu.VMEM((width, width), F32)],
         compiler_params=params(),
         cost_estimate=cost(2 * seqs * length * width * 6 * width, 40 * seqs * length * width),
         name="norm_one_back",
-    )(second, pre_low, norm, inv, ctx, up_bin, out_bin, small)
+    )(core, second, pre_low, norm, inv, ctx, up_bin, out_bin, small)
 
 
 GROUP = 256
@@ -464,8 +480,8 @@
 
 
 def attend_back_kernel(
-    tokens_ref, rows_ref, cols_ref, q_ref, k_ref, v_ref, cback_ref, lse_ref, rowdot_ref,
-    jlow_ref, grad_ref, sums_ref, acc, bias_ref,
+    core_ref, tokens_ref, rows_ref, cols_ref, q_ref, k_ref, v_ref, cback_ref, lse_ref, rowdot_ref,
+    jlow_ref, mine_ref, theirs_ref, sums_ref, acc, bias_ref,
 ):
     g, s = pl.program_id(0), pl.program_id(1)
     length = tokens_ref.shape[1]
@@ -529,18 +545,20 @@
 
     @pl.when(s == pl.num_programs(1) - 1)
     def _():
-        grad_ref[...] = acc[...].astype(BF)
-
-
-def attend_back(tokens, block_ids, joined, cback, lse, rowdot):
+        deal(core_ref[0], acc, mine_ref, theirs_ref)
+
+
+def attend_back(core, tokens, block_ids, joined, cback, lse, rowdot):
     seqs, length, width = tokens.shape
     rows = block_ids.reshape(seqs, 1, length)
     cols = block_ids.reshape(seqs, length, 1)
     groups = width // GROUP
-    whole = lambda *shape: pl.BlockSpec((1,) + shape, lambda g, s: (s,) + (0,) * len(shape))
-    part = lambda k: pl.BlockSpec((1, length, GROUP), lambda g, s: (s, 0, k * groups + g))
+    whole = lambda *shape: pl.BlockSpec((1,) + shape, lambda g, s, _: (s,) + (0,) * len(shape))
+    part = lambda k: pl.BlockSpec((1, length, GROUP), lambda g, s, _: (s, 0, k * groups + g))
     return pl.pallas_call(
         attend_back_kernel,
+        grid_spec=pltpu.PrefetchScalarGridSpec(
+        num_scalar_prefetch=1,
         grid=(groups, seqs),
         in_specs=[
             whole(length, width),
@@ -554,20 +572,23 @@
             whole(16, length),
         ],
         out_specs=[
-            pl.BlockSpec((1, length, 3 * GROUP), lambda g, s: (s, 0, g)),
-            pl.BlockSpec((width, 3 * GROUP), lambda g, s: (g, 0)),
-            pl.BlockSpec((1, 8, GROUP), lambda g, s: (g, 0, 0)),
-        ],
+            pl.BlockSpec((1, length, 3 * GROUP), lambda g, s, _: (s, 0, g)),
+            pl.BlockSpec((1, width, width // 2), lambda g, s, _: (g, 0, 0)),
+            pl.BlockSpec((1, width, width // 2), lambda g, s, _: (g, 0, 0)),
+            pl.BlockSpec((1, 8, GROUP), lambda g, s, _: (g, 0, 0)),
+        ],
+        scratch_shapes=[pltpu.VMEM((width, 3 * GROUP), F32), pltpu.VMEM((length, length), F32)],
+        ),
         out_shape=[
             jax.ShapeDtypeStruct((seqs, length, 3 * width), BF),
-            jax.ShapeDtypeStruct((groups * width, 3 * GROUP), BF),
+            jax.ShapeDtypeStruct((groups, width, width // 2), BF),
+            jax.ShapeDtypeStruct((groups, width, width // 2), BF),
             jax.ShapeDtypeStruct((groups, 8, GROUP), F32),
         ],
-        scratch_shapes=[pltpu.VMEM((width, 3 * GROUP), F32), pltpu.VMEM((length, length), F32)],
         compiler_params=params(),
         cost_estimate=cost(seqs * length * width * (6 * width + 40 * length), 30 * seqs * length * width),
         name="attend_back",
-    )(tokens, rows, cols, joined, joined, joined, cback, lse, rowdot)
+    )(core, tokens, rows, cols, joined, joined, joined, cback, lse, rowdot)
 
 
 def token_kernel(resid_ref, jlow_ref, qkv_ref, grad_ref):
@@ -602,15 +623,289 @@
     out_bin, up_bin, dn_bin = prep_rest(core, own[1], other[1], own[2], other[2], own[3], other[3])
     joined, ctx, lse, norm, inv = attend(tokens, block_ids, qkv_bin, out_bin, small)
     final, first_low, hidden, slope, second, mixed, sums_two = feed(norm, teacher, small, up_bin, dn_bin)
-    pre_low, dgrad, ugrad, hsum = feed_back(mixed, first_low, hidden, slope, up_bin, dn_bin)
-    resid, cback, rowdot, ograd, sums_one = norm_one_back(second, pre_low, norm, inv, ctx, up_bin, out_bin, small)
-    jlow, qgrad, sums_qv = attend_back(tokens, block_ids, joined, cback, lse, rowdot)
+    pre_low, *feed_grads, hsum = feed_back(core, mixed, first_low, hidden, slope, dn_bin)
+    resid, cback, rowdot, *out_grads, sums_one = norm_one_back(
+        core, second, pre_low, norm, inv, ctx, up_bin, out_bin, small
+    )
+    jlow, *qkv_grads, sums_qv = attend_back(core, tokens, block_ids, joined, cback, lse, rowdot)
     token_grad = token_back(resid, jlow, qkv_bin)
-    return final, token_grad, dgrad, ugrad, ograd, qgrad, sums_two, hsum, sums_one, sums_qv
-
-
-def as_sent(value):
-    return jax.tree.map(lambda a: a.astype(BF), value)
+    sums = jnp.concatenate(
+        [
+            sums_qv[:, 0].reshape(1, -1), sums_qv[:, 1].reshape(1, -1), sums_one[2:3], sums_two[2:3],
+            sums_one[0:1], sums_two[0:1], sums_one[1:2], sums_two[1:2], hsum[:, 0],
+        ],
+        axis=0,
+    )
+    return final, token_grad, feed_grads, out_grads, qkv_grads, sums
+
+
+MESH = pl.DeviceIdType.MESH
+
+
+def reduce_kernel(
+    feed_mine, feed_theirs, out_mine, out_theirs, qkv_mine, qkv_theirs, sums_ref,
+    result_ref, total_ref,
+    held, from_core, from_one, from_two, from_line, kept, came,
+    local_sem, core_send, core_recv, one_send, one_recv, two_send, two_recv, line_send, line_recv,
+    line_back_send, line_back_recv, two_back_send, two_back_recv, one_back_send, one_back_recv,
+    small_send, small_recv, done_sem,
+):
+    core, rep = lax.axis_index("shard"), lax.axis_index("rep")
+    x, y, z = rep % 2, (rep // 2) % 2, rep // 4
+    units, rows = held.shape[0], held.shape[1]
+    half, quarter, piece = rows // 2, rows // 4, rows // 16
+    partner_x, partner_y = rep + 1 - 2 * x, rep + 2 - 4 * y
+    sibling = {"shard": 1 - core}
+
+    def along(step):
+        return {"rep": rep % 4 + 4 * ((z + step) % 4)}
+
+    barrier = pltpu.get_barrier_semaphore()
+    peers = [sibling, {"rep": partner_x}, {"rep": partner_y}, along(1), along(2), along(3)]
+    for peer in peers:
+        pl.semaphore_signal(barrier, inc=1, device_id=peer, device_id_type=MESH)
+    pl.semaphore_wait(barrier, len(peers))
+
+    def send(src, dst, send_sem, recv_sem, peer):
+        return pltpu.make_async_remote_copy(
+            src_ref=src, dst_ref=dst, send_sem=send_sem, recv_sem=recv_sem, device_id=peer, device_id_type=MESH
+        )
+
+    sources = [(feed_mine, feed_theirs)] * feed_mine.shape[0]
+    places = list(range(feed_mine.shape[0]))
+    sources += [(out_mine, out_theirs)] + [(qkv_mine, qkv_theirs)] * qkv_mine.shape[0]
+    places += [0] + list(range(qkv_mine.shape[0]))
+
+    for u in range(units):
+        mine, theirs = sources[u]
+        send(theirs.at[places[u]], from_core.at[u], core_send.at[u], core_recv.at[u], sibling).start()
+        pltpu.make_async_copy(mine.at[places[u]], held.at[u], local_sem.at[u]).start()
+
+    def where(u):
+        odd = u % 2
+        bit_one = x + odd * (y - x)
+        bit_two = y + odd * (x - y)
+        peer_one = {"rep": partner_x + odd * (partner_y - partner_x)}
+        peer_two = {"rep": partner_y + odd * (partner_x - partner_y)}
+        base_one = bit_one * half
+        base_two = base_one + bit_two * quarter
+        return bit_one, bit_two, peer_one, peer_two, base_one, base_two
+
+    def block(at, size):
+        return pl.ds(pl.multiple_of(at, piece), size)
+
+    def add(u, at, size, other):
+        here = block(at, size)
+        held[u, here, :] = (held[u, here, :].astype(F32) + other.astype(F32)).astype(BF)
+
+    def copy_core(u):
+        return send(from_core.at[u], from_core.at[u], core_send.at[u], core_recv.at[u], sibling)
+
+    def copy_one(u):
+        bit_one, _, peer_one, _, _, _ = where(u)
+        away = block((1 - bit_one) * half, half)
+        return send(held.at[u, away], from_one.at[u], one_send.at[u], one_recv.at[u], peer_one)
+
+    def copy_two(u):
+        _, bit_two, _, peer_two, base_one, _ = where(u)
+        away = block(base_one + (1 - bit_two) * quarter, quarter)
+        return send(held.at[u, away], from_two.at[u], two_send.at[u], two_recv.at[u], peer_two)
+
+    def copy_line(u, d):
+        base_two = where(u)[5]
+        away = block(base_two + ((z + d) % 4) * piece, piece)
+        return send(held.at[u, away], from_line.at[u, d - 1], line_send.at[u, d - 1], line_recv.at[u, d - 1], along(d))
+
+    def copy_line_back(u, d):
+        base_two = where(u)[5]
+        mine = from_core.at[u, block(base_two + z * piece, piece)]
+        return send(mine, mine, line_back_send.at[u, d - 1], line_back_recv.at[u, d - 1], along(d))
+
+    def copy_two_back(u):
+        _, _, _, peer_two, _, base_two = where(u)
+        mine = from_core.at[u, block(base_two, quarter)]
+        return send(mine, mine, two_back_send.at[u], two_back_recv.at[u], peer_two)
+
+    def copy_one_back(u):
+        _, _, peer_one, _, base_one, _ = where(u)
+        mine = from_core.at[u, block(base_one, half)]
+        return send(mine, mine, one_back_send.at[u], one_back_recv.at[u], peer_one)
+
+    def copy_done(u):
+        return pltpu.make_async_copy(from_core.at[u], result_ref.at[u], done_sem.at[u])
+
+    def stage_one(u):
+        pltpu.make_async_copy(feed_mine.at[0], held.at[u], local_sem.at[u]).wait()
+        copy_core(u).wait_recv()
+        base_one = where(u)[4]
+        away = half - base_one
+        add(u, away, half, from_core[u, block(away, half), :])
+        copy_one(u).start()
+        add(u, base_one, half, from_core[u, block(base_one, half), :])
+
+    def stage_two(u):
+        copy_one(u).wait_recv()
+        _, bit_two, _, _, base_one, base_two = where(u)
+        off = (1 - bit_two) * quarter
+        add(u, base_one + off, quarter, from_one[u, block(off, quarter), :])
+        copy_two(u).start()
+        add(u, base_two, quarter, from_one[u, block(bit_two * quarter, quarter), :])
+
+    def stage_three(u):
+        copy_two(u).wait_recv()
+        base_two = where(u)[5]
+        add(u, base_two, quarter, from_two[u])
+        for d in (2, 1, 3):
+            copy_line(u, d).start()
+
+    def stage_four(u):
+        for d in (1, 2, 3):
+            copy_line(u, d).wait_recv()
+        base_two = where(u)[5]
+        here = block(base_two + z * piece, piece)
+        total = held[u, here, :].astype(F32) + from_line[u, 0].astype(F32)
+        total = total + from_line[u, 1].astype(F32) + from_line[u, 2].astype(F32)
+        from_core[u, here, :] = total.astype(BF)
+        for d in (2, 1, 3):
+            copy_line_back(u, d).start()
+
+    def stage_five(u):
+        for d in (1, 2, 3):
+            copy_line_back(u, d).wait_recv()
+        copy_two_back(u).start()
+
+    def stage_six(u):
+        copy_two_back(u).wait_recv()
+        copy_one_back(u).start()
+
+    def stage_seven(u):
+        copy_one_back(u).wait_recv()
+        copy_done(u).start()
+
+    stages = (stage_one, stage_two, stage_three, stage_four, stage_five, stage_six, stage_seven)
+
+    kept[0] = sums_ref[...]
+    small_peers = [
+        sibling, {"rep": partner_x}, {"rep": partner_y},
+        {"rep": rep + 4 - 8 * (z % 2)}, {"rep": rep + 8 - 16 * (z // 2)},
+    ]
+
+    def copy_small(k):
+        return send(kept.at[k], came.at[k], small_send.at[k], small_recv.at[k], small_peers[k])
+
+    def tick(t, _):
+        for k in reversed(range(len(stages))):
+            u = t - k
+
+            @pl.when((u >= 0) & (u < units))
+            def _():
+                stages[k](u)
+
+        return 0
+
+    copy_small(0).start()
+    for k in range(len(small_peers)):
+        tick(k, 0)
+        copy_small(k).wait_recv()
+        kept[k + 1] = kept[k] + came[k]
+        if k + 1 < len(small_peers):
+            copy_small(k + 1).start()
+    lax.fori_loop(len(small_peers), units + len(stages) - 1, tick, 0)
+    total_ref[...] = kept[len(small_peers)]
+
+    for k in range(len(small_peers)):
+        copy_small(k).wait_send()
+
+    def finish(u, _):
+        copy_core(u).wait_send()
+        copy_one(u).wait_send()
+        copy_two(u).wait_send()
+        for d in (1, 2, 3):
+            copy_line(u, d).wait_send()
+            copy_line_back(u, d).wait_send()
+        copy_two_back(u).wait_send()
+        copy_one_back(u).wait_send()
+        copy_done(u).wait()
+        return 0
+
+    lax.fori_loop(0, units, finish, 0)
+
+
+def reduce_all(feed_grads, out_grads, qkv_grads, sums):
+    rows, cols = out_grads[0].shape[1:]
+    units = feed_grads[0].shape[0] + out_grads[0].shape[0] + qkv_grads[0].shape[0]
+    anywhere = pl.BlockSpec(memory_space=pl.ANY)
+    vm = pl.BlockSpec(memory_space=pltpu.VMEM)
+    dma = pltpu.SemaphoreType.DMA
+    return pl.pallas_call(
+        reduce_kernel,
+        in_specs=[anywhere] * 6 + [vm],
+        out_specs=[anywhere, vm],
+        out_shape=[
+            jax.ShapeDtypeStruct((units, rows, cols), BF),
+            jax.ShapeDtypeStruct(sums.shape, F32),
+        ],
+        scratch_shapes=[
+            pltpu.VMEM((units, rows, cols), BF),
+            pltpu.VMEM((units, rows, cols), BF),
+            pltpu.VMEM((units, rows // 2, cols), BF),
+            pltpu.VMEM((units, rows // 4, cols), BF),
+            pltpu.VMEM((units, 3, rows // 16, cols), BF),
+            pltpu.VMEM((6,) + sums.shape, F32),
+            pltpu.VMEM((5,) + sums.shape, F32),
+            dma((units,)), dma((units,)), dma((units,)), dma((units,)), dma((units,)), dma((units,)), dma((units,)),
+            dma((units, 3)), dma((units, 3)), dma((units, 3)), dma((units, 3)),
+            dma((units,)), dma((units,)), dma((units,)), dma((units,)),
+            dma((5,)), dma((5,)), dma((units,)),
+        ],
+        compiler_params=params(collective_id=0, has_side_effects=True),
+        cost_estimate=cost(0, 4 * units * rows * cols),
+        name="reduce_all",
+    )(*feed_grads, *out_grads, *qkv_grads, sums)
+
+
+def finish_kernel(core_ref, units_ref, sums_ref, qkv_ref, out_ref, up_ref, dn_ref, small_ref):
+    units, rows, half = units_ref.shape
+    groups = rows // GROUP
+    chunks = (units - 1 - groups) // 2
+    wide = [slice(0, rows // 2), slice(rows // 2, rows)]
+    for c in range(chunks):
+        for p in range(2):
+            dn_ref[c * half : (c + 1) * half, p * half : (p + 1) * half] = units_ref[2 * c, wide[p], :].astype(F32)
+            at = p * chunks * half + c * half
+            up_ref[:, at : at + half] = units_ref[2 * c + 1, wide[p], :].astype(F32)
+    for p in range(2):
+        out_ref[:, p * half : (p + 1) * half] = units_ref[2 * chunks, wide[p], :].astype(F32)
+    for g in range(groups):
+        for j in range(3 * GROUP // 128):
+            col = j * 128
+            at = (col // GROUP) * rows + g * GROUP + col % GROUP
+            qkv_ref[:, at : at + 128] = units_ref[
+                2 * chunks + 1 + g, wide[col // half], col % half : col % half + 128
+            ].astype(F32)
+    mine = pl.ds(pl.multiple_of(core_ref[0] * half, half), half)
+    small_ref[...] = sums_ref[:, mine]
+
+
+def finish(core, units, sums):
+    count, rows, half = units.shape
+    groups = rows // GROUP
+    hidden = (count - 1 - groups) // 2 * rows
+    vm = pl.BlockSpec(memory_space=pltpu.VMEM)
+    return pl.pallas_call(
+        finish_kernel,
+        in_specs=[pl.BlockSpec(memory_space=pltpu.SMEM), vm, vm],
+        out_specs=[vm] * 5,
+        out_shape=[
+            jax.ShapeDtypeStruct((half, 3 * rows), F32),
+            jax.ShapeDtypeStruct((half, rows), F32),
+            jax.ShapeDtypeStruct((half, hidden), F32),
+            jax.ShapeDtypeStruct((hidden // 2, rows), F32),
+            jax.ShapeDtypeStruct((sums.shape[0], half), F32),
+        ],
+        compiler_params=params(),
+        name="finish",
+    )(core, units, sums)
 
 
 def swap(value):
@@ -622,10 +917,33 @@
     return jnp.concatenate([biases.T, gain.T, shift.T, hidden_bias.reshape(-1, rows)], axis=0)
 
 
+def reduce_plain(feed_grads, out_grads, qkv_grads, sums):
+    def whole(mine, theirs):
+        count, rows, half = mine.shape
+        cut = lambda a: a.reshape(count, 2, half, half).transpose(0, 2, 1, 3).reshape(count, half, rows)
+        return jnp.concatenate([cut(mine), cut(theirs)], axis=1)
+
+    feed_all, out_all, qkv_all = whole(*feed_grads), whole(*out_grads), whole(*qkv_grads)
+    chunks, groups, width = feed_all.shape[0] // 2, qkv_all.shape[0], feed_all.shape[2]
+    half, units = width // 2, chunks * width
+    grads = (
+        qkv_all.reshape(groups, width, 3, GROUP).transpose(1, 2, 0, 3).reshape(width, 3 * width),
+        out_all[0],
+        feed_all[1::2].reshape(chunks, width, 2, half).transpose(1, 2, 0, 3).reshape(width, units),
+        feed_all[0::2].reshape(chunks, 2, half, width).transpose(1, 0, 2, 3).reshape(units, width),
+        sums[0:4].T.astype(BF),
+        sums[8:].reshape(chunks, 2, half).transpose(1, 0, 2).reshape(-1).astype(BF),
+        sums[4:6].T.astype(BF),
+        sums[6:8].T.astype(BF),
+    )
+    owned = lax.psum_scatter(grads, "shard", scatter_dimension=0, tiled=True)
+    return jax.tree.map(lambda part: part.astype(F32), lax.psum(owned, "rep"))
+
+
 def body(tokens, teacher, block_ids, *weights):
     qkv, out, up, down, biases, hidden_bias, gain, shift = weights
-    shards = lax.axis_size("shard")
-    if shards == 2:
+    paired = lax.axis_size("shard") == 2 and lax.axis_size("rep") == 16
+    if paired:
         core = lax.axis_index("shard").reshape(1)
         own = (qkv, out, up, down)
         small_own = small_rows(biases, gain, shift, hidden_bias)
@@ -636,28 +954,17 @@
         gathered = [lax.all_gather(w, "shard", axis=0, tiled=True) for w in weights]
         cut = [jnp.split(w, 2, axis=0) for w in gathered]
         own, other = (tuple(c[i] for c in cut[:4]) for i in range(2))
-        small_own, small_other = (
-            small_rows(cut[4][i], cut[6][i], cut[7][i], cut[5][i]) for i in range(2)
-        )
-    final, token_grad, dgrad, ugrad, ograd, qgrad, sums_two, hsum, sums_one, sums_qv = layer(
-        core, tokens, teacher, block_ids, own, other, small_own, small_other
+        small_own, small_other = (small_rows(cut[4][i], cut[6][i], cut[7][i], cut[5][i]) for i in range(2))
+    final, token_grad, *grads, sums = layer(core, tokens, teacher, block_ids, own, other, small_own, small_other)
+    if not paired:
+        return (final, token_grad) + tuple(reduce_plain(*grads, sums))
+    sums = jnp.concatenate([sums, jnp.zeros((16 - sums.shape[0], sums.shape[1]), F32)], axis=0)
+    qkv_grad, out_grad, up_grad, dn_grad, small = finish(core, *reduce_all(*grads, sums))
+    hidden_rows = hidden_bias.shape[0] // small.shape[1]
+    return (
+        final, token_grad, qkv_grad, out_grad, up_grad, dn_grad,
+        small[0:4].T, small[8 : 8 + hidden_rows].reshape(-1), small[4:6].T, small[6:8].T,
     )
-    width, units = ograd.shape[0], dgrad.shape[0]
-    chunks, half = units // width, width // 2
-    groups = width // GROUP
-    grads = (
-        qgrad.reshape(groups, width, 3, GROUP).transpose(1, 2, 0, 3).reshape(width, 3 * width),
-        ograd,
-        ugrad.reshape(chunks, width, 2, half).transpose(1, 2, 0, 3).reshape(width, units),
-        dgrad.reshape(chunks, 2, half, width).transpose(1, 0, 2, 3).reshape(units, width),
-        jnp.stack([sums_qv[:, 0].reshape(-1), sums_qv[:, 1].reshape(-1), sums_one[2], sums_two[2]], axis=1),
-        hsum[:, 0].reshape(chunks, 2, half).transpose(1, 0, 2).reshape(-1),
-        jnp.stack([sums_one[0], sums_two[0]], axis=1),
-        jnp.stack([sums_one[1], sums_two[1]], axis=1),
-    )
-    owned = lax.psum_scatter(as_sent(grads), "shard", scatter_dimension=0, tiled=True)
-    summed = jax.tree.map(lambda part: part.astype(F32), lax.psum(owned, "rep"))
-    return (final, token_grad) + tuple(summed)
 
 
 def solution(mesh):

time: 641 us -> 471 us (0.73)
  Pallas kernels: 257 us -> 445 us
  waiting for transfers between devices: 192 us -> 5.4 us
  blocking collectives: 82.9 us -> 0 us
  local copies, waits for them, and re-layouts: 76 us -> 12 us
  between operations: 15.1 us -> 1.25 us
  other arithmetic: 10.8 us -> 0.73 us
    pallas_call x3 -> x5, Pallas kernels: 139 us -> 326 us  [the longest x1 179 us: reduce_all(): pl.pallas_call(reduce_kernel, in_specs=[anywhere] * 6 + [vm], out_specs=[...]
    psum x1 -> x0, waiting for transfers between devices: 154 us -> none  [body(): summed = jax.tree.map(lambda part: part.astype(F32), lax.psum(owned, 'rep'))]
    psum x1 -> x0, blocking collectives: 80.4 us -> none  [body(): summed = jax.tree.map(lambda part: part.astype(F32), lax.psum(owned, 'rep'))]
    reshape x3 -> x1, local copies, waits for them, and re-layouts: 27.9 us -> 0.61 us  [body(): small[8:8 + hidden_rows].reshape(-1)]
    transpose x3 -> x1, local copies, waits for them, and re-layouts: 22.2 us -> 1.37 us  [body(): small[6:8]]
    reduce_scatter x3 -> x0, waiting for transfers between devices: 19.5 us -> none  [body(): lax.psum_scatter(as_sent(grads), 'shard', scatter_dimension=0, tiled=True)]
    unnamed x31 -> x10, local copies, waits for them, and re-layouts: 20.8 us -> 1.58 us
    unnamed x12 -> x0, waiting for transfers between devices: 12.9 us -> none
  transfers between devices with their start and end apart: 13 -> 5, of which waited for: 7 -> 2; matrix products, arithmetic and copies ran while one was open for 8% -> 1% of each run, Pallas kernels for 3% -> 1%
where the time goes in v2:
time: 471 us; the launch traced here: 466 us
  Pallas kernels  445 us (94%)
  local copies, waits for them, and re-layouts  12 us (3%)
  waiting for transfers between devices  5.4 us (1%)
    pallas_call x1, Pallas kernels, reduce_all(): pl.pallas_call(reduce_kernel, in_specs=[anywhere] * 6 + [vm], out_specs=[...  179 us
    pallas_call x1, Pallas kernels, attend_back(): pl.pallas_call(attend_back_kernel, grid_spec=pltpu.PrefetchScalarGridSpec...  57.3 us
    pallas_call x1, Pallas kernels, attend(): pl.pallas_call(attend_kernel, grid=(seqs,), in_specs=[per_seq(length, wid...  49.9 us
    pallas_call x1, Pallas kernels, feed_back(): pl.pallas_call(feed_back_kernel, grid_spec=pltpu.PrefetchScalarGridSpec(n...  47.2 us
    pallas_call x1, Pallas kernels, feed(): pl.pallas_call(feed_kernel, grid=(seqs,), in_specs=[per_seq(length, width...  38.2 us
    pallas_call x1, Pallas kernels, norm_one_back(): pl.pallas_call(norm_kernel, grid_spec=pltpu.PrefetchScalarGridSpec(num_sc...  33.9 us
    pallas_call x1, Pallas kernels, token_back(): pl.pallas_call(token_kernel, grid=(seqs,), in_specs=[per_seq(length, widt...  13.8 us
    pallas_call x1, Pallas kernels, prep_rest(): pl.pallas_call(prep_rest_kernel, in_specs=[pl.BlockSpec(memory_space=pltp...  11.5 us
  transfers between devices with their start and end apart: 5, of which 2 were waited for; matrix products, arithmetic and copies ran while one was open for 1% of the time, Pallas kernels for 1%

profile of v2, /device:TPU:0, one launch (start us, length us, event | category | flops | bytes accessed | tf_op | source)
XLA Modules:
  0.0 465.9 jit_solution(18401206311397349991)
XLA Ops:
  0.6 0.5 collective-permute-start.3
  1.2 0.1 collective-permute-start.4
  1.2 0.4 collective-permute-start
  1.7 0.1 collective-permute-start.2
  1.8 0.7 reshape.40
  2.5 0.7 pad_maximum_fusion.small_own_ref
  3.2 0.0 copy-start.3
  3.2 0.5 collective-permute-start.1
  3.7 1.3 reshape.37.rows_ref
  5.0 2.0 copy.22.cols_ref
  7.0 0.9 collective-permute-done.1.small_other_ref
  7.9 0.0 copy-start.4
  7.9 4.5 collective-permute-done.other_ref
  12.4 0.0 copy-done.3
  12.4 0.0 copy-done.4
  12.4 5.2 %prep_qkv.1 = (bf16[768,2304]{1,0:T(8,128)(2,1)}, f32[12,768]{1,0:T(8,128)}) custom-call(s32[1]{0:T(128)} %bitcast.1.core_ref, bf16[384,2304]{1,0:T(8,128)(2,1)} %own_ref.1, bf16[384,2304]{1,0:T(8,128)(2,1)} %collective-permute-done.other_ref, bf16[12,384]{1,0:T(8,128)(2,1)} %copy-done.3, bf16[12,384]{1,0:T(8,128)(2,1)} %copy-done.4), custom_call_target="tpu_custom_call" | custom-call | flops 7077888 | bytes 7077888 | tf_op jit(solution)/shard_map/prep_qkv/pallas_call | solution.py:82
  17.7 0.0 collective-permute-done.2.out_b
  17.7 0.0 copy-start.1
  17.7 0.0 collective-permute-done.3.up_b
  17.7 0.0 copy-start
  17.7 0.0 collective-permute-done.4.dn_b
  17.7 0.8 copy-done.1
  18.5 0.8 copy-done
  19.3 11.5 %prep_rest.1 = (bf16[768,768]{1,0:T(8,128)(2,1)}, bf16[768,3072]{1,0:T(8,128)(2,1)}, bf16[3072,768]{1,0:T(8,128)(2,1)}) custom-call(s32[1]{0:T(128)} %bitcast.1.core_ref, bf16[384,768]{1,0:T(8,128)(2,1)} %out_a.1, bf16[384,768]{1,0:T(8,128)(2,1)} %copy-done.1, bf16[384,3072]{1,0:T(8,128)(2,1)} %up_a.1, bf16[384,3072]{1,0:T(8,128)(2,1)} %copy-done, ...), custom_call_target="tpu_custom_call" | custom-call | flops 18874368 | bytes 18874368 | tf_op jit(solution)/shard_map/prep_rest/pallas_call | solution.py:134
  30.8 49.9 %attend.1 = (bf16[4,512,2304]{2,1,0:T(8,128)(2,1)}, bf16[4,512,768]{2,1,0:T(8,128)(2,1)}, f32[4,16,512]{2,1,0:T(8,128)}, f32[4,512,768]{2,1,0:T(8,128)}, f32[4,512,1]{2,1,0:T(8,128)}) custom-call(bf16[4,512,768]{2,1,0:T(8,128)(2,1)} %tokens_ref.3, s32[4,1,512]{2,1,0:T(1,128)} %reshape.37.rows_ref, s32[4,512,1]{2,1,0:T(8,128)} %copy.22.cols_ref, ...), custom_call_target="tpu_custom_call" | custom-call | flops 22548578304 | bytes 47185920 | tf_op jit(solution)/shard_map/attend/pallas_call | solution.py:209
  80.7 38.2 %feed.1 = (bf16[4,512,768]{2,1,0:T(8,128)(2,1)}, bf16[4,512,768]{2,1,0:T(8,128)(2,1)}, bf16[4,512,3072]{2,1,0:T(8,128)(2,1)}, bf16[4,512,3072]{2,1,0:T(8,128)(2,...) custom-call(f32[4,512,768]{2,1,0:T(8,128)} %get-tuple-element.51.norm_ref, ...), custom_call_target="tpu_custom_call" | custom-call | flops 19327352832 | bytes 56623104 | tf_op jit(solution)/shard_map/feed/pallas_call | solution.py:300
  118.9 47.2 %feed_back.1 = (bf16[4,512,3072]{2,1,0:T(8,128)(2,1)}, bf16[8,768,384]{2,1,0:T(8,128)(2,1)}, bf16[8,768,384]{2,1,0:T(8,128)(2,1)}, f32[4,8,768]{2,1,0:T(8,128)}) custom-call(s32[1]{0:T(128)} %bitcast.1.core_ref, bf16[4,512,768]{2,1,0:T(8,128)(2,1)} %get-tuple-element.56.mixed_ref, bf16[4,512,768]{2,1,0:T(8,128)(2,1)} %get-tuple-element.57.first_ref, ...), custom_call_target="tpu_custom_call" | custom-call | flops 28991029248 | bytes 125829120 | tf_op jit(solution)/shard_map/feed_back/pallas_call | solution.py:364
  166.1 33.9 %norm_one_back.1 = (f32[4,512,768]{2,1,0:T(8,128)}, bf16[4,512,768]{2,1,0:T(8,128)(2,1)}, f32[4,16,512]{2,1,0:T(8,128)}, bf16[1,768,384]{2,1,0:T(8,128)(2,1)}, b...) custom-call(s32[1]{0:T(128)} %bitcast.1.core_ref, f32[4,512,768]{2,1,0:T(8,128)} %get-tuple-element.55.second_ref, ...), custom_call_target="tpu_custom_call" | custom-call | flops 14495514624 | bytes 62914560 | tf_op jit(solution)/shard_map/norm_one_back/pallas_call | solution.py:439
  199.9 0.0 copy-start.2
  200.0 57.3 %attend_back.1 = (bf16[4,512,2304]{2,1,0:T(8,128)(2,1)}, bf16[3,768,384]{2,1,0:T(8,128)(2,1)}, bf16[3,768,384]{2,1,0:T(8,128)(2,1)}, f32[3,8,256]{2,1,0:T(8,128)}) custom-call(s32[1]{0:T(128)} %bitcast.1.core_ref, bf16[4,512,768]{2,1,0:T(8,128)(2,1)} %tokens_ref.3, s32[4,1,512]{2,1,0:T(1,128)} %reshape.37.rows_ref, s32[4,512,1]{2,1,0:T(8,128)} %copy.22.cols_ref, ...), custom_call_target="tpu_custom_call" | custom-call | flops 39460012032 | bytes 47185920 | tf_op jit(solution)/shard_map/attend_back/pallas_call | solution.py:558
  257.3 0.8 fusion.3
  258.1 0.0 copy-done.2
  258.2 0.9 fusion.1
  259.1 1.3 concatenate.7.sums_ref
  260.4 179.4 %reduce_all.1 = (bf16[12,768,384]{2,1,0:T(8,128)(2,1)}, f32[16,768]{1,0:T(8,128)}) custom-call(bf16[8,768,384]{2,1,0:T(8,128)(2,1)} %get-tuple-element.69.feed_mine, bf16[8,768,384]{2,1,0:T(8,128)(2,1)} %get-tuple-element.70.feed_theirs, bf16[1,768,384]{2,1,0:T(8,128)(2,1)} %get-tuple-element.71.out_mine, bf16[1,768,384]{2,1,0:T(8,128)(2,1)} %get-tuple-element.72.out_theirs, ...), custom_call_target="tpu_custom_call" | custom-call | bytes 14155776 | tf_op jit(solution)/shard_map/reduce_all/pallas_call | solution.py:840
  439.8 8.4 %finish.1 = (f32[384,2304]{1,0:T(8,128)}, f32[384,768]{1,0:T(8,128)}, f32[384,3072]{1,0:T(8,128)}, f32[1536,768]{1,0:T(8,128)}, f32[16,384]{1,0:T(8,128)}) custom-call(s32[1]{0:T(128)} %bitcast.1.core_ref, bf16[12,768,384]{2,1,0:T(8,128)(2,1)} %get-tuple-element.79.units_ref, f32[16,768]{1,0:T(8,128)} %get-tuple-element.80.sums_ref), custom_call_target="tpu_custom_call" | custom-call | tf_op jit(solution)/shard_map/finish/pallas_call | solution.py:895
  448.3 1.3 fusion
  449.6 1.4 slice_bitcast_fusion.2
  451.0 0.6 reshape.41
  451.6 13.8 %token_back.1 = f32[4,512,768]{2,1,0:T(8,128)} custom-call(f32[4,512,768]{2,1,0:T(8,128)} %get-tuple-element.63.resid_ref, bf16[4,512,2304]{2,1,0:T(8,128)(2,1)} %get-tuple-element.68.jlow_ref, bf16[768,2304]{1,0:T(8,128)(2,1)} %get-tuple-element.48.qkv_ref), custom_call_target="tpu_custom_call" | custom-call | flops 7247757312 | bytes 25165824 | tf_op jit(solution)/shard_map/token_back/pallas_call | solution.py:609
  (3 shorter events, 0.0 us)
Async XLA Ops:
  0.6 17.0 %collective-permute-start.3 = (bf16[384,3072]{1,0:T(8,128)(2,1)}, bf16[384,3072]{1,0:T(8,128)(2,1)S(1)}, u32[]{:S(2)}, u32[]{:S(2)}) collective-permute-start(bf16[384,3072]{1,0:T(8,128)(2,1)} %up_a.1), channel_id=1, source_target_pairs={{0,16},{16,0},{1,17},{17,1},{2,18},{18,2},{3,19},{19,3},{4,20},{20... | collective-permute-start | bytes 7077896 | tf_op jit(solution)/shard_map/ppermute | solution.py:912
  1.2 16.6 %collective-permute-start.4 = (bf16[1536,768]{1,0:T(8,128)(2,1)}, bf16[1536,768]{1,0:T(8,128)(2,1)}, u32[]{:S(2)}, u32[]{:S(2)}) collective-permute-start(bf16[1536,768]{1,0:T(8,128)(2,1)} %dn_a.1), channel_id=1, source_target_pairs={{0,16},{16,0},{1,17},{17,1},{2,18},{18,2},{3,19},{19,3},{4,20},{20... | collective-permute-start | bytes 7077896 | tf_op jit(solution)/shard_map/ppermute | solution.py:912
  1.2 11.2 %collective-permute-start = (bf16[384,2304]{1,0:T(8,128)(2,1)}, bf16[384,2304]{1,0:T(8,128)(2,1)}, u32[]{:S(2)}, u32[]{:S(2)}) collective-permute-start(bf16[384,2304]{1,0:T(8,128)(2,1)} %own_ref.1), channel_id=1, source_target_pairs={{0,16},{16,0},{1,17},{17,1},{2,18},{18,2},{3,19},{19,3},{4,20},{20... | collective-permute-start | bytes 5308424 | tf_op jit(solution)/shard_map/ppermute | solution.py:912
  1.7 16.0 %collective-permute-start.2 = (bf16[384,768]{1,0:T(8,128)(2,1)}, bf16[384,768]{1,0:T(8,128)(2,1)S(1)}, u32[]{:S(2)}, u32[]{:S(2)}) collective-permute-start(bf16[384,768]{1,0:T(8,128)(2,1)} %out_a.1), channel_id=1, source_target_pairs={{0,16},{16,0},{1,17},{17,1},{2,18},{18,2},{3,19},{19,3},{4,20},{20... | collective-permute-start | bytes 1769480 | tf_op jit(solution)/shard_map/ppermute | solution.py:912
  3.2 9.2 %copy-start.3 = (bf16[12,384]{1,0:T(8,128)(2,1)}, bf16[12,384]{1,0:T(8,128)(2,1)S(1)}, u32[]{:S(2)}) copy-start(bf16[12,384]{1,0:T(8,128)(2,1)S(1)} %pad_maximum_fusion.small_own_ref) | copy-start | bytes 27652
  3.2 4.7 %collective-permute-start.1 = (bf16[12,384]{1,0:T(8,128)(2,1)S(1)}, bf16[12,384]{1,0:T(8,128)(2,1)S(1)}, u32[]{:S(2)}, u32[]{:S(2)}) collective-permute-start(bf16[12,384]{1,0:T(8,128)(2,1)S(1)} %pad_maximum_fusion.small_own_ref), channel_id=1, source_target_pairs={{0,16},{16,0},{1,17},{17,1},{2,18},{18,2},{3,19},{19,3},{4,20},{20... | collective-permute-start | bytes 27656 | tf_op jit(solution)/shard_map/ppermute | solution.py:912
  7.9 4.5 copy-start.4
  17.7 0.8 copy-start.1
  17.7 1.6 copy-start
  199.9 58.2 %copy-start.2 = (f32[4,8,768]{2,1,0:T(8,128)S(1)}, f32[4,8,768]{2,1,0:T(8,128)}, u32[]{:S(2)}) copy-start(f32[4,8,768]{2,1,0:T(8,128)} %get-tuple-element.78) | copy-start | bytes 294916

commit v3 on v1

--- a/solution.py
+++ b/solution.py
@@ -37,6 +37,15 @@
 
 def cost(flops, nbytes, trans=0):
     return pl.CostEstimate(flops=int(flops), bytes_accessed=int(nbytes), transcendentals=int(trans))
+
+
+def deal(core, acc, mine_ref, theirs_ref, at=0):
+    half = acc.shape[0] // 2
+    wide = acc.shape[1] // 2
+    for ref, who in ((mine_ref, core), (theirs_ref, 1 - core)):
+        rows = pl.ds(pl.multiple_of(who * half, half), half)
+        ref[at, 0:half, :] = acc[rows, 0:wide].astype(BF)
+        ref[at, half : 2 * half, :] = acc[rows, wide : 2 * wide].astype(BF)
 
 
 def binary_halves(first, second):
@@ -278,9 +287,9 @@
     def _():
         sums_ref[...] = jnp.zeros_like(sums_ref)
 
-    sums_ref[0:1, :] += gain_sum
-    sums_ref[1:2, :] += shift_sum
-    sums_ref[2:3, :] += jnp.sum(second, axis=0, keepdims=True)
+    sums_ref[3:4, :] += jnp.sum(second, axis=0, keepdims=True)
+    sums_ref[5:6, :] += gain_sum
+    sums_ref[7:8, :] += shift_sum
 
 
 def feed(norm, teacher, small, up_bin, dn_bin):
@@ -305,11 +314,11 @@
             per_seq(length, hidden),
             per_seq(length, width),
             per_seq(length, width),
-            full((8, width)),
+            full((16, width)),
         ],
         out_shape=[
             like(width, BF), like(width, BF), like(hidden, BF), like(hidden, BF), like(width, F32), like(width, BF),
-            jax.ShapeDtypeStruct((8, width), F32),
+            jax.ShapeDtypeStruct((16, width), F32),
         ],
         compiler_params=params(),
         cost_estimate=cost(4 * seqs * length * width * hidden, 36 * seqs * length * width),
@@ -318,10 +327,15 @@
 
 
 def feed_back_kernel(
-    mixed_ref, first_ref, hidden_ref, slope_ref, up_ref, dn_ref,
-    pre_ref, dgrad_ref, ugrad_ref, hsum_ref, dacc, uacc,
+    core_ref, mixed_ref, first_ref, hidden_ref, slope_ref, dn_ref, sums_in_ref,
+    pre_ref, mine_ref, theirs_ref, sums_ref, dacc, uacc,
 ):
-    tile = pl.program_id(1)
+    chunk, tile = pl.program_id(0), pl.program_id(1)
+
+    @pl.when((chunk == 0) & (tile == 0))
+    def _():
+        sums_ref[...] = sums_in_ref[...]
+
     mixed = mixed_ref[0]
     pre_back = dot_nt(mixed, dn_ref[...]) * slope_ref[0].astype(F32)
     pre_low = pre_back.astype(BF)
@@ -334,57 +348,60 @@
     def _():
         dacc[...] = dpart
         uacc[...] = upart
-        hsum_ref[0, 0:1, :] = hpart
 
     @pl.when(tile > 0)
     def _():
         dacc[...] += dpart
         uacc[...] += upart
-        hsum_ref[0, 0:1, :] += hpart
+
+    sums_ref[pl.ds(8 + chunk, 1), :] += hpart
 
     @pl.when(tile == pl.num_programs(1) - 1)
     def _():
-        dgrad_ref[...] = dacc[...].astype(BF)
-        ugrad_ref[...] = uacc[...].astype(BF)
-
-
-def feed_back(mixed, first_low, hidden, slope, up_bin, dn_bin):
+        deal(core_ref[0], dacc, mine_ref, theirs_ref, 0)
+        deal(core_ref[0], uacc, mine_ref, theirs_ref, 1)
+
+
+def feed_back(core, mixed, first_low, hidden, slope, dn_bin, sums):
     seqs, length, width = mixed.shape
     units = hidden.shape[2]
     chunks = units // width
     return pl.pallas_call(
         feed_back_kernel,
-        grid=(chunks, seqs),
-        in_specs=[
-            pl.BlockSpec((1, length, width), lambda c, s: (s, 0, 0)),
-            pl.BlockSpec((1, length, width), lambda c, s: (s, 0, 0)),
-            pl.BlockSpec((1, length, width), lambda c, s: (s, 0, c)),
-            pl.BlockSpec((1, length, width), lambda c, s: (s, 0, c)),
-            pl.BlockSpec((width, width), lambda c, s: (0, c)),
-            pl.BlockSpec((width, width), lambda c, s: (c, 0)),
-        ],
-        out_specs=[
-            pl.BlockSpec((1, length, width), lambda c, s: (s, 0, c)),
-            pl.BlockSpec((width, width), lambda c, s: (c, 0)),
-            pl.BlockSpec((width, width), lambda c, s: (c, 0)),
-            pl.BlockSpec((1, 8, width), lambda c, s: (c, 0, 0)),
-        ],
+        grid_spec=pltpu.PrefetchScalarGridSpec(
+            num_scalar_prefetch=1,
+            grid=(chunks, seqs),
+            in_specs=[
+                pl.BlockSpec((1, length, width), lambda c, s, _: (s, 0, 0)),
+                pl.BlockSpec((1, length, width), lambda c, s, _: (s, 0, 0)),
+                pl.BlockSpec((1, length, width), lambda c, s, _: (s, 0, c)),
+                pl.BlockSpec((1, length, width), lambda c, s, _: (s, 0, c)),
+                pl.BlockSpec((width, width), lambda c, s, _: (c, 0)),
+                full(sums.shape),
+            ],
+            out_specs=[
+                pl.BlockSpec((1, length, width), lambda c, s, _: (s, 0, c)),
+                pl.BlockSpec((2, width, width // 2), lambda c, s, _: (c, 0, 0)),
+                pl.BlockSpec((2, width, width // 2), lambda c, s, _: (c, 0, 0)),
+                full(sums.shape),
+            ],
+            scratch_shapes=[pltpu.VMEM((width, width), F32), pltpu.VMEM((width, width), F32)],
+        ),
         out_shape=[
             jax.ShapeDtypeStruct((seqs, length, units), BF),
-            jax.ShapeDtypeStruct((units, width), BF),
-            jax.ShapeDtypeStruct((units, width), BF),
-            jax.ShapeDtypeStruct((chunks, 8, width), F32),
-        ],
-        scratch_shapes=[pltpu.VMEM((width, width), F32), pltpu.VMEM((width, width), F32)],
+            jax.ShapeDtypeStruct((2 * chunks, width, width // 2), BF),
+            jax.ShapeDtypeStruct((2 * chunks, width, width // 2), BF),
+            jax.ShapeDtypeStruct(sums.shape, F32),
+        ],
         compiler_params=params(),
         cost_estimate=cost(6 * seqs * length * width * units, 20 * seqs * length * units),
         name="feed_back",
-    )(mixed, first_low, hidden, slope, up_bin, dn_bin)
+    )(core, mixed, first_low, hidden, slope, dn_bin, sums)
 
 
 def norm_kernel(
-    second_ref, pre_ref, norm_ref, inv_ref, ctx_ref, up_ref, out_ref, small_ref,
-    resid_ref, cback_ref, rowdot_ref, ograd_ref, sums_ref, oacc,
+    core_ref, second_ref, pre_ref, norm_ref, inv_ref, ctx_ref, up_ref, out_ref, small_ref, sums_in_ref,
+    resid_ref, cback_ref, rowdot_ref, mine_ref, theirs_ref, sums_ref, oacc,
 ):
     s = pl.program_id(0)
     width = second_ref.shape[2]
@@ -407,26 +424,28 @@
     @pl.when(s == 0)
     def _():
         oacc[...] = opart
-        sums_ref[...] = jnp.zeros_like(sums_ref)
+        sums_ref[...] = sums_in_ref[...]
 
     @pl.when(s > 0)
     def _():
         oacc[...] += opart
 
-    sums_ref[0:1, :] += gain_sum
-    sums_ref[1:2, :] += shift_sum
     sums_ref[2:3, :] += jnp.sum(resid, axis=0, keepdims=True)
+    sums_ref[4:5, :] += gain_sum
+    sums_ref[6:7, :] += shift_sum
 
     @pl.when(s == pl.num_programs(0) - 1)
     def _():
-        ograd_ref[...] = oacc[...].astype(BF)
-
-
-def norm_one_back(second, pre_low, norm, inv, ctx, up_bin, out_bin, small):
+        deal(core_ref[0], oacc, mine_ref, theirs_ref)
+
+
+def norm_one_back(core, second, pre_low, norm, inv, ctx, up_bin, out_bin, small, sums):
     seqs, length, width = second.shape
-    per_seq = lambda *shape: pl.BlockSpec((1,) + shape, lambda s: (s,) + (0,) * len(shape))
+    per_seq = lambda *shape: pl.BlockSpec((1,) + shape, lambda s, _: (s,) + (0,) * len(shape))
     return pl.pallas_call(
         norm_kernel,
+        grid_spec=pltpu.PrefetchScalarGridSpec(
+        num_scalar_prefetch=1,
         grid=(seqs,),
         in_specs=[
             per_seq(length, width),
@@ -437,37 +456,277 @@
             full(up_bin.shape),
             full(out_bin.shape),
             full(small.shape),
+            full(sums.shape),
         ],
         out_specs=[
             per_seq(length, width),
             per_seq(length, width),
             per_seq(16, length),
-            full((width, width)),
-            full((8, width)),
-        ],
+            full((1, width, width // 2)),
+            full((1, width, width // 2)),
+            full(sums.shape),
+        ],
+        scratch_shapes=[pltpu.VMEM((width, width), F32)],
+        ),
         out_shape=[
             jax.ShapeDtypeStruct((seqs, length, width), F32),
             jax.ShapeDtypeStruct((seqs, length, width), BF),
             jax.ShapeDtypeStruct((seqs, 16, length), F32),
-            jax.ShapeDtypeStruct((width, width), BF),
-            jax.ShapeDtypeStruct((8, width), F32),
-        ],
-        scratch_shapes=[pltpu.VMEM((width, width), F32)],
+            jax.ShapeDtypeStruct((1, width, width // 2), BF),
+            jax.ShapeDtypeStruct((1, width, width // 2), BF),
+            jax.ShapeDtypeStruct(sums.shape, F32),
+        ],
         compiler_params=params(),
         cost_estimate=cost(2 * seqs * length * width * 6 * width, 40 * seqs * length * width),
         name="norm_one_back",
-    )(second, pre_low, norm, inv, ctx, up_bin, out_bin, small)
+    )(core, second, pre_low, norm, inv, ctx, up_bin, out_bin, small, sums)
+
+
+MESH = pl.DeviceIdType.MESH
+
+LATE = (0, 2, 4, 6, 8, 10, 12)
+SMALL = 5
+
+
+class Exchange:
+    def __init__(self, result_ref, held, from_core, from_one, from_two, from_line, kept, came, sems):
+        (
+            local_sem, core_send, core_recv, one_send, one_recv, two_send, two_recv, line_send, line_recv,
+            line_back_send, line_back_recv, two_back_send, two_back_recv, one_back_send, one_back_recv,
+            small_send, small_recv, done_sem,
+        ) = sems
+        core, rep = lax.axis_index("shard"), lax.axis_index("rep")
+        x, y, z = rep % 2, (rep // 2) % 2, rep // 4
+        units, rows = held.shape[0], held.shape[1]
+        half, quarter, piece = rows // 2, rows // 4, rows // 16
+        partner_x, partner_y = rep + 1 - 2 * x, rep + 2 - 4 * y
+        sibling = {"shard": 1 - core}
+
+        def along(step):
+            return {"rep": rep % 4 + 4 * ((z + step) % 4)}
+
+        def meet():
+            barrier = pltpu.get_barrier_semaphore()
+            peers = [sibling, {"rep": partner_x}, {"rep": partner_y}, along(1), along(2), along(3)]
+            for peer in peers:
+                pl.semaphore_signal(barrier, inc=1, device_id=peer, device_id_type=MESH)
+            pl.semaphore_wait(barrier, len(peers))
+
+        def send(src, dst, send_sem, recv_sem, peer):
+            return pltpu.make_async_remote_copy(
+                src_ref=src, dst_ref=dst, send_sem=send_sem, recv_sem=recv_sem, device_id=peer, device_id_type=MESH
+            )
+
+        def begin(u, theirs, mine=None):
+            send(theirs, from_core.at[u], core_send.at[u], core_recv.at[u], sibling).start()
+            if mine is not None:
+                pltpu.make_async_copy(mine, held.at[u], local_sem.at[u]).start()
+
+        def fetched(u):
+            pltpu.make_async_copy(from_core.at[u], held.at[u], local_sem.at[u]).wait()
+
+        def where(u):
+            odd = u % 2
+            bit_one = x + odd * (y - x)
+            bit_two = y + odd * (x - y)
+            peer_one = {"rep": partner_x + odd * (partner_y - partner_x)}
+            peer_two = {"rep": partner_y + odd * (partner_x - partner_y)}
+            base_one = bit_one * half
+            base_two = base_one + bit_two * quarter
+            return bit_one, bit_two, peer_one, peer_two, base_one, base_two
+
+        def block(at, size):
+            return pl.ds(pl.multiple_of(at, piece), size)
+
+        def add(u, at, size, other):
+            here = block(at, size)
+            held[u, here, :] = (held[u, here, :].astype(F32) + other.astype(F32)).astype(BF)
+
+        def copy_core(u):
+            return send(from_core.at[u], from_core.at[u], core_send.at[u], core_recv.at[u], sibling)
+
+        def copy_one(u):
+            bit_one, _, peer_one, _, _, _ = where(u)
+            away = block((1 - bit_one) * half, half)
+            return send(held.at[u, away], from_one.at[u], one_send.at[u], one_recv.at[u], peer_one)
+
+        def copy_two(u):
+            _, bit_two, _, peer_two, base_one, _ = where(u)
+            away = block(base_one + (1 - bit_two) * quarter, quarter)
+            return send(held.at[u, away], from_two.at[u], two_send.at[u], two_recv.at[u], peer_two)
+
+        def copy_line(u, d):
+            base_two = where(u)[5]
+            away = block(base_two + ((z + d) % 4) * piece, piece)
+            return send(held.at[u, away], from_line.at[u, d - 1], line_send.at[u, d - 1], line_recv.at[u, d - 1], along(d))
+
+        def copy_line_back(u, d):
+            base_two = where(u)[5]
+            mine = from_core.at[u, block(base_two + z * piece, piece)]
+            return send(mine, mine, line_back_send.at[u, d - 1], line_back_recv.at[u, d - 1], along(d))
+
+        def copy_two_back(u):
+            _, _, _, peer_two, _, base_two = where(u)
+            mine = from_core.at[u, block(base_two, quarter)]
+            return send(mine, mine, two_back_send.at[u], two_back_recv.at[u], peer_two)
+
+        def copy_one_back(u):
+            _, _, peer_one, _, base_one, _ = where(u)
+            mine = from_core.at[u, block(base_one, half)]
+            return send(mine, mine, one_back_send.at[u], one_back_recv.at[u], peer_one)
+
+        def copy_done(u):
+            return pltpu.make_async_copy(from_core.at[u], result_ref.at[u], done_sem.at[u])
+
+        def stage_one(u):
+            copy_core(u).wait_recv()
+            base_one = where(u)[4]
+            away = half - base_one
+            add(u, away, half, from_core[u, block(away, half), :])
+            copy_one(u).start()
+            add(u, base_one, half, from_core[u, block(base_one, half), :])
+
+        def stage_two(u):
+            copy_one(u).wait_recv()
+            _, bit_two, _, _, base_one, base_two = where(u)
+            off = (1 - bit_two) * quarter
+            add(u, base_one + off, quarter, from_one[u, block(off, quarter), :])
+            copy_two(u).start()
+            add(u, base_two, quarter, from_one[u, block(bit_two * quarter, quarter), :])
+
+        def stage_three(u):
+            copy_two(u).wait_recv()
+            base_two = where(u)[5]
+            add(u, base_two, quarter, from_two[u])
+            for d in (2, 1, 3):
+                copy_line(u, d).start()
+
+        def stage_four(u):
+            for d in (1, 2, 3):
+                copy_line(u, d).wait_recv()
+            base_two = where(u)[5]
+            here = block(base_two + z * piece, piece)
+            total = held[u, here, :].astype(F32) + from_line[u, 0].astype(F32)
+            total = total + from_line[u, 1].astype(F32) + from_line[u, 2].astype(F32)
+            from_core[u, here, :] = total.astype(BF)
+            for d in (2, 1, 3):
+                copy_line_back(u, d).start()
+
+        def stage_five(u):
+            for d in (1, 2, 3):
+                copy_line_back(u, d).wait_recv()
+            copy_two_back(u).start()
+
+        def stage_six(u):
+            copy_two_back(u).wait_recv()
+            copy_one_back(u).start()
+
+        def stage_seven(u):
+            copy_one_back(u).wait_recv()
+            copy_done(u).start()
+
+        stages = (stage_one, stage_two, stage_three, stage_four, stage_five, stage_six, stage_seven)
+
+        small_peers = [
+            sibling, {"rep": partner_x}, {"rep": partner_y},
+            {"rep": rep + 4 - 8 * (z % 2)}, {"rep": rep + 8 - 16 * (z // 2)},
+        ]
+
+        def copy_small(k):
+            return send(kept.at[k], came.at[k], small_send.at[k], small_recv.at[k], small_peers[k])
+
+        def small_next(k):
+            copy_small(k).wait_recv()
+            kept[k + 1] = kept[k] + came[k]
+            if k + 1 < SMALL:
+                copy_small(k + 1).start()
+
+        def tick(t, _=0):
+            for k, late in enumerate(LATE):
+                u = t - late
+
+                @pl.when((u >= 0) & (u < units))
+                def _():
+                    stages[k](u)
+
+            return 0
+
+        def settle():
+            for k in range(SMALL):
+                copy_small(k).wait_send()
+
+            def finish(u, _):
+                copy_core(u).wait_send()
+                copy_one(u).wait_send()
+                copy_two(u).wait_send()
+                for d in (1, 2, 3):
+                    copy_line(u, d).wait_send()
+                    copy_line_back(u, d).wait_send()
+                copy_two_back(u).wait_send()
+                copy_one_back(u).wait_send()
+                copy_done(u).wait()
+                return 0
+
+            lax.fori_loop(0, units, finish, 0)
+
+        self.meet, self.begin, self.fetched, self.tick, self.settle = meet, begin, fetched, tick, settle
+        self.small_start, self.small_next = (lambda: copy_small(0).start()), small_next
+        self.ticks = units + LATE[-1]
+
+    @staticmethod
+    def buffers(units, rows, cols, small):
+        dma = pltpu.SemaphoreType.DMA
+        return [
+            pltpu.VMEM((units, rows, cols), BF),
+            pltpu.VMEM((units, rows, cols), BF),
+            pltpu.VMEM((units, rows // 2, cols), BF),
+            pltpu.VMEM((units, rows // 4, cols), BF),
+            pltpu.VMEM((units, 3, rows // 16, cols), BF),
+            pltpu.VMEM((SMALL + 1,) + small, F32),
+            pltpu.VMEM((SMALL,) + small, F32),
+        ] + [dma((units,))] * 7 + [dma((units, 3))] * 4 + [dma((units,))] * 4 + [dma((SMALL,))] * 2 + [dma((units,))]
 
 
 GROUP = 256
 TILE_B = 256
 
 
-def attend_back_kernel(
-    tokens_ref, rows_ref, cols_ref, q_ref, k_ref, v_ref, cback_ref, lse_ref, rowdot_ref,
-    jlow_ref, grad_ref, sums_ref, acc, bias_ref,
-):
+def attend_back_kernel(linked, *refs):
+    (tokens_ref, rows_ref, cols_ref, q_ref, k_ref, v_ref, cback_ref, lse_ref, rowdot_ref, sums_in_ref), refs = (
+        refs[:10], refs[10:]
+    )
     g, s = pl.program_id(0), pl.program_id(1)
+    last_g, last_s = pl.num_programs(0) - 1, pl.num_programs(1) - 1
+    if linked:
+        feed_mine, feed_theirs, out_mine, out_theirs, jlow_ref, result_ref, total_ref, acc, bias_ref, theirs = refs[:10]
+        buffers, sems = refs[10:17], refs[17:]
+        exchange = Exchange(result_ref, *buffers, sems)
+        held, kept = buffers[0], buffers[5]
+        core = lax.axis_index("shard")
+        early = feed_mine.shape[0] + 1
+        sums_ref = kept.at[0]
+        step = g * pl.num_programs(1) + s
+    else:
+        jlow_ref, mine_ref, theirs_ref, sums_ref, acc, bias_ref = refs
+        core = 0
+
+    @pl.when((g == 0) & (s == 0))
+    def _():
+        if linked:
+            exchange.meet()
+            for u in range(early - 1):
+                exchange.begin(u, feed_theirs.at[u], feed_mine.at[u])
+            exchange.begin(early - 1, out_theirs.at[0], out_mine.at[0])
+            for u in range(early):
+                exchange.fetched(u)
+        sums_ref[...] = sums_in_ref[...]
+
+    if linked:
+
+        @pl.when(step < pl.num_programs(0) * pl.num_programs(1) - 1)
+        def _():
+            exchange.tick(step)
+
     length = tokens_ref.shape[1]
     tile = min(TILE_B, length)
     bias_ref[...] = jnp.where(rows_ref[0] >= cols_ref[0], 0.0, NEG).astype(F32)
@@ -505,69 +764,84 @@
             vsum = jnp.sum(dv, axis=0, keepdims=True)
             vtotal = vsum if t == 0 else vtotal + vsum
         jlow_ref[0, :, at] = dq.astype(BF)
-        qsum = jnp.sum(dq, axis=0, keepdims=True)
-
-        @pl.when(s == 0)
+        lanes = pl.ds(pl.multiple_of(g * GROUP + pair * 128, 128), 128)
+        sums_ref[0:1, lanes] += jnp.sum(dq, axis=0, keepdims=True)
+        sums_ref[1:2, lanes] += vtotal
+
+    part = dot_tn(tokens_ref[0], jlow_ref[0])
+
+    @pl.when(s == 0)
+    def _():
+        acc[...] = part
+
+    @pl.when(s > 0)
+    def _():
+        acc[...] += part
+
+    @pl.when(s == last_s)
+    def _():
+        if linked:
+            deal(core, acc, held.at[pl.ds(early + g, 1)], theirs.at[pl.ds(g, 1)])
+            exchange.begin(early + g, theirs.at[g])
+        else:
+            deal(core, acc, mine_ref, theirs_ref)
+
+    if linked:
+
+        @pl.when((g == last_g) & (s == last_s))
         def _():
-            sums_ref[0, 0:1, at] = qsum
-            sums_ref[0, 1:2, at] = vtotal
-
-        @pl.when(s > 0)
-        def _():
-            sums_ref[0, 0:1, at] += qsum
-            sums_ref[0, 1:2, at] += vtotal
-
-    part = dot_tn(tokens_ref[0], jlow_ref[0])
-
-    @pl.when(s == 0)
-    def _():
-        acc[...] = part
-
-    @pl.when(s > 0)
-    def _():
-        acc[...] += part
-
-    @pl.when(s == pl.num_programs(1) - 1)
-    def _():
-        grad_ref[...] = acc[...].astype(BF)
-
-
-def attend_back(tokens, block_ids, joined, cback, lse, rowdot):
+            start = pl.num_programs(0) * pl.num_programs(1) - 1
+            exchange.small_start()
+            for k in range(SMALL):
+                exchange.tick(start + k)
+                exchange.small_next(k)
+            lax.fori_loop(start + SMALL, exchange.ticks, exchange.tick, 0)
+            total_ref[...] = kept[SMALL]
+            exchange.settle()
+
+
+def attend_back(tokens, block_ids, joined, cback, lse, rowdot, sums, feed_grads=None, out_grads=None):
     seqs, length, width = tokens.shape
     rows = block_ids.reshape(seqs, 1, length)
     cols = block_ids.reshape(seqs, length, 1)
     groups = width // GROUP
+    linked = feed_grads is not None
     whole = lambda *shape: pl.BlockSpec((1,) + shape, lambda g, s: (s,) + (0,) * len(shape))
     part = lambda k: pl.BlockSpec((1, length, GROUP), lambda g, s: (s, 0, k * groups + g))
+    anywhere = pl.BlockSpec(memory_space=pl.ANY)
+    unit = (width, width // 2)
+    like = jax.ShapeDtypeStruct
+    in_specs = [
+        whole(length, width), whole(1, length), whole(length, 1), part(0), part(1), part(2), part(0),
+        whole(16, length), whole(16, length), full(sums.shape),
+    ]
+    operands = [tokens, rows, cols, joined, joined, joined, cback, lse, rowdot, sums]
+    out_specs = [pl.BlockSpec((1, length, 3 * GROUP), lambda g, s: (s, 0, g))]
+    out_shape = [like((seqs, length, 3 * width), BF)]
+    scratch = [pltpu.VMEM((width, 3 * GROUP), F32), pltpu.VMEM((length, length), F32)]
+    if linked:
+        units = feed_grads[0].shape[0] + 1 + groups
+        in_specs += [anywhere] * 4
+        operands += [*feed_grads, *out_grads]
+        out_specs += [anywhere, full(sums.shape)]
+        out_shape += [like((units,) + unit, BF), like(sums.shape, F32)]
+        scratch += [pltpu.VMEM((groups,) + unit, BF)] + Exchange.buffers(units, *unit, sums.shape)
+        extra = dict(collective_id=0, has_side_effects=True)
+    else:
+        out_specs += [pl.BlockSpec((1,) + unit, lambda g, s: (g, 0, 0))] * 2 + [full(sums.shape)]
+        out_shape += [like((groups,) + unit, BF)] * 2 + [like(sums.shape, F32)]
+        extra = {}
     return pl.pallas_call(
-        attend_back_kernel,
+        functools.partial(attend_back_kernel, linked),
         grid=(groups, seqs),
-        in_specs=[
-            whole(length, width),
-            whole(1, length),
-            whole(length, 1),
-            part(0),
-            part(1),
-            part(2),
-            part(0),
-            whole(16, length),
-            whole(16, length),
-        ],
-        out_specs=[
-            pl.BlockSpec((1, length, 3 * GROUP), lambda g, s: (s, 0, g)),
-            pl.BlockSpec((width, 3 * GROUP), lambda g, s: (g, 0)),
-            pl.BlockSpec((1, 8, GROUP), lambda g, s: (g, 0, 0)),
-        ],
-        out_shape=[
-            jax.ShapeDtypeStruct((seqs, length, 3 * width), BF),
-            jax.ShapeDtypeStruct((groups * width, 3 * GROUP), BF),
-            jax.ShapeDtypeStruct((groups, 8, GROUP), F32),
-        ],
-        scratch_shapes=[pltpu.VMEM((width, 3 * GROUP), F32), pltpu.VMEM((length, length), F32)],
-        compiler_params=params(),
+        in_specs=in_specs,
+        out_specs=out_specs,
+        out_shape=out_shape,
+        scratch_shapes=scratch,
+        compiler_params=params(**extra),
         cost_estimate=cost(seqs * length * width * (6 * width + 40 * length), 30 * seqs * length * width),
         name="attend_back",
-    )(tokens, rows, cols, joined, joined, joined, cback, lse, rowdot)
+    )(*operands)
 
 
 def token_kernel(resid_ref, jlow_ref, qkv_ref, grad_ref):
@@ -597,20 +871,48 @@
     )(resid, jlow, qkv_bin)
 
 
-def layer(core, tokens, teacher, block_ids, own, other, small_own, small_other):
-    qkv_bin, small = prep_qkv(core, own[0], other[0], small_own, small_other)
-    out_bin, up_bin, dn_bin = prep_rest(core, own[1], other[1], own[2], other[2], own[3], other[3])
-    joined, ctx, lse, norm, inv = attend(tokens, block_ids, qkv_bin, out_bin, small)
-    final, first_low, hidden, slope, second, mixed, sums_two = feed(norm, teacher, small, up_bin, dn_bin)
-    pre_low, dgrad, ugrad, hsum = feed_back(mixed, first_low, hidden, slope, up_bin, dn_bin)
-    resid, cback, rowdot, ograd, sums_one = norm_one_back(second, pre_low, norm, inv, ctx, up_bin, out_bin, small)
-    jlow, qgrad, sums_qv = attend_back(tokens, block_ids, joined, cback, lse, rowdot)
-    token_grad = token_back(resid, jlow, qkv_bin)
-    return final, token_grad, dgrad, ugrad, ograd, qgrad, sums_two, hsum, sums_one, sums_qv
-
-
-def as_sent(value):
-    return jax.tree.map(lambda a: a.astype(BF), value)
+def finish_kernel(core_ref, units_ref, sums_ref, qkv_ref, out_ref, up_ref, dn_ref, small_ref):
+    units, rows, half = units_ref.shape
+    groups = rows // GROUP
+    chunks = (units - 1 - groups) // 2
+    wide = [slice(0, rows // 2), slice(rows // 2, rows)]
+    for c in range(chunks):
+        for p in range(2):
+            dn_ref[c * half : (c + 1) * half, p * half : (p + 1) * half] = units_ref[2 * c, wide[p], :].astype(F32)
+            at = p * chunks * half + c * half
+            up_ref[:, at : at + half] = units_ref[2 * c + 1, wide[p], :].astype(F32)
+    for p in range(2):
+        out_ref[:, p * half : (p + 1) * half] = units_ref[2 * chunks, wide[p], :].astype(F32)
+    for g in range(groups):
+        for j in range(3 * GROUP // 128):
+            col = j * 128
+            at = (col // GROUP) * rows + g * GROUP + col % GROUP
+            qkv_ref[:, at : at + 128] = units_ref[
+                2 * chunks + 1 + g, wide[col // half], col % half : col % half + 128
+            ].astype(F32)
+    mine = pl.ds(pl.multiple_of(core_ref[0] * half, half), half)
+    small_ref[...] = sums_ref[:, mine]
+
+
+def finish(core, units, sums):
+    count, rows, half = units.shape
+    groups = rows // GROUP
+    hidden = (count - 1 - groups) // 2 * rows
+    vm = pl.BlockSpec(memory_space=pltpu.VMEM)
+    return pl.pallas_call(
+        finish_kernel,
+        in_specs=[pl.BlockSpec(memory_space=pltpu.SMEM), vm, vm],
+        out_specs=[vm] * 5,
+        out_shape=[
+            jax.ShapeDtypeStruct((half, 3 * rows), F32),
+            jax.ShapeDtypeStruct((half, rows), F32),
+            jax.ShapeDtypeStruct((half, hidden), F32),
+            jax.ShapeDtypeStruct((hidden // 2, rows), F32),
+            jax.ShapeDtypeStruct((sums.shape[0], half), F32),
+        ],
+        compiler_params=params(),
+        name="finish",
+    )(core, units, sums)
 
 
 def swap(value):
@@ -622,10 +924,33 @@
     return jnp.concatenate([biases.T, gain.T, shift.T, hidden_bias.reshape(-1, rows)], axis=0)
 
 
+def reduce_plain(feed_grads, out_grads, qkv_grads, sums):
+    def whole(mine, theirs):
+        count, rows, half = mine.shape
+        cut = lambda a: a.reshape(count, 2, half, half).transpose(0, 2, 1, 3).reshape(count, half, rows)
+        return jnp.concatenate([cut(mine), cut(theirs)], axis=1)
+
+    feed_all, out_all, qkv_all = whole(*feed_grads), whole(*out_grads), whole(*qkv_grads)
+    chunks, groups, width = feed_all.shape[0] // 2, qkv_all.shape[0], feed_all.shape[2]
+    half, units = width // 2, chunks * width
+    grads = (
+        qkv_all.reshape(groups, width, 3, GROUP).transpose(1, 2, 0, 3).reshape(width, 3 * width),
+        out_all[0],
+        feed_all[1::2].reshape(chunks, width, 2, half).transpose(1, 2, 0, 3).reshape(width, units),
+        feed_all[0::2].reshape(chunks, 2, half, width).transpose(1, 0, 2, 3).reshape(units, width),
+        sums[0:4].T.astype(BF),
+        sums[8:].reshape(chunks, 2, half).transpose(1, 0, 2).reshape(-1).astype(BF),
+        sums[4:6].T.astype(BF),
+        sums[6:8].T.astype(BF),
+    )
+    owned = lax.psum_scatter(grads, "shard", scatter_dimension=0, tiled=True)
+    return jax.tree.map(lambda part: part.astype(F32), lax.psum(owned, "rep"))
+
+
 def body(tokens, teacher, block_ids, *weights):
     qkv, out, up, down, biases, hidden_bias, gain, shift = weights
-    shards = lax.axis_size("shard")
-    if shards == 2:
+    paired = lax.axis_size("shard") == 2 and lax.axis_size("rep") == 16
+    if paired:
         core = lax.axis_index("shard").reshape(1)
         own = (qkv, out, up, down)
         small_own = small_rows(biases, gain, shift, hidden_bias)
@@ -636,28 +961,29 @@
         gathered = [lax.all_gather(w, "shard", axis=0, tiled=True) for w in weights]
         cut = [jnp.split(w, 2, axis=0) for w in gathered]
         own, other = (tuple(c[i] for c in cut[:4]) for i in range(2))
-        small_own, small_other = (
-            small_rows(cut[4][i], cut[6][i], cut[7][i], cut[5][i]) for i in range(2)
-        )
-    final, token_grad, dgrad, ugrad, ograd, qgrad, sums_two, hsum, sums_one, sums_qv = layer(
-        core, tokens, teacher, block_ids, own, other, small_own, small_other
+        small_own, small_other = (small_rows(cut[4][i], cut[6][i], cut[7][i], cut[5][i]) for i in range(2))
+    qkv_bin, small = prep_qkv(core, own[0], other[0], small_own, small_other)
+    out_bin, up_bin, dn_bin = prep_rest(core, own[1], other[1], own[2], other[2], own[3], other[3])
+    joined, ctx, lse, norm, inv = attend(tokens, block_ids, qkv_bin, out_bin, small)
+    final, first_low, hidden, slope, second, mixed, sums = feed(norm, teacher, small, up_bin, dn_bin)
+    pre_low, *feed_grads, sums = feed_back(core, mixed, first_low, hidden, slope, dn_bin, sums)
+    resid, cback, rowdot, *out_grads, sums = norm_one_back(
+        core, second, pre_low, norm, inv, ctx, up_bin, out_bin, small, sums
     )
-    width, units = ograd.shape[0], dgrad.shape[0]
-    chunks, half = units // width, width // 2
-    groups = width // GROUP
-    grads = (
-        qgrad.reshape(groups, width, 3, GROUP).transpose(1, 2, 0, 3).reshape(width, 3 * width),
-        ograd,
-        ugrad.reshape(chunks, width, 2, half).transpose(1, 2, 0, 3).reshape(width, units),
-        dgrad.reshape(chunks, 2, half, width).transpose(1, 0, 2, 3).reshape(units, width),
-        jnp.stack([sums_qv[:, 0].reshape(-1), sums_qv[:, 1].reshape(-1), sums_one[2], sums_two[2]], axis=1),
-        hsum[:, 0].reshape(chunks, 2, half).transpose(1, 0, 2).reshape(-1),
-        jnp.stack([sums_one[0], sums_two[0]], axis=1),
-        jnp.stack([sums_one[1], sums_two[1]], axis=1),
+    if not paired:
+        jlow, *qkv_grads, sums = attend_back(tokens, block_ids, joined, cback, lse, rowdot, sums)
+        token_grad = token_back(resid, jlow, qkv_bin)
+        return (final, token_grad) + tuple(reduce_plain(feed_grads, out_grads, qkv_grads, sums[:12]))
+    jlow, units, sums = attend_back(
+        tokens, block_ids, joined, cback, lse, rowdot, sums, feed_grads, out_grads
     )
-    owned = lax.psum_scatter(as_sent(grads), "shard", scatter_dimension=0, tiled=True)
-    summed = jax.tree.map(lambda part: part.astype(F32), lax.psum(owned, "rep"))
-    return (final, token_grad) + tuple(summed)
+    token_grad = token_back(resid, jlow, qkv_bin)
+    qkv_grad, out_grad, up_grad, dn_grad, small = finish(core, units, sums)
+    hidden_rows = hidden_bias.shape[0] // small.shape[1]
+    return (
+        final, token_grad, qkv_grad, out_grad, up_grad, dn_grad,
+        small[0:4].T, small[8 : 8 + hidden_rows].reshape(-1), small[4:6].T, small[6:8].T,
+    )
 
 
 def solution(mesh):

time: 641 us -> 371 us (0.58)
  waiting for transfers between devices: 192 us -> 5.39 us
  Pallas kernels: 257 us -> 346 us
  blocking collectives: 82.9 us -> 0 us
  local copies, waits for them, and re-layouts: 76 us -> 8.91 us
  between operations: 15.1 us -> 1.22 us
  other arithmetic: 10.8 us -> 0.73 us
    psum x1 -> x0, waiting for transfers between devices: 154 us -> none  [body(): summed = jax.tree.map(lambda part: part.astype(F32), lax.psum(owned, 'rep'))]
    pallas_call x3 -> x4, Pallas kernels: 139 us -> 228 us  [the longest x1 138 us: attend_back(): pl.pallas_call(functools.partial(attend_back_kernel, linked), grid=(group...]
    psum x1 -> x0, blocking collectives: 80.4 us -> none  [body(): summed = jax.tree.map(lambda part: part.astype(F32), lax.psum(owned, 'rep'))]
    reshape x3 -> x1, local copies, waits for them, and re-layouts: 27.9 us -> 0.61 us  [body(): small[8:8 + hidden_rows].reshape(-1)]
    transpose x3 -> x1, local copies, waits for them, and re-layouts: 22.2 us -> 1.37 us  [body(): small[6:8]]
    reduce_scatter x3 -> x0, waiting for transfers between devices: 19.5 us -> none  [body(): lax.psum_scatter(as_sent(grads), 'shard', scatter_dimension=0, tiled=True)]
    unnamed x31 -> x8, local copies, waits for them, and re-layouts: 20.8 us -> 1.57 us
    unnamed x12 -> x0, waiting for transfers between devices: 12.9 us -> none
  transfers between devices with their start and end apart: 13 -> 5, of which waited for: 7 -> 2; matrix products, arithmetic and copies ran while one was open for 8% -> 1% of each run, Pallas kernels for 3% -> 1%
where the time goes in v3:
time: 371 us; the launch traced here: 364 us
  Pallas kernels  346 us (93%)
  local copies, waits for them, and re-layouts  8.91 us (2%)
  waiting for transfers between devices  5.39 us (1%)
    pallas_call x1, Pallas kernels, attend_back(): pl.pallas_call(functools.partial(attend_back_kernel, linked), grid=(group...  138 us
    pallas_call x1, Pallas kernels, attend(): pl.pallas_call(attend_kernel, grid=(seqs,), in_specs=[per_seq(length, wid...  49.9 us
    pallas_call x1, Pallas kernels, feed_back(): pl.pallas_call(feed_back_kernel, grid_spec=pltpu.PrefetchScalarGridSpec(n...  47.6 us
    pallas_call x1, Pallas kernels, feed(): pl.pallas_call(feed_kernel, grid=(seqs,), in_specs=[per_seq(length, width...  38.2 us
    pallas_call x1, Pallas kernels, norm_one_back(): pl.pallas_call(norm_kernel, grid_spec=pltpu.PrefetchScalarGridSpec(num_sc...  33.9 us
    pallas_call x1, Pallas kernels, token_back(): pl.pallas_call(token_kernel, grid=(seqs,), in_specs=[per_seq(length, widt...  13.8 us
    pallas_call x1, Pallas kernels, prep_rest(): pl.pallas_call(prep_rest_kernel, in_specs=[pl.BlockSpec(memory_space=pltp...  11.5 us
    pallas_call x1, Pallas kernels, finish(): pl.pallas_call(finish_kernel, in_specs=[pl.BlockSpec(memory_space=pltpu.S...  8.45 us
  transfers between devices with their start and end apart: 5, of which 2 were waited for; matrix products, arithmetic and copies ran while one was open for 1% of the time, Pallas kernels for 1%

profile of v3, /device:TPU:0, one launch (start us, length us, event | category | flops | bytes accessed | tf_op | source)
XLA Modules:
  0.0 364.3 jit_solution(11038437204708589157)
XLA Ops:
  0.6 0.5 collective-permute-start.3
  1.2 0.1 collective-permute-start.4
  1.2 0.4 collective-permute-start
  1.7 0.1 collective-permute-start.2
  1.8 0.7 reshape.40
  2.5 0.7 pad_maximum_fusion.small_own_ref
  3.2 0.0 copy-start.2
  3.2 0.5 collective-permute-start.1
  3.7 1.3 reshape.37.rows_ref.refs_1_
  5.0 2.0 copy.21.cols_ref.refs_2_
  7.0 0.9 collective-permute-done.1.small_other_ref
  7.9 0.0 copy-start.3
  7.9 4.5 %collective-permute-done.other_ref = bf16[384,2304]{1,0:T(8,128)(2,1)} collective-permute-done((bf16[384,2304]{1,0:T(8,128)(2,1)}, bf16[384,2304]{1,0:T(8,128)(2,1)}, u32[]{:S(2)}, u32[]{:S(2)}) %collective-permute-start) | collective-permute-done | bytes 1769504 | tf_op jit(solution)/shard_map/ppermute | solution.py:919
  12.4 0.0 copy-done.2
  12.4 0.0 copy-done.3
  12.4 5.2 %prep_qkv.1 = (bf16[768,2304]{1,0:T(8,128)(2,1)}, f32[12,768]{1,0:T(8,128)}) custom-call(s32[1]{0:T(128)} %bitcast.1.core_ref, bf16[384,2304]{1,0:T(8,128)(2,1)} %own_ref.1, bf16[384,2304]{1,0:T(8,128)(2,1)} %collective-permute-done.other_ref, bf16[12,384]{1,0:T(8,128)(2,1)} %copy-done.2, bf16[12,384]{1,0:T(8,128)(2,1)} %copy-done.3), custom_call_target="tpu_custom_call" | custom-call | flops 7077888 | bytes 7077888 | tf_op jit(solution)/shard_map/prep_qkv/pallas_call | solution.py:82
  17.6 0.0 collective-permute-done.2.out_b
  17.6 0.0 copy-start.1
  17.6 0.0 collective-permute-done.3.up_b
  17.7 0.0 copy-start
  17.7 0.0 collective-permute-done.4.dn_b
  17.7 0.8 copy-done.1
  18.5 0.8 copy-done
  19.2 11.5 %prep_rest.1 = (bf16[768,768]{1,0:T(8,128)(2,1)}, bf16[768,3072]{1,0:T(8,128)(2,1)}, bf16[3072,768]{1,0:T(8,128)(2,1)}) custom-call(s32[1]{0:T(128)} %bitcast.1.core_ref, bf16[384,768]{1,0:T(8,128)(2,1)} %out_a.1, bf16[384,768]{1,0:T(8,128)(2,1)} %copy-done.1, bf16[384,3072]{1,0:T(8,128)(2,1)} %up_a.1, bf16[384,3072]{1,0:T(8,128)(2,1)} %copy-done, ...), custom_call_target="tpu_custom_call" | custom-call | flops 18874368 | bytes 18874368 | tf_op jit(solution)/shard_map/prep_rest/pallas_call | solution.py:134
  30.8 49.9 %attend.1 = (bf16[4,512,2304]{2,1,0:T(8,128)(2,1)}, bf16[4,512,768]{2,1,0:T(8,128)(2,1)}, f32[4,16,512]{2,1,0:T(8,128)}, f32[4,512,768]{2,1,0:T(8,128)}, f32[4,512,1]{2,1,0:T(8,128)}) custom-call(bf16[4,512,768]{2,1,0:T(8,128)(2,1)} %refs_0_.1, s32[4,1,512]{2,1,0:T(1,128)} %reshape.37.rows_ref.refs_1_, s32[4,512,1]{2,1,0:T(8,128)} %copy.21.cols_ref.refs_2_, ...), custom_call_target="tpu_custom_call" | custom-call | flops 22548578304 | bytes 47185920 | tf_op jit(solution)/shard_map/attend/pallas_call | solution.py:209
  80.6 38.2 %feed.1 = (bf16[4,512,768]{2,1,0:T(8,128)(2,1)}, bf16[4,512,768]{2,1,0:T(8,128)(2,1)}, bf16[4,512,3072]{2,1,0:T(8,128)(2,1)}, bf16[4,512,3072]{2,1,0:T(8,128)(2,...) custom-call(f32[4,512,768]{2,1,0:T(8,128)} %get-tuple-element.48.norm_ref, ...), custom_call_target="tpu_custom_call" | custom-call | flops 19327352832 | bytes 56623104 | tf_op jit(solution)/shard_map/feed/pallas_call | solution.py:300
  118.8 47.6 %feed_back.1 = (bf16[4,512,3072]{2,1,0:T(8,128)(2,1)}, bf16[8,768,384]{2,1,0:T(8,128)(2,1)}, bf16[8,768,384]{2,1,0:T(8,128)(2,1)}, f32[16,768]{1,0:T(8,128)}) custom-call(s32[1]{0:T(128)} %bitcast.1.core_ref, bf16[4,512,768]{2,1,0:T(8,128)(2,1)} %get-tuple-element.53.mixed_ref, bf16[4,512,768]{2,1,0:T(8,128)(2,1)} %get-tuple-element.54.first_ref, ...), custom_call_target="tpu_custom_call" | custom-call | flops 28991029248 | bytes 125829120 | tf_op jit(solution)/shard_map/feed_back/pallas_call | solution.py:369
  166.5 33.9 %norm_one_back.1 = (f32[4,512,768]{2,1,0:T(8,128)}, bf16[4,512,768]{2,1,0:T(8,128)(2,1)}, f32[4,16,512]{2,1,0:T(8,128)}, bf16[1,768,384]{2,1,0:T(8,128)(2,1)}, b...) custom-call(s32[1]{0:T(128)} %bitcast.1.core_ref, f32[4,512,768]{2,1,0:T(8,128)} %get-tuple-element.52.second_ref, ...), custom_call_target="tpu_custom_call" | custom-call | flops 14495514624 | bytes 62914560 | tf_op jit(solution)/shard_map/norm_one_back/pallas_call | solution.py:445
  200.4 137.8 %attend_back.1 = (bf16[4,512,2304]{2,1,0:T(8,128)(2,1)}, bf16[12,768,384]{2,1,0:T(8,128)(2,1)}, f32[16,768]{1,0:T(8,128)}) custom-call(bf16[4,512,768]{2,1,0:T(8,128)(2,1)} %refs_0_.1, s32[4,1,512]{2,1,0:T(1,128)} %reshape.37.rows_ref.refs_1_, s32[4,512,1]{2,1,0:T(8,128)} %copy.21.cols_ref.refs_2_, ...), custom_call_target="tpu_custom_call" | custom-call | flops 39460012032 | bytes 47185920 | tf_op jit(solution)/shard_map/attend_back/pallas_call | solution.py:834
  338.2 8.4 %finish.1 = (f32[384,2304]{1,0:T(8,128)}, f32[384,768]{1,0:T(8,128)}, f32[384,3072]{1,0:T(8,128)}, f32[1536,768]{1,0:T(8,128)}, f32[16,384]{1,0:T(8,128)}) custom-call(s32[1]{0:T(128)} %bitcast.1.core_ref, bf16[12,768,384]{2,1,0:T(8,128)(2,1)} %get-tuple-element.73.units_ref, f32[16,768]{1,0:T(8,128)} %get-tuple-element.74.sums_ref), custom_call_target="tpu_custom_call" | custom-call | tf_op jit(solution)/shard_map/finish/pallas_call | solution.py:902
  346.7 1.4 slice_bitcast_fusion.1
  348.0 1.3 fusion
  349.4 0.6 reshape.41
  350.0 13.8 %token_back.1 = f32[4,512,768]{2,1,0:T(8,128)} custom-call(f32[4,512,768]{2,1,0:T(8,128)} %get-tuple-element.62.resid_ref, bf16[4,512,2304]{2,1,0:T(8,128)(2,1)} %get-tuple-element.72.jlow_ref, bf16[768,2304]{1,0:T(8,128)(2,1)} %get-tuple-element.45.qkv_ref), custom_call_target="tpu_custom_call" | custom-call | flops 7247757312 | bytes 25165824 | tf_op jit(solution)/shard_map/token_back/pallas_call | solution.py:862
Async XLA Ops:
  0.6 17.0 %collective-permute-start.3 = (bf16[384,3072]{1,0:T(8,128)(2,1)}, bf16[384,3072]{1,0:T(8,128)(2,1)S(1)}, u32[]{:S(2)}, u32[]{:S(2)}) collective-permute-start(bf16[384,3072]{1,0:T(8,128)(2,1)} %up_a.1), channel_id=1, source_target_pairs={{0,16},{16,0},{1,17},{17,1},{2,18},{18,2},{3,19},{19,3},{4,20},{20... | collective-permute-start | bytes 7077896 | tf_op jit(solution)/shard_map/ppermute | solution.py:919
  1.2 16.5 %collective-permute-start.4 = (bf16[1536,768]{1,0:T(8,128)(2,1)}, bf16[1536,768]{1,0:T(8,128)(2,1)}, u32[]{:S(2)}, u32[]{:S(2)}) collective-permute-start(bf16[1536,768]{1,0:T(8,128)(2,1)} %dn_a.1), channel_id=1, source_target_pairs={{0,16},{16,0},{1,17},{17,1},{2,18},{18,2},{3,19},{19,3},{4,20},{20... | collective-permute-start | bytes 7077896 | tf_op jit(solution)/shard_map/ppermute | solution.py:919
  1.2 11.2 %collective-permute-start = (bf16[384,2304]{1,0:T(8,128)(2,1)}, bf16[384,2304]{1,0:T(8,128)(2,1)}, u32[]{:S(2)}, u32[]{:S(2)}) collective-permute-start(bf16[384,2304]{1,0:T(8,128)(2,1)} %own_ref.1), channel_id=1, source_target_pairs={{0,16},{16,0},{1,17},{17,1},{2,18},{18,2},{3,19},{19,3},{4,20},{20... | collective-permute-start | bytes 5308424 | tf_op jit(solution)/shard_map/ppermute | solution.py:919
  1.7 16.0 %collective-permute-start.2 = (bf16[384,768]{1,0:T(8,128)(2,1)}, bf16[384,768]{1,0:T(8,128)(2,1)S(1)}, u32[]{:S(2)}, u32[]{:S(2)}) collective-permute-start(bf16[384,768]{1,0:T(8,128)(2,1)} %out_a.1), channel_id=1, source_target_pairs={{0,16},{16,0},{1,17},{17,1},{2,18},{18,2},{3,19},{19,3},{4,20},{20... | collective-permute-start | bytes 1769480 | tf_op jit(solution)/shard_map/ppermute | solution.py:919
  3.2 9.2 %copy-start.2 = (bf16[12,384]{1,0:T(8,128)(2,1)}, bf16[12,384]{1,0:T(8,128)(2,1)S(1)}, u32[]{:S(2)}) copy-start(bf16[12,384]{1,0:T(8,128)(2,1)S(1)} %pad_maximum_fusion.small_own_ref) | copy-start | bytes 27652
  3.2 4.7 %collective-permute-start.1 = (bf16[12,384]{1,0:T(8,128)(2,1)S(1)}, bf16[12,384]{1,0:T(8,128)(2,1)S(1)}, u32[]{:S(2)}, u32[]{:S(2)}) collective-permute-start(bf16[12,384]{1,0:T(8,128)(2,1)S(1)} %pad_maximum_fusion.small_own_ref), channel_id=1, source_target_pairs={{0,16},{16,0},{1,17},{17,1},{2,18},{18,2},{3,19},{19,3},{4,20},{20... | collective-permute-start | bytes 27656 | tf_op jit(solution)/shard_map/ppermute | solution.py:919
  7.9 4.5 %copy-start.3 = (bf16[12,384]{1,0:T(8,128)(2,1)}, bf16[12,384]{1,0:T(8,128)(2,1)S(1)}, u32[]{:S(2)}) copy-start(bf16[12,384]{1,0:T(8,128)(2,1)S(1)} %collective-permute-done.1.small_other_ref) | copy-start | bytes 27652
  17.6 0.8 copy-start.1
  17.7 1.6 copy-start

commit v4 on v3

--- a/solution.py
+++ b/solution.py
@@ -399,92 +399,28 @@
     )(core, mixed, first_low, hidden, slope, dn_bin, sums)
 
 
-def norm_kernel(
-    core_ref, second_ref, pre_ref, norm_ref, inv_ref, ctx_ref, up_ref, out_ref, small_ref, sums_in_ref,
-    resid_ref, cback_ref, rowdot_ref, mine_ref, theirs_ref, sums_ref, oacc,
-):
-    s = pl.program_id(0)
-    width = second_ref.shape[2]
-    back = second_ref[0] + dot_nt(pre_ref[0], up_ref[...])
-    resid, gain_sum, shift_sum = norm_back(back, norm_ref[0], inv_ref[0], small_ref[4:5, :])
-    resid_ref[0] = resid
+def norm_step(second, pre_low, norm, inv, ctx, up_ref, out_ref, small_ref, sums_ref):
+    width = second.shape[1]
+    back = second + dot_nt(pre_low, up_ref[...])
+    resid, gain_sum, shift_sum = norm_back(back, norm, inv, small_ref[4:5, :])
+    sums_ref[2:3, :] += jnp.sum(resid, axis=0, keepdims=True)
+    sums_ref[4:5, :] += gain_sum
+    sums_ref[6:7, :] += shift_sum
     low = resid.astype(BF)
     cback = dot_nt(low, out_ref[...]).astype(BF)
-    cback_ref[0] = cback
-    ctx = ctx_ref[0]
-    opart = dot_tn(ctx, low)
     prod = cback.astype(F32) * ctx.astype(F32)
     high = prod.astype(BF)
     rest = (prod - high.astype(F32)).astype(BF)
     heads = lax.broadcasted_iota(jnp.int32, (16, width), 0)
     lanes = lax.broadcasted_iota(jnp.int32, (16, width), 1)
     pick = jnp.where((lanes >= heads * HEAD_DIM) & (lanes < heads * HEAD_DIM + HEAD_DIM), 1.0, 0.0).astype(BF)
-    rowdot_ref[0] = dot_nt(pick, high) + dot_nt(pick, rest)
-
-    @pl.when(s == 0)
-    def _():
-        oacc[...] = opart
-        sums_ref[...] = sums_in_ref[...]
-
-    @pl.when(s > 0)
-    def _():
-        oacc[...] += opart
-
-    sums_ref[2:3, :] += jnp.sum(resid, axis=0, keepdims=True)
-    sums_ref[4:5, :] += gain_sum
-    sums_ref[6:7, :] += shift_sum
-
-    @pl.when(s == pl.num_programs(0) - 1)
-    def _():
-        deal(core_ref[0], oacc, mine_ref, theirs_ref)
-
-
-def norm_one_back(core, second, pre_low, norm, inv, ctx, up_bin, out_bin, small, sums):
-    seqs, length, width = second.shape
-    per_seq = lambda *shape: pl.BlockSpec((1,) + shape, lambda s, _: (s,) + (0,) * len(shape))
-    return pl.pallas_call(
-        norm_kernel,
-        grid_spec=pltpu.PrefetchScalarGridSpec(
-        num_scalar_prefetch=1,
-        grid=(seqs,),
-        in_specs=[
-            per_seq(length, width),
-            per_seq(length, pre_low.shape[2]),
-            per_seq(length, width),
-            per_seq(length, 1),
-            per_seq(length, width),
-            full(up_bin.shape),
-            full(out_bin.shape),
-            full(small.shape),
-            full(sums.shape),
-        ],
-        out_specs=[
-            per_seq(length, width),
-            per_seq(length, width),
-            per_seq(16, length),
-            full((1, width, width // 2)),
-            full((1, width, width // 2)),
-            full(sums.shape),
-        ],
-        scratch_shapes=[pltpu.VMEM((width, width), F32)],
-        ),
-        out_shape=[
-            jax.ShapeDtypeStruct((seqs, length, width), F32),
-            jax.ShapeDtypeStruct((seqs, length, width), BF),
-            jax.ShapeDtypeStruct((seqs, 16, length), F32),
-            jax.ShapeDtypeStruct((1, width, width // 2), BF),
-            jax.ShapeDtypeStruct((1, width, width // 2), BF),
-            jax.ShapeDtypeStruct(sums.shape, F32),
-        ],
-        compiler_params=params(),
-        cost_estimate=cost(2 * seqs * length * width * 6 * width, 40 * seqs * length * width),
-        name="norm_one_back",
-    )(core, second, pre_low, norm, inv, ctx, up_bin, out_bin, small, sums)
+    return resid, cback, dot_nt(pick, high) + dot_nt(pick, rest), dot_tn(ctx, low)
 
 
 MESH = pl.DeviceIdType.MESH
 
 LATE = (0, 2, 4, 6, 8, 10, 12)
+EARLY = 9
 SMALL = 5
 
 
@@ -643,9 +579,11 @@
 
         def tick(t, _=0):
             for k, late in enumerate(LATE):
-                u = t - late
-
-                @pl.when((u >= 0) & (u < units))
+                slot = t - late
+                spread = (slot + 64 - EARLY) // 64
+                u = slot + spread * (slot // 4 + 6 - slot)
+
+                @pl.when((slot >= 0) & (u < units) & (spread * (slot % 4) == 0))
                 def _():
                     stages[k](u)
 
@@ -671,7 +609,7 @@
 
         self.meet, self.begin, self.fetched, self.tick, self.settle = meet, begin, fetched, tick, settle
         self.small_start, self.small_next = (lambda: copy_small(0).start()), small_next
-        self.ticks = units + LATE[-1]
+        self.ticks = (units - 1 - 6) * 4 + 1 + LATE[-1]
 
     @staticmethod
     def buffers(units, rows, cols, small):
@@ -691,42 +629,101 @@
 TILE_B = 256
 
 
-def attend_back_kernel(linked, *refs):
-    (tokens_ref, rows_ref, cols_ref, q_ref, k_ref, v_ref, cback_ref, lse_ref, rowdot_ref, sums_in_ref), refs = (
-        refs[:10], refs[10:]
-    )
-    g, s = pl.program_id(0), pl.program_id(1)
-    last_g, last_s = pl.num_programs(0) - 1, pl.num_programs(1) - 1
+def late_back_kernel(linked, seqs, groups, *refs):
+    (
+        second_ref, pre_ref, norm_ref, inv_ref, ctx_ref, up_ref, out_ref, small_ref,
+        tokens_ref, rows_ref, cols_ref, q_ref, k_ref, v_ref, lse_ref, sums_in_ref,
+    ), refs = refs[:16], refs[16:]
+    step = pl.program_id(0)
+    last = pl.num_programs(0) - 1
     if linked:
-        feed_mine, feed_theirs, out_mine, out_theirs, jlow_ref, result_ref, total_ref, acc, bias_ref, theirs = refs[:10]
-        buffers, sems = refs[10:17], refs[17:]
+        feed_mine, feed_theirs, resid_ref, jlow_ref, result_ref, total_ref = refs[:6]
+        cback_ref, rowdot_ref, acc, bias_ref, theirs = refs[6:11]
+        buffers, sems = refs[11:18], refs[18:]
         exchange = Exchange(result_ref, *buffers, sems)
         held, kept = buffers[0], buffers[5]
         core = lax.axis_index("shard")
-        early = feed_mine.shape[0] + 1
+        early = feed_mine.shape[0]
         sums_ref = kept.at[0]
-        step = g * pl.num_programs(1) + s
     else:
-        jlow_ref, mine_ref, theirs_ref, sums_ref, acc, bias_ref = refs
-        core = 0
-
-    @pl.when((g == 0) & (s == 0))
+        resid_ref, jlow_ref, mine_ref, theirs_ref, sums_ref, cback_ref, rowdot_ref, acc, bias_ref = refs
+
+    def hand_over(n):
+        if linked:
+            deal(core, acc, held.at[pl.ds(early + n, 1)], theirs.at[pl.ds(n, 1)])
+            exchange.begin(early + n, theirs.at[n])
+        else:
+            deal(0, acc, mine_ref.at[pl.ds(n, 1)], theirs_ref.at[pl.ds(n, 1)])
+
+    @pl.when(step == 0)
     def _():
         if linked:
             exchange.meet()
-            for u in range(early - 1):
+            for u in range(early):
                 exchange.begin(u, feed_theirs.at[u], feed_mine.at[u])
-            exchange.begin(early - 1, out_theirs.at[0], out_mine.at[0])
             for u in range(early):
                 exchange.fetched(u)
         sums_ref[...] = sums_in_ref[...]
 
+    @pl.when(step < seqs)
+    def _():
+        if linked:
+            exchange.tick(2 * step)
+        resid, cback, rowdot, part = norm_step(
+            second_ref[0], pre_ref[0], norm_ref[0], inv_ref[0], ctx_ref[0], up_ref, out_ref, small_ref, sums_ref
+        )
+        resid_ref[0] = resid
+        for n in range(groups):
+            cback_ref[step, n] = cback[:, n * GROUP : (n + 1) * GROUP]
+        rowdot_ref[step] = rowdot
+
+        @pl.when(step == 0)
+        def _():
+            acc[...] = part
+
+        @pl.when(step > 0)
+        def _():
+            acc[...] += part
+
+        @pl.when(step == seqs - 1)
+        def _():
+            hand_over(0)
+
+        if linked:
+            exchange.tick(2 * step + 1)
+
+    @pl.when(step >= seqs)
+    def _():
+        g, s = (step - seqs) // seqs, step % seqs
+        if linked:
+            exchange.tick(2 * seqs + step - seqs)
+        attend_step(
+            g, s, tokens_ref, rows_ref, cols_ref, q_ref, k_ref, v_ref, cback_ref, lse_ref, rowdot_ref,
+            jlow_ref, sums_ref, bias_ref, acc,
+        )
+
+        @pl.when(s == seqs - 1)
+        def _():
+            hand_over(1 + g)
+
     if linked:
 
-        @pl.when(step < pl.num_programs(0) * pl.num_programs(1) - 1)
+        @pl.when(step == last)
         def _():
-            exchange.tick(step)
-
+            start = 2 * seqs + seqs * groups
+            exchange.small_start()
+            for k in range(SMALL):
+                exchange.tick(start + k)
+                exchange.small_next(k)
+            lax.fori_loop(start + SMALL, exchange.ticks, exchange.tick, 0)
+            total_ref[...] = kept[SMALL]
+            exchange.settle()
+
+
+def attend_step(
+    g, s, tokens_ref, rows_ref, cols_ref, q_ref, k_ref, v_ref, cback_ref, lse_ref, rowdot_ref,
+    jlow_ref, sums_ref, bias_ref, acc,
+):
     length = tokens_ref.shape[1]
     tile = min(TILE_B, length)
     bias_ref[...] = jnp.where(rows_ref[0] >= cols_ref[0], 0.0, NEG).astype(F32)
@@ -738,7 +735,7 @@
         q2 = q_ref[0, :, at] * BF(0.125)
         k2 = k_ref[0, :, at]
         v2 = v_ref[0, :, at]
-        do2 = cback_ref[0, :, at]
+        do2 = cback_ref[s, g, :, at]
         dq = None
         for t in range(length // tile):
             rows = slice(t * tile, (t + 1) * tile)
@@ -749,7 +746,7 @@
                 vm = jnp.where(mine, v2[rows], BF(0))
                 head = g * (GROUP // HEAD_DIM) + pair * 2 + h
                 lse = lse_ref[0, pl.ds(head, 1), :]
-                rowdot = rowdot_ref[0, pl.ds(head, 1), :]
+                rowdot = rowdot_ref[s, pl.ds(head, 1), :]
                 probs = jnp.exp(dot_nt(km, q2) + bias_ref[rows, :] - lse)
                 dprobs = dot_nt(vm, do2)
                 dscore = (probs * (dprobs - rowdot)).astype(BF)
@@ -778,73 +775,65 @@
     def _():
         acc[...] += part
 
-    @pl.when(s == last_s)
-    def _():
-        if linked:
-            deal(core, acc, held.at[pl.ds(early + g, 1)], theirs.at[pl.ds(g, 1)])
-            exchange.begin(early + g, theirs.at[g])
-        else:
-            deal(core, acc, mine_ref, theirs_ref)
-
-    if linked:
-
-        @pl.when((g == last_g) & (s == last_s))
-        def _():
-            start = pl.num_programs(0) * pl.num_programs(1) - 1
-            exchange.small_start()
-            for k in range(SMALL):
-                exchange.tick(start + k)
-                exchange.small_next(k)
-            lax.fori_loop(start + SMALL, exchange.ticks, exchange.tick, 0)
-            total_ref[...] = kept[SMALL]
-            exchange.settle()
-
-
-def attend_back(tokens, block_ids, joined, cback, lse, rowdot, sums, feed_grads=None, out_grads=None):
+
+def late_back(second, pre_low, norm, inv, ctx, up_bin, out_bin, small, tokens, block_ids, joined, lse, sums, feed_grads=None):
     seqs, length, width = tokens.shape
     rows = block_ids.reshape(seqs, 1, length)
     cols = block_ids.reshape(seqs, length, 1)
     groups = width // GROUP
     linked = feed_grads is not None
-    whole = lambda *shape: pl.BlockSpec((1,) + shape, lambda g, s: (s,) + (0,) * len(shape))
-    part = lambda k: pl.BlockSpec((1, length, GROUP), lambda g, s: (s, 0, k * groups + g))
+    phase = lambda i: (i + 64 - seqs) // 64
+    seq_one = lambda i: i + phase(i) * (seqs - 1 - i)
+    seq_two = lambda i: phase(i) * (i % seqs)
+    group_two = lambda i: phase(i) * ((i - seqs) // seqs)
+    one = lambda *shape: pl.BlockSpec((1,) + shape, lambda i: (seq_one(i),) + (0,) * len(shape))
+    two = lambda *shape: pl.BlockSpec((1,) + shape, lambda i: (seq_two(i),) + (0,) * len(shape))
+    part = lambda k: pl.BlockSpec((1, length, GROUP), lambda i: (seq_two(i), 0, k * groups + group_two(i)))
+    held = lambda a: pl.BlockSpec(a.shape, lambda i: (0,) * a.ndim, pipeline_mode=pl.Buffered(1))
     anywhere = pl.BlockSpec(memory_space=pl.ANY)
     unit = (width, width // 2)
     like = jax.ShapeDtypeStruct
     in_specs = [
-        whole(length, width), whole(1, length), whole(length, 1), part(0), part(1), part(2), part(0),
-        whole(16, length), whole(16, length), full(sums.shape),
+        one(length, width), one(length, pre_low.shape[2]), one(length, width), one(length, 1), one(length, width),
+        held(up_bin), held(out_bin), held(small),
+        two(length, width), two(1, length), two(length, 1), part(0), part(1), part(2), two(16, length), held(sums),
     ]
-    operands = [tokens, rows, cols, joined, joined, joined, cback, lse, rowdot, sums]
-    out_specs = [pl.BlockSpec((1, length, 3 * GROUP), lambda g, s: (s, 0, g))]
-    out_shape = [like((seqs, length, 3 * width), BF)]
-    scratch = [pltpu.VMEM((width, 3 * GROUP), F32), pltpu.VMEM((length, length), F32)]
+    operands = [
+        second, pre_low, norm, inv, ctx, up_bin, out_bin, small,
+        tokens, rows, cols, joined, joined, joined, lse, sums,
+    ]
+    out_specs = [one(length, width), pl.BlockSpec((1, length, 3 * GROUP), lambda i: (seq_two(i), 0, group_two(i)))]
+    out_shape = [like((seqs, length, width), F32), like((seqs, length, 3 * width), BF)]
+    scratch = [
+        pltpu.VMEM((seqs, groups, length, GROUP), BF), pltpu.VMEM((seqs, 16, length), F32),
+        pltpu.VMEM((width, width), F32), pltpu.VMEM((length, length), F32),
+    ]
     if linked:
         units = feed_grads[0].shape[0] + 1 + groups
-        in_specs += [anywhere] * 4
-        operands += [*feed_grads, *out_grads]
+        in_specs += [anywhere] * 2
+        operands += feed_grads
         out_specs += [anywhere, full(sums.shape)]
         out_shape += [like((units,) + unit, BF), like(sums.shape, F32)]
-        scratch += [pltpu.VMEM((groups,) + unit, BF)] + Exchange.buffers(units, *unit, sums.shape)
+        scratch += [pltpu.VMEM((1 + groups,) + unit, BF)] + Exchange.buffers(units, *unit, sums.shape)
         extra = dict(collective_id=0, has_side_effects=True)
     else:
-        out_specs += [pl.BlockSpec((1,) + unit, lambda g, s: (g, 0, 0))] * 2 + [full(sums.shape)]
-        out_shape += [like((groups,) + unit, BF)] * 2 + [like(sums.shape, F32)]
+        out_specs += [full((1 + groups,) + unit)] * 2 + [full(sums.shape)]
+        out_shape += [like((1 + groups,) + unit, BF)] * 2 + [like(sums.shape, F32)]
         extra = {}
     return pl.pallas_call(
-        functools.partial(attend_back_kernel, linked),
-        grid=(groups, seqs),
+        functools.partial(late_back_kernel, linked, seqs, groups),
+        grid=(seqs * (1 + groups),),
         in_specs=in_specs,
         out_specs=out_specs,
         out_shape=out_shape,
         scratch_shapes=scratch,
-        compiler_params=params(**extra),
-        cost_estimate=cost(seqs * length * width * (6 * width + 40 * length), 30 * seqs * length * width),
-        name="attend_back",
+        compiler_params=params(62, **extra),
+        cost_estimate=cost(seqs * length * width * (20 * width + 40 * length), 70 * seqs * length * width),
+        name="late_back",
     )(*operands)
 
 
-def token_kernel(resid_ref, jlow_ref, qkv_ref, grad_ref):
+def token_total(resid_ref, jlow_ref, qkv_ref):
     width = resid_ref.shape[2]
     groups = width // GROUP
     total = resid_ref[0]
@@ -853,7 +842,111 @@
             at = (3 * g + k) * GROUP
             col = k * width + g * GROUP
             total = total + dot_nt(jlow_ref[0, :, at : at + GROUP], qkv_ref[:, col : col + GROUP])
-    grad_ref[0] = total
+    return total
+
+
+def token_kernel(resid_ref, jlow_ref, qkv_ref, grad_ref):
+    grad_ref[0] = token_total(resid_ref, jlow_ref, qkv_ref)
+
+
+def finish_kernel(
+    core_ref, resid_ref, jlow_ref, qkv_bin_ref, feed_ref, out_unit_ref, qkv_unit_ref, sums_ref,
+    grad_ref, qkv_ref, out_ref, up_ref, dn_ref, small_ref, up_stage, qkv_stage, up_sem, qkv_sem,
+):
+    step, last = pl.program_id(0), pl.num_programs(0) - 1
+    _, rows, half = feed_ref.shape
+    groups = qkv_sem.shape[0]
+    parts = (slice(0, half), slice(half, rows))
+
+    def up_copy(c, p):
+        at = pl.ds(pl.multiple_of((p * (last + 1) + c) * half, half), half)
+        return pltpu.make_async_copy(up_stage.at[c, p], up_ref.at[:, at], up_sem.at[c, p])
+
+    def qkv_copy(g, k):
+        at = pl.ds(pl.multiple_of(k * rows + g * GROUP, GROUP), GROUP)
+        return pltpu.make_async_copy(qkv_stage.at[g, k], qkv_ref.at[:, at], qkv_sem.at[g, k])
+
+    for p in range(2):
+        up_stage[step, p] = feed_ref[1, parts[p], :].astype(F32)
+        up_copy(step, p).start()
+        dn_ref[:, parts[p]] = feed_ref[0, parts[p], :].astype(F32)
+
+    @pl.when(step == 0)
+    def _():
+        for p in range(2):
+            out_ref[:, parts[p]] = out_unit_ref[0, parts[p], :].astype(F32)
+        mine = pl.ds(pl.multiple_of(core_ref[0] * half, half), half)
+        small_ref[...] = sums_ref[:, mine]
+
+    @pl.when(step > 0)
+    def _():
+        for j in range(3 * GROUP // 128):
+            col = j * 128
+            qkv_stage[step - 1, col // GROUP, :, col % GROUP : col % GROUP + 128] = qkv_unit_ref[
+                0, parts[col // half], col % half : col % half + 128
+            ].astype(F32)
+        for k in range(3):
+            qkv_copy(step - 1, k).start()
+
+    grad_ref[0] = token_total(resid_ref, jlow_ref, qkv_bin_ref)
+
+    @pl.when(step == last)
+    def _():
+        for c in range(up_sem.shape[0]):
+            for p in range(2):
+                up_copy(c, p).wait()
+        for g in range(groups):
+            for k in range(3):
+                qkv_copy(g, k).wait()
+
+
+def finish(core, resid, jlow, qkv_bin, units, sums):
+    seqs, length, width = resid.shape
+    count, rows, half = units.shape
+    groups = rows // GROUP
+    chunks = (count - 1 - groups) // 2
+    assert chunks == seqs and groups == seqs - 1
+    per_seq = lambda *shape: pl.BlockSpec((1,) + shape, lambda s, _: (s,) + (0,) * len(shape))
+    late = lambda s: s - (s + 63) // 64
+    like = lambda *shape: jax.ShapeDtypeStruct(shape, F32)
+    anywhere = pl.BlockSpec(memory_space=pl.ANY)
+    return pl.pallas_call(
+        finish_kernel,
+        grid_spec=pltpu.PrefetchScalarGridSpec(
+            num_scalar_prefetch=1,
+            grid=(chunks,),
+            in_specs=[
+                per_seq(length, width),
+                per_seq(length, 3 * width),
+                full(qkv_bin.shape),
+                pl.BlockSpec((2, rows, half), lambda s, _: (s, 0, 0)),
+                pl.BlockSpec((1, rows, half), lambda s, _: (2 * chunks, 0, 0)),
+                pl.BlockSpec((1, rows, half), lambda s, _: (2 * chunks + 1 + late(s), 0, 0)),
+                full(sums.shape),
+            ],
+            out_specs=[
+                per_seq(length, width),
+                anywhere,
+                full((half, rows)),
+                anywhere,
+                pl.BlockSpec((half, rows), lambda s, _: (s, 0)),
+                full((sums.shape[0], half)),
+            ],
+            scratch_shapes=[
+                pltpu.VMEM((chunks, 2, half, half), F32),
+                pltpu.VMEM((groups, 3, half, GROUP), F32),
+                pltpu.SemaphoreType.DMA((chunks, 2)),
+                pltpu.SemaphoreType.DMA((groups, 3)),
+            ],
+        ),
+        out_shape=[
+            like(seqs, length, width), like(half, 3 * rows), like(half, rows), like(half, 2 * chunks * half),
+            like(chunks * half, rows), like(sums.shape[0], half),
+        ],
+        compiler_params=params(),
+        cost_estimate=cost(6 * seqs * length * width * width, 16 * seqs * length * width),
+        name="finish",
+    )(core, resid, jlow, qkv_bin, units, units, units, sums)
 
 
 def token_back(resid, jlow, qkv_bin):
@@ -869,50 +962,6 @@
         cost_estimate=cost(6 * seqs * length * width * width, 16 * seqs * length * width),
         name="token_back",
     )(resid, jlow, qkv_bin)
-
-
-def finish_kernel(core_ref, units_ref, sums_ref, qkv_ref, out_ref, up_ref, dn_ref, small_ref):
-    units, rows, half = units_ref.shape
-    groups = rows // GROUP
-    chunks = (units - 1 - groups) // 2
-    wide = [slice(0, rows // 2), slice(rows // 2, rows)]
-    for c in range(chunks):
-        for p in range(2):
-            dn_ref[c * half : (c + 1) * half, p * half : (p + 1) * half] = units_ref[2 * c, wide[p], :].astype(F32)
-            at = p * chunks * half + c * half
-            up_ref[:, at : at + half] = units_ref[2 * c + 1, wide[p], :].astype(F32)
-    for p in range(2):
-        out_ref[:, p * half : (p + 1) * half] = units_ref[2 * chunks, wide[p], :].astype(F32)
-    for g in range(groups):
-        for j in range(3 * GROUP // 128):
-            col = j * 128
-            at = (col // GROUP) * rows + g * GROUP + col % GROUP
-            qkv_ref[:, at : at + 128] = units_ref[
-                2 * chunks + 1 + g, wide[col // half], col % half : col % half + 128
-            ].astype(F32)
-    mine = pl.ds(pl.multiple_of(core_ref[0] * half, half), half)
-    small_ref[...] = sums_ref[:, mine]
-
-
-def finish(core, units, sums):
-    count, rows, half = units.shape
-    groups = rows // GROUP
-    hidden = (count - 1 - groups) // 2 * rows
-    vm = pl.BlockSpec(memory_space=pltpu.VMEM)
-    return pl.pallas_call(
-        finish_kernel,
-        in_specs=[pl.BlockSpec(memory_space=pltpu.SMEM), vm, vm],
-        out_specs=[vm] * 5,
-        out_shape=[
-            jax.ShapeDtypeStruct((half, 3 * rows), F32),
-            jax.ShapeDtypeStruct((half, rows), F32),
-            jax.ShapeDtypeStruct((half, hidden), F32),
-            jax.ShapeDtypeStruct((hidden // 2, rows), F32),
-            jax.ShapeDtypeStruct((sums.shape[0], half), F32),
-        ],
-        compiler_params=params(),
-        name="finish",
-    )(core, units, sums)
 
 
 def swap(value):
@@ -967,18 +1016,14 @@
     joined, ctx, lse, norm, inv = attend(tokens, block_ids, qkv_bin, out_bin, small)
     final, first_low, hidden, slope, second, mixed, sums = feed(norm, teacher, small, up_bin, dn_bin)
     pre_low, *feed_grads, sums = feed_back(core, mixed, first_low, hidden, slope, dn_bin, sums)
-    resid, cback, rowdot, *out_grads, sums = norm_one_back(
-        core, second, pre_low, norm, inv, ctx, up_bin, out_bin, small, sums
-    )
+    operands = (second, pre_low, norm, inv, ctx, up_bin, out_bin, small, tokens, block_ids, joined, lse, sums)
     if not paired:
-        jlow, *qkv_grads, sums = attend_back(tokens, block_ids, joined, cback, lse, rowdot, sums)
+        resid, jlow, *grads, sums = late_back(*operands)
         token_grad = token_back(resid, jlow, qkv_bin)
+        out_grads, qkv_grads = ([a[cut] for a in grads] for cut in (slice(0, 1), slice(1, None)))
         return (final, token_grad) + tuple(reduce_plain(feed_grads, out_grads, qkv_grads, sums[:12]))
-    jlow, units, sums = attend_back(
-        tokens, block_ids, joined, cback, lse, rowdot, sums, feed_grads, out_grads
-    )
-    token_grad = token_back(resid, jlow, qkv_bin)
-    qkv_grad, out_grad, up_grad, dn_grad, small = finish(core, units, sums)
+    resid, jlow, units, sums = late_back(*operands, feed_grads)
+    token_grad, qkv_grad, out_grad, up_grad, dn_grad, small = finish(core, resid, jlow, qkv_bin, units, sums)
     hidden_rows = hidden_bias.shape[0] // small.shape[1]
     return (
         final, token_grad, qkv_grad, out_grad, up_grad, dn_grad,

time: 371 us -> 366 us (0.987)
    pallas_call x4 -> x2, Pallas kernels: 194 us -> 192 us  [the longest x1 172 us: late_back(): pl.pallas_call(functools.partial(late_back_kernel, linked, seqs, groups),...]
where the time goes in v4:
time: 366 us; the launch traced here: 362 us
  Pallas kernels  344 us (94%)
  local copies, waits for them, and re-layouts  8.9 us (2%)
  waiting for transfers between devices  5.41 us (1%)
    pallas_call x1, Pallas kernels, late_back(): pl.pallas_call(functools.partial(late_back_kernel, linked, seqs, groups),...  172 us
    pallas_call x1, Pallas kernels, attend(): pl.pallas_call(attend_kernel, grid=(seqs,), in_specs=[per_seq(length, wid...  49.9 us
    pallas_call x1, Pallas kernels, feed_back(): pl.pallas_call(feed_back_kernel, grid_spec=pltpu.PrefetchScalarGridSpec(n...  47.6 us
    pallas_call x1, Pallas kernels, feed(): pl.pallas_call(feed_kernel, grid=(seqs,), in_specs=[per_seq(length, width...  38.2 us
    pallas_call x1, Pallas kernels, finish(): pl.pallas_call(finish_kernel, grid_spec=pltpu.PrefetchScalarGridSpec(num_...  19.2 us
    pallas_call x1, Pallas kernels, prep_rest(): pl.pallas_call(prep_rest_kernel, in_specs=[pl.BlockSpec(memory_space=pltp...  11.5 us
  transfers between devices with their start and end apart: 5, of which 2 were waited for; matrix products, arithmetic and copies ran while one was open for 1% of the time, Pallas kernels for 1%

profile of v4, /device:TPU:0, one launch (start us, length us, event | category | flops | bytes accessed | tf_op | source)
XLA Modules:
  0.0 361.8 jit_solution(17159314625850310232)
XLA Ops:
  0.6 0.5 collective-permute-start.3
  1.2 0.1 collective-permute-start.4
  1.2 0.4 collective-permute-start
  1.7 0.1 collective-permute-start.2
  1.8 0.7 reshape.40
  2.5 0.7 pad_maximum_fusion.small_own_ref
  3.2 0.0 copy-start.2
  3.2 0.5 collective-permute-start.1
  3.7 1.3 reshape.37.rows_ref.refs_9_
  5.0 2.0 copy.21.cols_ref.refs_10_
  7.0 0.9 collective-permute-done.1.small_other_ref
  7.9 0.0 copy-start.3
  7.9 4.5 %collective-permute-done.other_ref = bf16[384,2304]{1,0:T(8,128)(2,1)} collective-permute-done((bf16[384,2304]{1,0:T(8,128)(2,1)}, bf16[384,2304]{1,0:T(8,128)(2,1)}, u32[]{:S(2)}, u32[]{:S(2)}) %collective-permute-start) | collective-permute-done | bytes 1769504 | tf_op jit(solution)/shard_map/ppermute | solution.py:968
  12.4 0.0 copy-done.2
  12.4 0.0 copy-done.3
  12.4 5.2 %prep_qkv.1 = (bf16[768,2304]{1,0:T(8,128)(2,1)}, f32[12,768]{1,0:T(8,128)}) custom-call(s32[1]{0:T(128)} %bitcast.1.core_ref, bf16[384,2304]{1,0:T(8,128)(2,1)} %own_ref.1, bf16[384,2304]{1,0:T(8,128)(2,1)} %collective-permute-done.other_ref, bf16[12,384]{1,0:T(8,128)(2,1)} %copy-done.2, bf16[12,384]{1,0:T(8,128)(2,1)} %copy-done.3), custom_call_target="tpu_custom_call" | custom-call | flops 7077888 | bytes 7077888 | tf_op jit(solution)/shard_map/prep_qkv/pallas_call | solution.py:82
  17.6 0.0 collective-permute-done.2.out_b
  17.6 0.0 copy-start.1
  17.7 0.0 collective-permute-done.3.up_b
  17.7 0.0 copy-start
  17.7 0.0 collective-permute-done.4.dn_b
  17.7 0.8 copy-done.1
  18.5 0.8 copy-done
  19.2 11.5 %prep_rest.1 = (bf16[768,768]{1,0:T(8,128)(2,1)}, bf16[768,3072]{1,0:T(8,128)(2,1)}, bf16[3072,768]{1,0:T(8,128)(2,1)}) custom-call(s32[1]{0:T(128)} %bitcast.1.core_ref, bf16[384,768]{1,0:T(8,128)(2,1)} %out_a.1, bf16[384,768]{1,0:T(8,128)(2,1)} %copy-done.1, bf16[384,3072]{1,0:T(8,128)(2,1)} %up_a.1, bf16[384,3072]{1,0:T(8,128)(2,1)} %copy-done, ...), custom_call_target="tpu_custom_call" | custom-call | flops 18874368 | bytes 18874368 | tf_op jit(solution)/shard_map/prep_rest/pallas_call | solution.py:134
  30.8 49.9 %attend.1 = (bf16[4,512,2304]{2,1,0:T(8,128)(2,1)}, bf16[4,512,768]{2,1,0:T(8,128)(2,1)}, f32[4,16,512]{2,1,0:T(8,128)}, f32[4,512,768]{2,1,0:T(8,128)}, f32[4,512,1]{2,1,0:T(8,128)}) custom-call(bf16[4,512,768]{2,1,0:T(8,128)(2,1)} %refs_8_.1, s32[4,1,512]{2,1,0:T(1,128)} %reshape.37.rows_ref.refs_9_, s32[4,512,1]{2,1,0:T(8,128)} %copy.21.cols_ref.refs_10_, ...), custom_call_target="tpu_custom_call" | custom-call | flops 22548578304 | bytes 47185920 | tf_op jit(solution)/shard_map/attend/pallas_call | solution.py:209
  80.6 38.2 %feed.1 = (bf16[4,512,768]{2,1,0:T(8,128)(2,1)}, bf16[4,512,768]{2,1,0:T(8,128)(2,1)}, bf16[4,512,3072]{2,1,0:T(8,128)(2,1)}, bf16[4,512,3072]{2,1,0:T(8,128)(2,...) custom-call(f32[4,512,768]{2,1,0:T(8,128)} %get-tuple-element.44.norm_ref.refs_2_, ...), custom_call_target="tpu_custom_call" | custom-call | flops 19327352832 | bytes 56623104 | tf_op jit(solution)/shard_map/feed/pallas_call | solution.py:300
  118.8 47.6 %feed_back.1 = (bf16[4,512,3072]{2,1,0:T(8,128)(2,1)}, bf16[8,768,384]{2,1,0:T(8,128)(2,1)}, bf16[8,768,384]{2,1,0:T(8,128)(2,1)}, f32[16,768]{1,0:T(8,128)}) custom-call(s32[1]{0:T(128)} %bitcast.1.core_ref, bf16[4,512,768]{2,1,0:T(8,128)(2,1)} %get-tuple-element.49.mixed_ref, bf16[4,512,768]{2,1,0:T(8,128)(2,1)} %get-tuple-element.50.first_ref, ...), custom_call_target="tpu_custom_call" | custom-call | flops 28991029248 | bytes 125829120 | tf_op jit(solution)/shard_map/feed_back/pallas_call | solution.py:369
  166.4 172.3 %late_back.1 = (f32[4,512,768]{2,1,0:T(8,128)}, bf16[4,512,2304]{2,1,0:T(8,128)(2,1)}, bf16[12,768,384]{2,1,0:T(8,128)(2,1)}, f32[16,768]{1,0:T(8,128)}) custom-call(f32[4,512,768]{2,1,0:T(8,128)} %get-tuple-element.48.refs_0_, bf16[4,512,3072]{2,1,0:T(8,128)(2,1)} %get-tuple-element.54.refs_1_, f32[4,512,768]{2,1,0:T(8,128)} %get-tuple-element.44.norm_ref.refs_2_, ...), custom_call_target="tpu_custom_call" | custom-call | flops 56371445760 | bytes 110100480 | tf_op jit(solution)/shard_map/late_back/pallas_call | solution.py:823
  338.7 19.2 %finish.1 = (f32[4,512,768]{2,1,0:T(8,128)}, f32[384,2304]{1,0:T(8,128)}, f32[384,768]{1,0:T(8,128)}, f32[384,3072]{1,0:T(8,128)}, f32[1536,768]{1,0:T(8,128)}, /*index=5*/f32[16,384]{1,0:T(8,128)}) custom-call(s32[1]{0:T(128)} %bitcast.1.core_ref, f32[4,512,768]{2,1,0:T(8,128)} %get-tuple-element.62.resid_ref, ...), custom_call_target="tpu_custom_call" | custom-call | flops 7247757312 | bytes 25165824 | tf_op jit(solution)/shard_map/finish/pallas_call | solution.py:913
  358.0 1.4 slice_bitcast_fusion.1
  359.4 1.3 fusion
  360.7 0.6 reshape.41
Async XLA Ops:
  0.6 17.0 %collective-permute-start.3 = (bf16[384,3072]{1,0:T(8,128)(2,1)}, bf16[384,3072]{1,0:T(8,128)(2,1)S(1)}, u32[]{:S(2)}, u32[]{:S(2)}) collective-permute-start(bf16[384,3072]{1,0:T(8,128)(2,1)} %up_a.1), channel_id=1, source_target_pairs={{0,16},{16,0},{1,17},{17,1},{2,18},{18,2},{3,19},{19,3},{4,20},{20... | collective-permute-start | bytes 7077896 | tf_op jit(solution)/shard_map/ppermute | solution.py:968
  1.2 16.5 %collective-permute-start.4 = (bf16[1536,768]{1,0:T(8,128)(2,1)}, bf16[1536,768]{1,0:T(8,128)(2,1)}, u32[]{:S(2)}, u32[]{:S(2)}) collective-permute-start(bf16[1536,768]{1,0:T(8,128)(2,1)} %dn_a.1), channel_id=1, source_target_pairs={{0,16},{16,0},{1,17},{17,1},{2,18},{18,2},{3,19},{19,3},{4,20},{20... | collective-permute-start | bytes 7077896 | tf_op jit(solution)/shard_map/ppermute | solution.py:968
  1.2 11.2 %collective-permute-start = (bf16[384,2304]{1,0:T(8,128)(2,1)}, bf16[384,2304]{1,0:T(8,128)(2,1)}, u32[]{:S(2)}, u32[]{:S(2)}) collective-permute-start(bf16[384,2304]{1,0:T(8,128)(2,1)} %own_ref.1), channel_id=1, source_target_pairs={{0,16},{16,0},{1,17},{17,1},{2,18},{18,2},{3,19},{19,3},{4,20},{20... | collective-permute-start | bytes 5308424 | tf_op jit(solution)/shard_map/ppermute | solution.py:968
  1.7 16.0 %collective-permute-start.2 = (bf16[384,768]{1,0:T(8,128)(2,1)}, bf16[384,768]{1,0:T(8,128)(2,1)S(1)}, u32[]{:S(2)}, u32[]{:S(2)}) collective-permute-start(bf16[384,768]{1,0:T(8,128)(2,1)} %out_a.1), channel_id=1, source_target_pairs={{0,16},{16,0},{1,17},{17,1},{2,18},{18,2},{3,19},{19,3},{4,20},{20... | collective-permute-start | bytes 1769480 | tf_op jit(solution)/shard_map/ppermute | solution.py:968
  3.2 9.2 %copy-start.2 = (bf16[12,384]{1,0:T(8,128)(2,1)}, bf16[12,384]{1,0:T(8,128)(2,1)S(1)}, u32[]{:S(2)}) copy-start(bf16[12,384]{1,0:T(8,128)(2,1)S(1)} %pad_maximum_fusion.small_own_ref) | copy-start | bytes 27652
  3.2 4.7 %collective-permute-start.1 = (bf16[12,384]{1,0:T(8,128)(2,1)S(1)}, bf16[12,384]{1,0:T(8,128)(2,1)S(1)}, u32[]{:S(2)}, u32[]{:S(2)}) collective-permute-start(bf16[12,384]{1,0:T(8,128)(2,1)S(1)} %pad_maximum_fusion.small_own_ref), channel_id=1, source_target_pairs={{0,16},{16,0},{1,17},{17,1},{2,18},{18,2},{3,19},{19,3},{4,20},{20... | collective-permute-start | bytes 27656 | tf_op jit(solution)/shard_map/ppermute | solution.py:968
  7.9 4.5 %copy-start.3 = (bf16[12,384]{1,0:T(8,128)(2,1)}, bf16[12,384]{1,0:T(8,128)(2,1)S(1)}, u32[]{:S(2)}) copy-start(bf16[12,384]{1,0:T(8,128)(2,1)S(1)} %collective-permute-done.1.small_other_ref) | copy-start | bytes 27652
  17.6 0.8 copy-start.1
  17.7 1.6 copy-start
